TPU v7x, 32 devices: a whole 2x2x4 slice. The times are simulated.
32 devices in a mesh: dp: 4 (over z), expert: 8 (over y, x, core).
Axes of the slice: x: 2, y: 2, z: 4, core: 2. Of those that a mesh axis runs over, the one named last changes fastest.
Arguments:
- tokens_in: bfloat16 [10240, 2048], P(('dp', 'expert')), may hold values from -6 to 6
- cotangent: bfloat16 [10240, 2048], P(('dp', 'expert')), may hold values from -6 to 6
- segment_id: int32 [10240], P('dp'), may hold values from 0 to 12, as said below
- parent_id: int32 [10240], P('dp'), may hold values from 0 to 4, as said below
- adapter_index: int32 [4], replicated, may hold values from 0 to 7
- routes: int32 [10240, 6], P(('dp', 'expert')), may hold values from 0 to 63, all different within a row; in each aligned block of 320 rows (0 to 319, 320 to 639, ...) at most 40 rows name the same one
- mixer_gain: float32 [2048], replicated, may hold values from 0.5 to 1.5
- latent_gain: float32 [512], replicated, may hold values from 0.5 to 1.5
- feed_gain: float32 [2048], replicated, may hold values from 0.5 to 1.5
- query_matrix: bfloat16 [2048, 3072], P(('dp', 'expert')), may hold values from -0.125 to 0.125
- latent_down: bfloat16 [2048, 576], P(('dp', 'expert')), may hold values from -0.125 to 0.125
- latent_up: bfloat16 [512, 4096], P(('dp', 'expert')), may hold values from -0.25 to 0.25
- output_matrix: bfloat16 [2048, 2048], P(('dp', 'expert')), may hold values from -0.75 to 0.75
- router_matrix: bfloat16 [2048, 64], P(('dp', 'expert')), may hold values from -0.0625 to 0.0625
- shared_in: bfloat16 [2048, 5632], P(('dp', 'expert')), may hold values from -0.125 to 0.125
- shared_out: bfloat16 [2816, 2048], P(('dp', 'expert')), may hold values from -0.109375 to 0.109375
- expert_in: bfloat16 [64, 2048, 2816], P('expert'), may hold values from -0.125 to 0.125
- expert_out: bfloat16 [64, 1408, 2048], P('expert'), may hold values from -6 to 6
- query_entry: bfloat16 [8, 16, 2048], replicated, may hold values from -0.125 to 0.125
- query_exit: bfloat16 [8, 16, 3072], replicated, may hold values from -0.625 to 0.625
- lower_entry: bfloat16 [8, 16, 2048], replicated, may hold values from -0.125 to 0.125
- lower_exit: bfloat16 [8, 16, 576], replicated, may hold values from -0.625 to 0.625
- upper_entry: bfloat16 [8, 16, 512], replicated, may hold values from -0.25 to 0.25
- upper_exit: bfloat16 [8, 16, 4096], replicated, may hold values from -0.625 to 0.625
- output_entry: bfloat16 [8, 16, 2048], replicated, may hold values from -0.125 to 0.125
- output_exit: bfloat16 [8, 16, 2048], replicated, may hold values from -3 to 3
Outputs:
- block_output: bfloat16 [10240, 2048], P(('dp', 'expert'))
- grad_input: bfloat16 [10240, 2048], P(('dp', 'expert'))
- grad_query_entry: float32 [8, 16, 2048], replicated
- grad_query_exit: float32 [8, 16, 3072], replicated
- grad_lower_entry: float32 [8, 16, 2048], replicated
- grad_lower_exit: float32 [8, 16, 576], replicated
- grad_upper_entry: float32 [8, 16, 512], replicated
- grad_upper_exit: float32 [8, 16, 4096], replicated
- grad_output_entry: float32 [8, 16, 2048], replicated
- grad_output_exit: float32 [8, 16, 2048], replicated
Inputs may be any that keep to these rules, and one draw needn't show every extreme that they name: `segment_id`: each tree is 20 aligned blocks of 128 tokens: the first 8 blocks are segment 0 (the trunk), the other 12 hold segments 1 to 12, one block each, in some order; segments 1 to 4 are branches, 5 to 12 leaves. `parent_id`: 0 for the trunk and the branches; a leaf's parent is a branch, and each branch has two leaves. `routes`: each row names 6 different experts; in the 320 rows of one device no expert is named more than 40 times.
All inputs are finite; a program needn't handle non-finite values.
Results may differ from a plain program's by a relative error of at most 0.025.
Values may be sent and summed in bfloat16 or wider, within the bound.
A program may use at most 640 MiB of HBM per device.

v0:
```python
import jax
import jax.numpy as jnp
from jax import lax
from jax.sharding import PartitionSpec as P

D = 2048
HEADS = 16
NOPE = 128
ROPE = 64
VDIM = 128
KVR = 512
TOPK = 6
SEGLEN = 128
TRUNK = 1024
TREE = 2560


def product(left, right):
    return jnp.dot(left, right, preferred_element_type=jnp.float32)


def product_t(left, right):
    return lax.dot_general(
        left, right, (((1,), (1,)), ((), ())), preferred_element_type=jnp.float32
    )


def product_left(left, right):
    return lax.dot_general(
        left, right, (((0,), (0,)), ((), ())), preferred_element_type=jnp.float32
    )


def normed(operand, gain):
    return operand * lax.rsqrt(jnp.mean(operand * operand, axis=-1, keepdims=True) + 1e-06) * gain


def swish(operand):
    return operand / (1.0 + jnp.exp(-operand))


def gated(gate_up):
    half_width = gate_up.shape[-1] // 2
    return swish(gate_up[..., :half_width]) * gate_up[..., half_width:]


def rope_tables(position, width):
    half_width = width // 2
    inverse = 10000.0 ** (-(jnp.arange(half_width, dtype=jnp.float32) * 2.0 / width))
    angles = position.astype(jnp.float32)[:, None] * inverse[None, :]
    return (
        jnp.concatenate([jnp.cos(angles), jnp.cos(angles)], -1),
        jnp.concatenate([jnp.sin(angles), jnp.sin(angles)], -1),
    )


def rotate(operand, cosine, sine):
    half_width = operand.shape[-1] // 2
    turned = jnp.concatenate([-operand[..., half_width:], operand[..., :half_width]], -1)
    return operand * cosine + turned * sine


def select_slot(bank, chosen):
    return lax.dynamic_index_in_dim(bank, chosen, 0, keepdims=False)


def body(
    tokens_in,
    cotangent,
    segment_id,
    parent_id,
    adapter_index,
    routes,
    mixer_gain,
    latent_gain,
    feed_gain,
    query_matrix,
    latent_down,
    latent_up,
    output_matrix,
    router_matrix,
    shared_in,
    shared_out,
    expert_in,
    expert_out,
    query_entry,
    query_exit,
    lower_entry,
    lower_exit,
    upper_entry,
    upper_exit,
    output_entry,
    output_exit,
):
    rows_here = tokens_in.shape[0]
    groups = lax.axis_size("expert")
    group_pos = lax.axis_index("expert")
    trees_here = segment_id.shape[0] // TREE
    local_tree = group_pos * rows_here // TREE
    tree_offset = group_pos * rows_here - local_tree * TREE
    chosen = adapter_index[lax.axis_index("dp") * trees_here + local_tree]
    query_in = select_slot(query_entry, chosen)
    query_out = select_slot(query_exit, chosen)
    lower_in = select_slot(lower_entry, chosen)
    lower_out = select_slot(lower_exit, chosen)
    upper_in = select_slot(upper_entry, chosen)
    upper_out = select_slot(upper_exit, chosen)
    output_in = select_slot(output_entry, chosen)
    output_out = select_slot(output_exit, chosen)
    experts_all = router_matrix.shape[1]
    per_owner = expert_in.shape[0]
    capacity = max(2, 4 * rows_here * TOPK // (3 * experts_all))
    scaling = 1.0 / (NOPE + ROPE) ** 0.5
    mix_query, mix_down, mix_up, mix_out = (
        lax.all_gather(query_matrix, ("dp", "expert"), axis=0, tiled=True),
        lax.all_gather(latent_down, ("dp", "expert"), axis=0, tiled=True),
        lax.all_gather(latent_up, ("dp", "expert"), axis=0, tiled=True),
        lax.all_gather(output_matrix, ("dp", "expert"), axis=0, tiled=True),
    )
    feed_in, feed_out, feed_router = (
        lax.all_gather(shared_in, ("dp", "expert"), axis=0, tiled=True),
        lax.all_gather(shared_out, ("dp", "expert"), axis=0, tiled=True),
        lax.all_gather(router_matrix, ("dp", "expert"), axis=0, tiled=True),
    )
    seg_tree = lax.dynamic_slice_in_dim(segment_id, local_tree * TREE, TREE)
    par_tree = lax.dynamic_slice_in_dim(parent_id, local_tree * TREE, TREE)
    key_index = jnp.arange(TREE, dtype=jnp.int32)
    start_pos = jnp.where(par_tree == 0, TRUNK, TRUNK + SEGLEN)
    key_pos = jnp.where(seg_tree == 0, key_index, start_pos + key_index % SEGLEN)
    row_index = lax.dynamic_slice_in_dim(key_index, tree_offset, rows_here)
    row_pos = lax.dynamic_slice_in_dim(key_pos, tree_offset, rows_here)
    row_seg = lax.dynamic_slice_in_dim(seg_tree, tree_offset, rows_here)
    row_par = lax.dynamic_slice_in_dim(par_tree, tree_offset, rows_here)
    visible = (seg_tree[None, :] == row_seg[:, None]) & (
        key_index[None, :] <= row_index[:, None]
    ) | (row_seg[:, None] != 0) & (
        (seg_tree[None, :] == 0) | (seg_tree[None, :] == row_par[:, None])
    )
    cosine, sine = rope_tables(row_pos, ROPE)
    inputs = tokens_in.astype(jnp.float32)
    hidden = normed(inputs, mixer_gain).astype(jnp.bfloat16)
    query_mid = product_t(hidden, query_in).astype(jnp.bfloat16)
    query_lin = product(hidden, mix_query) + product(query_mid, query_out)
    query_three = query_lin.reshape(rows_here, HEADS, NOPE + ROPE)
    query_all = jnp.concatenate(
        [
            query_three[:, :, :NOPE],
            rotate(query_three[:, :, NOPE:], cosine[:, None, :], sine[:, None, :]),
        ],
        -1,
    ).astype(jnp.bfloat16)
    lower_mid = product_t(hidden, lower_in).astype(jnp.bfloat16)
    latent_full = product(hidden, mix_down) + product(lower_mid, lower_out)
    latent_raw = latent_full[:, :KVR]
    rope_raw = latent_full[:, KVR:]
    latent_norm = normed(latent_raw, latent_gain).astype(jnp.bfloat16)
    key_rope = rotate(rope_raw, cosine, sine).astype(jnp.bfloat16)
    all_latent, all_rope = (
        lax.all_gather(latent_norm, "expert", axis=0, tiled=True),
        lax.all_gather(key_rope, "expert", axis=0, tiled=True),
    )
    tree_latent = lax.dynamic_slice_in_dim(all_latent, local_tree * TREE, TREE, 0)
    tree_rope = lax.dynamic_slice_in_dim(all_rope, local_tree * TREE, TREE, 0)
    upper_mid = product_t(tree_latent, upper_in).astype(jnp.bfloat16)
    key_value = (
        (product(tree_latent, mix_up) + product(upper_mid, upper_out))
        .astype(jnp.bfloat16)
        .reshape(TREE, HEADS, NOPE + VDIM)
    )
    key_nope = key_value[:, :, :NOPE]
    values = key_value[:, :, NOPE:]

    def score_block():
        nope_part = jnp.einsum(
            "qhd,khd->hqk", query_all[:, :, :NOPE], key_nope, preferred_element_type=jnp.float32
        )
        rope_part = jnp.einsum(
            "qhd,kd->hqk", query_all[:, :, NOPE:], tree_rope, preferred_element_type=jnp.float32
        )
        return jnp.where(visible[None], (nope_part + rope_part) * scaling, -1e30)

    scores = score_block()
    row_peak = jnp.max(scores, axis=2, keepdims=True)
    exp_scores = jnp.exp(scores - row_peak)
    row_total = jnp.sum(exp_scores, axis=2, keepdims=True)
    log_total = row_peak + jnp.log(row_total)
    soft_low = (exp_scores / row_total).astype(jnp.bfloat16)
    attended = (
        jnp.einsum("hqk,khd->qhd", soft_low, values, preferred_element_type=jnp.float32)
        .reshape(rows_here, HEADS * VDIM)
        .astype(jnp.bfloat16)
    )
    output_mid = product_t(attended, output_in).astype(jnp.bfloat16)
    mixed_state = inputs + product(attended, mix_out) + product(output_mid, output_out)
    feed_hidden = normed(mixed_state, feed_gain).astype(jnp.bfloat16)
    logits = product(feed_hidden, feed_router)
    logit_peak = jnp.max(logits, axis=1, keepdims=True)
    logit_exp = jnp.exp(logits - logit_peak)
    router_probs = logit_exp / jnp.sum(logit_exp, axis=1, keepdims=True)
    one_hot = (routes[:, :, None] == jnp.arange(experts_all, dtype=jnp.int32)).astype(jnp.float32)
    gate_weights = jnp.sum(one_hot * router_probs[:, None, :], axis=2)
    flat_routes = routes.reshape(-1)
    flat_hot = (flat_routes[:, None] == jnp.arange(experts_all, dtype=jnp.int32)).astype(jnp.int32)
    before = jnp.cumsum(flat_hot, axis=0) - flat_hot
    slot_index = jnp.sum(before * flat_hot, axis=1)
    target = flat_routes * capacity + slot_index
    token_rows = jnp.repeat(jnp.arange(rows_here, dtype=jnp.int32), TOPK)
    sender = (
        jnp.zeros((experts_all * capacity, D), jnp.bfloat16).at[target].set(feed_hidden[token_rows])
    )
    sender = sender.reshape(groups, per_owner, capacity, D)
    gate_up = jnp.einsum(
        "secd,edf->secf",
        lax.all_to_all(sender, "expert", split_axis=0, concat_axis=0, tiled=True),
        expert_in,
        preferred_element_type=jnp.float32,
    )
    inner_act = gated(gate_up).astype(jnp.bfloat16)
    result = jnp.einsum("secf,efd->secd", inner_act, expert_out, preferred_element_type=jnp.float32)
    expert_result = result.astype(jnp.bfloat16)
    returned = lax.all_to_all(
        expert_result, "expert", split_axis=0, concat_axis=0, tiled=True
    ).reshape(experts_all * capacity, D)
    per_route = returned[target].reshape(rows_here, TOPK, D).astype(jnp.float32)
    routed = jnp.sum(gate_weights[:, :, None] * per_route, axis=1)
    shared_act = product(feed_hidden, feed_in)
    shared_inner = gated(shared_act).astype(jnp.bfloat16)
    shared_res = product(shared_inner, feed_out)
    block_output = (mixed_state + routed + shared_res).astype(jnp.bfloat16)
    mix_query, mix_down, mix_up, mix_out = (
        lax.all_gather(query_matrix, ("dp", "expert"), axis=0, tiled=True),
        lax.all_gather(latent_down, ("dp", "expert"), axis=0, tiled=True),
        lax.all_gather(latent_up, ("dp", "expert"), axis=0, tiled=True),
        lax.all_gather(output_matrix, ("dp", "expert"), axis=0, tiled=True),
    )
    feed_in, feed_out, feed_router = (
        lax.all_gather(shared_in, ("dp", "expert"), axis=0, tiled=True),
        lax.all_gather(shared_out, ("dp", "expert"), axis=0, tiled=True),
        lax.all_gather(router_matrix, ("dp", "expert"), axis=0, tiled=True),
    )
    grad_output = cotangent.astype(jnp.float32)
    shared_primal, shared_back = jax.vjp(gated, shared_act)
    grad_shared_act = shared_back(product_t(cotangent, feed_out))[0].astype(jnp.bfloat16)
    grad_feed = product_t(grad_shared_act, feed_in)
    grad_gates = jnp.sum(grad_output[:, None, :] * per_route, axis=2)
    grad_probs = jnp.sum(one_hot * grad_gates[:, :, None], axis=1)
    grad_logits = router_probs * (
        grad_probs - jnp.sum(router_probs * grad_probs, axis=1, keepdims=True)
    )
    grad_feed = grad_feed + product_t(grad_logits.astype(jnp.bfloat16), feed_router)
    grad_rows = (
        (gate_weights[:, :, None] * grad_output[:, None, :])
        .reshape(rows_here * TOPK, D)
        .astype(jnp.bfloat16)
    )
    grad_send = jnp.zeros((experts_all * capacity, D), jnp.bfloat16).at[target].set(grad_rows)
    grad_received = lax.all_to_all(
        grad_send.reshape(groups, per_owner, capacity, D),
        "expert",
        split_axis=0,
        concat_axis=0,
        tiled=True,
    )
    grad_inner = jnp.einsum(
        "secd,efd->secf", grad_received, expert_out, preferred_element_type=jnp.float32
    )
    expert_primal, expert_back = jax.vjp(gated, gate_up)
    grad_gate_up = expert_back(grad_inner)[0].astype(jnp.bfloat16)
    grad_slot = jnp.einsum(
        "secf,edf->secd", grad_gate_up, expert_in, preferred_element_type=jnp.float32
    ).astype(jnp.bfloat16)
    grad_back = lax.all_to_all(
        grad_slot, "expert", split_axis=0, concat_axis=0, tiled=True
    ).reshape(experts_all * capacity, D)
    grad_feed = grad_feed + jnp.sum(
        grad_back[target].reshape(rows_here, TOPK, D).astype(jnp.float32), axis=1
    )
    norm_primal, norm_two_back = jax.vjp(lambda operand: normed(operand, feed_gain), mixed_state)
    grad_mixed = grad_output + norm_two_back(grad_feed)[0]
    grad_attn = grad_mixed.astype(jnp.bfloat16)
    grad_output_mid = product_t(grad_attn, output_out).astype(jnp.bfloat16)
    grad_output_exit = product_left(output_mid, grad_attn)
    grad_output_entry = product_left(grad_output_mid, attended)
    grad_attended = (
        (product_t(grad_attn, mix_out) + product(grad_output_mid, output_in))
        .astype(jnp.bfloat16)
        .reshape(rows_here, HEADS, VDIM)
    )
    soft_again = jnp.exp(score_block() - log_total)
    grad_soft = jnp.einsum(
        "qhd,khd->hqk", grad_attended, values, preferred_element_type=jnp.float32
    )
    grad_scores = (
        soft_again * (grad_soft - jnp.sum(soft_again * grad_soft, axis=2, keepdims=True))
    ).astype(jnp.bfloat16)
    grad_query_nope = (
        jnp.einsum("hqk,khd->qhd", grad_scores, key_nope, preferred_element_type=jnp.float32)
        * scaling
    )
    grad_query_rope = (
        jnp.einsum("hqk,kd->qhd", grad_scores, tree_rope, preferred_element_type=jnp.float32)
        * scaling
    )
    grad_key_nope = (
        jnp.einsum(
            "hqk,qhd->khd", grad_scores, query_all[:, :, :NOPE], preferred_element_type=jnp.float32
        )
        * scaling
    )
    grad_key_rope = (
        jnp.einsum(
            "hqk,qhd->kd", grad_scores, query_all[:, :, NOPE:], preferred_element_type=jnp.float32
        )
        * scaling
    )
    grad_values = jnp.einsum(
        "hqk,qhd->khd",
        soft_again.astype(jnp.bfloat16),
        grad_attended,
        preferred_element_type=jnp.float32,
    )
    grad_kv = (
        jnp.concatenate([grad_key_nope, grad_values], -1)
        .reshape(TREE, HEADS * (NOPE + VDIM))
        .astype(jnp.bfloat16)
    )
    grad_upper_mid = product_t(grad_kv, upper_out).astype(jnp.bfloat16)
    grad_upper_exit = product_left(upper_mid, grad_kv)
    grad_upper_entry = product_left(grad_upper_mid, tree_latent)
    grad_tree_latent = product_t(grad_kv, mix_up) + product(grad_upper_mid, upper_in)
    spread_latent = lax.dynamic_update_slice_in_dim(
        jnp.zeros((groups * rows_here, KVR), jnp.float32), grad_tree_latent, local_tree * TREE, 0
    )
    spread_rope = lax.dynamic_update_slice_in_dim(
        jnp.zeros((groups * rows_here, ROPE), jnp.float32), grad_key_rope, local_tree * TREE, 0
    )
    grad_latent, grad_rope = (
        lax.psum_scatter(
            spread_latent.astype(jnp.bfloat16), "expert", scatter_dimension=0, tiled=True
        ).astype(jnp.float32),
        lax.psum_scatter(
            spread_rope.astype(jnp.bfloat16), "expert", scatter_dimension=0, tiled=True
        ).astype(jnp.float32),
    )
    latent_primal, latent_back = jax.vjp(lambda operand: normed(operand, latent_gain), latent_raw)
    key_primal, key_back = jax.vjp(lambda operand: rotate(operand, cosine, sine), rope_raw)
    grad_latent_full = jnp.concatenate(
        [latent_back(grad_latent)[0], key_back(grad_rope)[0]], -1
    ).astype(jnp.bfloat16)
    grad_lower_mid = product_t(grad_latent_full, lower_out).astype(jnp.bfloat16)
    grad_lower_exit = product_left(lower_mid, grad_latent_full)
    grad_lower_entry = product_left(grad_lower_mid, hidden)
    query_primal, query_back = jax.vjp(
        lambda operand: rotate(operand, cosine[:, None, :], sine[:, None, :]),
        query_three[:, :, NOPE:],
    )
    grad_query_lin = (
        jnp.concatenate([grad_query_nope, query_back(grad_query_rope)[0]], -1)
        .reshape(rows_here, HEADS * (NOPE + ROPE))
        .astype(jnp.bfloat16)
    )
    grad_query_mid = product_t(grad_query_lin, query_out).astype(jnp.bfloat16)
    grad_query_exit = product_left(query_mid, grad_query_lin)
    grad_query_entry = product_left(grad_query_mid, hidden)
    grad_hidden = (
        product_t(grad_query_lin, mix_query)
        + product(grad_query_mid, query_in)
        + product_t(grad_latent_full, mix_down)
        + product(grad_lower_mid, lower_in)
    )
    input_primal, norm_one_back = jax.vjp(lambda operand: normed(operand, mixer_gain), inputs)
    grad_input = (grad_mixed + norm_one_back(grad_hidden)[0]).astype(jnp.bfloat16)
    slot_hot = (jnp.arange(query_entry.shape[0], dtype=jnp.int32) == chosen).astype(jnp.float32)

    def place_slot(gradient):
        return slot_hot[:, None, None] * gradient[None]

    summed = lax.psum(
        (
            place_slot(grad_query_entry),
            place_slot(grad_query_exit),
            place_slot(grad_lower_entry),
            place_slot(grad_lower_exit),
            place_slot(grad_upper_entry),
            place_slot(grad_upper_exit),
            place_slot(grad_output_entry),
            place_slot(grad_output_exit),
        ),
        ("dp", "expert"),
    )
    return (
        block_output,
        grad_input,
        summed[0],
        summed[1],
        summed[2],
        summed[3],
        summed[4],
        summed[5],
        summed[6],
        summed[7],
    )


def solution(mesh):
    in_specs = (
        P(("dp", "expert"), None),
        P(("dp", "expert"), None),
        P("dp"),
        P("dp"),
        P(),
        P(("dp", "expert"), None),
        P(),
        P(),
        P(),
        P(("dp", "expert"), None),
        P(("dp", "expert"), None),
        P(("dp", "expert"), None),
        P(("dp", "expert"), None),
        P(("dp", "expert"), None),
        P(("dp", "expert"), None),
        P(("dp", "expert"), None),
        P("expert", None, None),
        P("expert", None, None),
        P(),
        P(),
        P(),
        P(),
        P(),
        P(),
        P(),
        P(),
    )
    out_specs = (
        P(("dp", "expert"), None),
        P(("dp", "expert"), None),
        P(),
        P(),
        P(),
        P(),
        P(),
        P(),
        P(),
        P(),
    )
    return jax.shard_map(body, mesh=mesh, in_specs=in_specs, out_specs=out_specs, check_vma=False)
```

profile of v0, /device:TPU:0, one launch (start us, length us, event | category | flops | bytes accessed | tf_op | source)
XLA Modules:
  0.0 1593.4 jit_solution(12408658953968711289)
XLA Ops:
  16.5 55.0 %all-gather.9.cloned.1.call-done = bf16[2048,576]{1,0:T(8,128)(2,1)} async-done(((bf16[64,576]{1,0:T(8,128)(2,1)}), bf16[2048,576]{1,0:T(8,128)(2,1)}) %all-gather.9.cloned.1.call-update) | async-done | bytes 2359312 | tf_op jit(solution)/shard_map/all_gather | solution.py:116
  71.5 2.9 fusion.177
  80.3 18.1 %reduce-window.6 = s32[64,15,128]{2,1,0:T(8,128)S(1)} reduce-window(s32[64,15,128]{2,1,0:T(8,128)S(1)} %fusion.88, s32[]{:T(128)} %constant.106.clone.1), window={size=1x1x128 pad=0_0x0_0x127_0}, to_apply=%region_8.9 | reduce-window | flops 15605760 | bytes 983044 | tf_op jit(solution)/shard_map/reduce-window
  111.5 9.6 all-gather
  123.3 3.3 convolution_convert_fusion
  126.6 44.8 %all-gather.13.cloned.1.call-done = bf16[512,4096]{1,0:T(8,128)(2,1)} async-done(((bf16[16,4096]{1,0:T(8,128)(2,1)}), bf16[512,4096]{1,0:T(8,128)(2,1)}) %all-gather.13.cloned.1.call-update) | async-done | bytes 4194320 | tf_op jit(solution)/shard_map/all_gather | solution.py:117
  171.4 22.1 %fusion.178 = f32[2560,4096]{1,0:T(8,128)} fusion(bf16[2560,512]{1,0:T(8,128)(2,1)} %all-gather.11.cloned.1.call-done, bf16[512,4096]{1,0:T(8,128)(2,1)} %all-gather.13.cloned.1.call-done), kind=kOutput, calls=%fused_computation.284 | convolution fusion | flops 10737418240 | bytes 48758784 | tf_op jit(solution)/shard_map/dot_general | solution.py:19
  193.5 21.4 %add_convert_fusion = bf16[2560,4096]{1,0:T(8,128)(2,1)} fusion(f32[2560,4096]{1,0:T(8,128)} %fusion.178, bf16[2560,16]{0,1:T(8,128)(2,1)} %convolution_convert_fusion, bf16[8,16,4096]{2,1,0:T(8,128)(2,1)S(1)} %copy-done, s32[]{:T(128)S(6)} %select_n.79), kind=kOutput, calls=%fused_computation.23 | convolution fusion | flops 356515840 | bytes 63127556 | tf_op jit(solution)/shard_map/dot_general | solution.py:19
  214.9 12.6 copy.222
  227.5 8.1 fusion.172
  235.6 33.1 %all-gather.15.cloned.1.call-done = bf16[2048,3072]{1,0:T(8,128)(2,1)} async-done(((bf16[64,3072]{1,0:T(8,128)(2,1)}), bf16[2048,3072]{1,0:T(8,128)(2,1)}) %all-gather.15.cloned.1.call-update) | async-done | bytes 12582928 | tf_op jit(solution)/shard_map/all_gather | solution.py:115
  268.8 7.2 fusion.179
  276.0 3.5 convolution_add_fusion
  279.5 5.8 copy.180
  288.5 21.0 %fusion.180 = f32[2560,320,16]{0,1,2:T(8,128)} fusion(bf16[2560,64,1]{0,1,2:T(8,128)(2,1)S(1)} %reshape.406, bf16[320,16,64]{0,2,1:T(8,128)(2,1)S(1)} %fusion.64), kind=kOutput, calls=%fused_computation.286 | convolution fusion | flops 1677721600 | bytes 53411840 | tf_op jit(solution)/shard_map/qhd,kd->hqk/dot_general | solution.py:177
  309.5 41.1 %fusion.175 = (f32[16,320]{1,0:T(8,128)S(1)}, f32[16,320,2560]{2,1,0:T(8,128)}) fusion(f32[2560,320,16]{0,1,2:T(8,128)} %fusion.180, bf16[2560,16,128]{2,1,0:T(8,128)(2,1)} %get-tuple-element.26, f32[320,16,192]{0,2,1:T(8,128)} %bitcast.223, pred[320,2560]{1,0:T(8,128)(4,1)S(1)} %fusion.44), kind=kOutput, calls=%fused_computation.281 | convolution fusion | flops 3407866880 | bytes 117755904 | tf_op jit(solution)/shard_map/qhd,khd->hqk/dot_general | solution.py:174
  350.6 17.6 %fusion.6 = f32[16,320]{1,0:T(8,128)S(1)} fusion(f32[16,320,2560]{2,1,0:T(8,128)} %get-tuple-element.50, f32[16,320]{1,0:T(8,128)S(1)} %get-tuple-element.49), kind=kLoop, calls=%fused_computation.17 | loop fusion | flops 26209280 | bytes 52469760 | tf_op jit(solution)/shard_map/reduce_sum | solution.py:185
  368.2 24.5 %fusion.68 = bf16[16,40,8,128]{3,2,1,0:T(8,128)(2,1)S(1)} fusion(bf16[2560,16,128]{2,1,0:T(8,128)(2,1)} %get-tuple-element.27, f32[16,320,2560]{2,1,0:T(8,128)} %get-tuple-element.50, f32[16,320]{1,0:T(8,128)S(1)} %fusion.6, f32[16,320]{1,0:T(8,128)S(1)} %get-tuple-element.49), kind=kOutput, calls=%fused_computation.115 | convolution fusion | flops 3395420160 | bytes 64266240 | tf_op jit(solution)/shard_map/hqk,khd->qhd/dot_general | solution.py:189
  395.1 5.9 convert_add_fusion
  404.3 46.2 %scatter_custom_fusion = bf16[2560,2048]{1,0:T(8,128)(2,1)} fusion(s32[1920]{0:T(1024)} %fusion.136, bf16[320,2048]{1,0:T(8,128)(2,1)S(1)} %multiply_convert_fusion.8, s32[2048]{0:T(1024)} %pad_clamp_fusion.1, bf16[]{:T(256)} %constant.120.clone.1), kind=kCustom, calls=%fused_computation.52 | custom fusion | bytes 10486272 | tf_op jit(solution)/shard_map/scatter | solution.py:209
  450.5 5.3 all-to-all-start
  456.6 7.7 mul.528
  464.2 18.7 %mul.536 = f32[1920,2048]{1,0:T(8,128)} reshape(f32[320,6,2048]{2,1,0:T(8,128)} %mul.528) | data formatting | bytes 31457280 | tf_op jit(solution)/shard_map/mul | solution.py:245
  482.9 144.0 %all_gather.40 = bf16[2048,64]{1,0:T(8,128)(2,1)S(1)} all-gather(bf16[64,64]{1,0:T(8,128)(2,1)S(1)} %copy-done.96), channel_id=1, replica_groups=mesh['dp'=4,'expert'=8] {'dp','expert'}, dimensions={0}, use_global_device_ids=true | all-gather | bytes 270336 | tf_op jit(solution)/shard_map/all_gather | solution.py:123
  630.0 27.3 %scatter_custom_fusion.1 = bf16[2560,2048]{1,0:T(8,128)(2,1)} fusion(s32[1920]{0:T(1024)} %fusion.136, f32[1920,2048]{1,0:T(8,128)} %mul.536, f32[1920]{0:T(1024)S(1)} %mul.534, bf16[]{:T(256)} %constant.120.clone.1), kind=kCustom, calls=%fused_computation.51 | custom fusion | flops 7864320 | bytes 26222592 | tf_op jit(solution)/shard_map/scatter | solution.py:256
  657.3 5.4 all-to-all-start.2
  662.7 49.2 %fusion.16 = f32[8,8,40,2816]{3,2,0,1:T(8,128)} fusion(bf16[8,2048,2816]{2,1,0:T(8,128)(2,1)} %param.42, bf16[8,8,40,2048]{3,2,1,0:T(8,128)(2,1)} %all-to-all-done), kind=kOutput, calls=%fused_computation.39 | convolution fusion | flops 29527900160 | bytes 131596288 | tf_op jit(solution)/shard_map/secd,edf->secf/dot_general | solution.py:212
  711.8 30.5 %convert_bitcast_fusion.1 = bf16[8,8,40,2048]{3,2,0,1:T(8,128)(2,1)} fusion(bf16[8,1408,2048]{2,1,0:T(8,128)(2,1)} %param.43, f32[8,8,40,2816]{3,2,0,1:T(8,128)} %fusion.16), kind=kOutput, calls=%fused_computation.43 | convolution fusion | flops 14787215360 | bytes 85458944 | tf_op jit(solution)/shard_map/secf,efd->secd/dot_general | solution.py:219
  742.4 10.0 copy.195
  752.4 26.8 %all-to-all-done.2 = bf16[8,8,40,2048]{3,2,1,0:T(8,128)(2,1)} async-done(((bf16[8,8,40,2048]{3,2,1,0:T(8,128)(2,1)}), bf16[8,8,40,2048]{3,2,1,0:T(8,128)(2,1)}, u32[]{:S(2)}, u32[]{:S(2)}) %all-to-all-start.2) | async-done | bytes 10485792 | tf_op jit(solution)/shard_map/all_to_all | solution.py:257
  779.2 5.2 all-to-all-start.1
  784.4 45.9 %bitcast_multiply_fusion.1 = (f32[8,8,40,1408]{3,2,0,1:T(8,128)}, f32[8,8,40,1408]{3,2,0,1:T(8,128)}) fusion(f32[8,8,40,2816]{3,2,0,1:T(8,128)} %fusion.16, bf16[8,1408,2048]{2,1,0:T(8,128)(2,1)} %param.43, bf16[8,8,40,2048]{3,2,1,0:T(8,128)(2,1)} %all-to-all-done.2), kind=kOutput, calls=%fused_computation.34 | convolution fusion | flops 14814412800 | bytes 114294784 | tf_op jit(solution)/shard_map/secd,efd->secf/dot_general | solution.py:264
  830.3 51.8 %convert_bitcast_fusion = bf16[8,8,40,2048]{3,2,0,1:T(8,128)(2,1)} fusion(bf16[8,2048,2816]{2,1,0:T(8,128)(2,1)} %param.42, f32[8,8,40,1408]{3,2,0,1:T(8,128)} %get-tuple-element.25, f32[8,8,40,1408]{3,2,0,1:T(8,128)} %get-tuple-element.24), kind=kOutput, calls=%fused_computation.42 | convolution fusion | flops 29547560960 | bytes 131596288 | tf_op jit(solution)/shard_map/secf,edf->secd/dot_general | solution.py:269
  882.0 10.1 copy.199
  892.1 8.8 all-to-all-done.1
  900.9 5.2 all-to-all-start.3
  910.9 21.6 %gather_fusion = bf16[1920,2048]{1,0:T(8,128)(2,1)} fusion(bf16[2560,2048]{1,0:T(8,128)(2,1)} %bitcast.22, s32[2048]{0:T(1024)S(1)} %pad_clamp_fusion), kind=kCustom, calls=%fused_computation.1 | custom fusion | bytes 15736320 | tf_op jit(solution)/shard_map/gather | solution.py:224
  932.5 14.3 reshape.362
  946.8 14.7 multiply_reduce_fusion.1
  961.6 61.0 %all-to-all-done.3 = bf16[8,8,40,2048]{3,2,1,0:T(8,128)(2,1)} async-done(((bf16[8,8,40,2048]{3,2,1,0:T(8,128)(2,1)}), bf16[8,8,40,2048]{3,2,1,0:T(8,128)(2,1)}, u32[]{:S(2)}, u32[]{:S(2)}) %all-to-all-start.3) | async-done | bytes 10485792 | tf_op jit(solution)/shard_map/all_to_all | solution.py:272
  1022.6 21.6 %gather_fusion.1 = bf16[1920,2048]{1,0:T(8,128)(2,1)} fusion(bf16[2560,2048]{1,0:T(8,128)(2,1)} %bitcast.28, s32[2048]{0:T(1024)S(1)} %pad_clamp_fusion), kind=kCustom, calls=%fused_computation.2 | custom fusion | bytes 15736320 | tf_op jit(solution)/shard_map/gather | solution.py:276
  1044.2 14.3 reshape.363
  1058.5 12.0 reduce_sum.182
  1070.7 14.7 fusion.181
  1085.4 16.3 %fusion.87 = (f32[320,2816]{1,0:T(8,128)}, f32[320,2816]{1,0:T(8,128)}) fusion(f32[320,5632]{1,0:T(8,128)} %fusion.181, bf16[320,2048]{1,0:T(8,128)(2,1)S(1)} %copy-done.17, bf16[2816,2048]{1,0:T(8,128)(2,1)} %all-gather.21.cloned.1.call-done), kind=kOutput, calls=%fused_computation.145 | convolution fusion | flops 3703603200 | bytes 27262976 | tf_op jit(solution)/shard_map/dot_general | solution.py:23
  1101.7 15.7 fusion.40
  1117.5 3.8 multiply_reduce_fusion.3
  1124.5 2.9 fusion.166
  1128.8 42.6 %multiply_reduce_fusion = (f32[16,320]{1,0:T(8,128)S(1)}, f32[16,320,2560]{2,1,0:T(8,128)}) fusion(f32[16,320,2560]{2,1,0:T(8,128)} %get-tuple-element.50, f32[16,320]{1,0:T(8,128)S(1)} %log_add_fusion, bf16[2560,16,128]{2,1,0:T(8,128)(2,1)} %get-tuple-element.27, bf16[40,16,8,128]{3,2,1,0:T(8,128)(2,1)S(1)} %fusion.67), kind=kOutput, calls=%fused_computation.13 | convolution fusion | flops 3394759680 | bytes 116695040 | tf_op jit(solution)/shard_map/qhd,khd->hqk/dot_general | solution.py:290
  1171.4 22.1 %fusion.21 = bf16[2560,16,128]{0,2,1:T(8,128)(2,1)} fusion(f32[16,320,2560]{2,1,0:T(8,128)} %get-tuple-element.50, f32[16,320]{1,0:T(8,128)S(1)} %log_add_fusion, bf16[40,16,8,128]{3,2,1,0:T(8,128)(2,1)S(1)} %fusion.67), kind=kOutput, calls=%fused_computation.44 | convolution fusion | flops 3381657600 | bytes 64245760 | tf_op jit(solution)/shard_map/hqk,qhd->khd/dot_general | solution.py:316
  1193.5 41.4 %multiply_convert_fusion = bf16[16,320,2560]{2,1,0:T(8,128)(2,1)} fusion(f32[16,320,2560]{2,1,0:T(8,128)} %get-tuple-element.58, f32[16,320,2560]{2,1,0:T(8,128)} %get-tuple-element.50, f32[16,320]{1,0:T(8,128)S(1)} %get-tuple-element.57, f32[16,320]{1,0:T(8,128)S(1)} %log_add_fusion), kind=kLoop, calls=%fused_computation.12 | loop fusion | flops 52428800 | bytes 131112960 | tf_op jit(solution)/shard_map/convert_element_type | solution.py:295
  1234.9 15.1 multiply_bitcast_fusion
  1250.0 11.0 fusion.42
  1262.0 18.3 %multiply_bitcast_fusion.1 = bf16[320,16,128]{0,2,1:T(8,128)(2,1)} fusion(bf16[16,320,2560]{2,1,0:T(8,128)(2,1)} %multiply_convert_fusion, bf16[2560,16,128]{2,1,0:T(8,128)(2,1)} %get-tuple-element.26), kind=kOutput, calls=%fused_computation.82 | convolution fusion | flops 3356753920 | bytes 38010880 | tf_op jit(solution)/shard_map/hqk,khd->qhd/dot_general | solution.py:297
  1280.4 10.0 maximum_convert_fusion
  1293.2 4.2 copy-done.1
  1297.4 3.9 fusion.131
  1302.5 15.2 bitcast_multiply_fusion.2
  1323.1 17.4 %add_convert_fusion.6 = bf16[2560,512]{1,0:T(8,128)(2,1)} fusion(f32[2560,512]{1,0:T(8,128)} %fusion.131, bf16[2560,4096]{0,1:T(8,128)(2,1)} %bitcast.217, bf16[512,4096]{1,0:T(8,128)(2,1)S(1)} %copy-done.98), kind=kOutput, calls=%fused_computation.56 | convolution fusion | flops 10740039680 | bytes 33030144 | tf_op jit(solution)/shard_map/dot_general | solution.py:23
  1349.6 10.5 fusion.187
  1364.5 19.4 %reduce-scatter.7.cloned.1.call-done = bf16[320,512]{1,0:T(8,128)(2,1)} async-done(((bf16[2560,512]{1,0:T(8,128)(2,1)}), bf16[320,512]{1,0:T(8,128)(2,1)}) %reduce-scatter.7.cloned.1.call-update) | async-done | bytes 327696 | tf_op jit(solution)/shard_map/reduce_scatter | solution.py:338
  1393.6 8.6 fusion.182
  1402.3 12.1 fusion.50
  1420.8 154.7 %all-reduce.11.cloned.1.call-done = (f32[8,16,2048]{2,1,0:T(8,128)}, f32[8,16,3072]{2,1,0:T(8,128)}, f32[8,16,2048]{2,1,0:T(8,128)}, f32[8,16,576]{2,1,0:T(8,128...) async-done(((f32[8,16,2048]{2,1,0:T(8,128)}, f32[8,16,3072]{2,1,0:T(8,128)}, f32[8,16,2048]{2,1,0:T(8,128)}, ...) | async-done | bytes 8421392 | tf_op jit(solution)/shard_map/psum | solution.py:378
  (335 shorter events, 100.9 us)
Async XLA Ops:
  7.2 186.3 %copy-start = (bf16[8,16,4096]{2,1,0:T(8,128)(2,1)S(1)}, bf16[8,16,4096]{2,1,0:T(8,128)(2,1)}, u32[]{:S(2)}) copy-start(bf16[8,16,4096]{2,1,0:T(8,128)(2,1)} %param.49) | copy-start | bytes 3145732
  7.2 64.3 %all-gather.9.cloned.1.call-start = ((), (), s32[]{:S(2)}) async-start(), calls=%async_computation.6 | async-start | bytes 2703360 | tf_op jit(solution)/shard_map/all_gather | solution.py:116
  7.9 115.4 %all-gather.11.cloned.1.call-start = ((), (), s32[]{:S(2)}) async-start(), calls=%async_computation.7 | async-start | bytes 2949120 | tf_op jit(solution)/shard_map/all_gather | solution.py:159
  15.1 253.7 %copy-start.8 = (bf16[320,2048]{1,0:T(8,128)(2,1)}, bf16[320,2048]{1,0:T(8,128)(2,1)S(1)}, u32[]{:S(2)}) copy-start(bf16[320,2048]{1,0:T(8,128)(2,1)S(1)} %fusion.56) | copy-start | bytes 3932164
  16.5 59.0 %copy-start.70 = (bf16[320,16]{0,1:T(8,128)(2,1)}, bf16[320,16]{0,1:T(8,128)(2,1)S(1)}, u32[]{:S(2)}) copy-start(bf16[320,16]{0,1:T(8,128)(2,1)S(1)} %convolution_convert_fusion.4) | copy-start | bytes 30724
  16.5 59.9 %copy-start.80 = (f32[512]{0:T(512)S(1)}, f32[512]{0:T(512)}, u32[]{:S(2)}) copy-start(f32[512]{0:T(512)} %param.33) | copy-start | bytes 6148
  75.5 24.0 %copy-start.69 = (s32[2560]{0:T(1024)S(1)}, s32[2560]{0:T(1024)}, u32[]{:S(2)}) copy-start(s32[2560]{0:T(1024)} %param.28) | copy-start | bytes 30724
  77.3 94.2 %all-gather.13.cloned.1.call-start = ((), (), s32[]{:S(2)}) async-start(), calls=%async_computation.8 | async-start | bytes 4325376 | tf_op jit(solution)/shard_map/all_gather | solution.py:117
  78.0 190.8 %all-gather.15.cloned.1.call-start = ((), (), s32[]{:S(2)}) async-start(), calls=%async_computation.9 | async-start | bytes 12976128 | tf_op jit(solution)/shard_map/all_gather | solution.py:115
  78.6 316.5 %all-gather.17.cloned.1.call-start = ((), (), s32[]{:S(2)}) async-start(), calls=%async_computation.10 | async-start | bytes 8650752 | tf_op jit(solution)/shard_map/all_gather | solution.py:118
  79.2 991.6 %all-gather.19.cloned.1.call-start = ((), (), s32[]{:S(2)}) async-start(), calls=%async_computation.11 | async-start | bytes 23789568 | tf_op jit(solution)/shard_map/all_gather | solution.py:121
  104.2 171.8 %copy-start.64 = (bf16[320,16]{0,1:T(8,128)(2,1)}, bf16[320,16]{0,1:T(8,128)(2,1)S(1)}, u32[]{:S(2)}) copy-start(bf16[320,16]{0,1:T(8,128)(2,1)S(1)} %convolution_convert_fusion.3) | copy-start | bytes 30724
  123.3 165.2 %copy-start.24 = (bf16[2560,64,1]{0,1,2:T(8,128)(2,1)}, bf16[2560,64,1]{0,1,2:T(8,128)(2,1)S(1)}, u32[]{:S(2)}) copy-start(bf16[2560,64,1]{0,1,2:T(8,128)(2,1)S(1)} %reshape.406) | copy-start | bytes 983044
  279.5 7.2 copy-start.52
  279.5 7.3 copy-start.53
  288.5 21.0 %copy-start.18 = (bf16[320,16,64]{0,2,1:T(8,128)(2,1)}, bf16[320,16,64]{0,2,1:T(8,128)(2,1)S(1)}, u32[]{:S(2)}) copy-start(bf16[320,16,64]{0,2,1:T(8,128)(2,1)S(1)} %fusion.64) | copy-start | bytes 1966084
  350.6 17.6 %copy-start.59 = (f32[16,320]{1,0:T(8,128)}, f32[16,320]{1,0:T(8,128)S(1)}, u32[]{:S(2)}) copy-start(f32[16,320]{1,0:T(8,128)S(1)} %get-tuple-element.49) | copy-start | bytes 61444
  368.2 24.5 %copy-start.66 = (f32[16,320]{1,0:T(8,128)}, f32[16,320]{1,0:T(8,128)S(1)}, u32[]{:S(2)}) copy-start(f32[16,320]{1,0:T(8,128)S(1)} %fusion.6) | copy-start | bytes 61444
  368.2 26.9 %copy-start.12 = (bf16[320,2048]{1,0:T(8,128)(2,1)S(1)}, bf16[320,2048]{1,0:T(8,128)(2,1)}, u32[]{:S(2)}) copy-start(bf16[320,2048]{1,0:T(8,128)(2,1)} %param.26) | copy-start | bytes 3932164
  404.3 46.2 %copy-start.21 = (bf16[320,2048]{1,0:T(8,128)(2,1)}, bf16[320,2048]{1,0:T(8,128)(2,1)S(1)}, u32[]{:S(2)}) copy-start(bf16[320,2048]{1,0:T(8,128)(2,1)S(1)} %multiply_convert_fusion.8) | copy-start | bytes 3932164
  450.5 206.8 %all-to-all-start = ((bf16[8,8,40,2048]{3,2,1,0:T(8,128)(2,1)}), bf16[8,8,40,2048]{3,2,1,0:T(8,128)(2,1)}, u32[]{:S(2)}, u32[]{:S(2)}) async-start(bf16[8,8,40,2048]{3,2,1,0:T(8,128)(2,1)} %bitcast.225), calls=%async_computation | async-start | bytes 20971520 | tf_op jit(solution)/shard_map/all_to_all | solution.py:214
  455.8 629.6 %all-gather.21.cloned.1.call-start = ((), (), s32[]{:S(2)}) async-start(), calls=%async_computation.12 | async-start | bytes 11894784 | tf_op jit(solution)/shard_map/all_gather | solution.py:122
  464.2 18.7 %copy-start.96 = (bf16[64,64]{1,0:T(8,128)(2,1)S(1)}, bf16[64,64]{1,0:T(8,128)(2,1)}, u32[]{:S(2)}) copy-start(bf16[64,64]{1,0:T(8,128)(2,1)} %param.39) | copy-start | bytes 24580
  464.2 162.7 %copy-start.22 = (bf16[320,2048]{1,0:T(8,128)(2,1)S(1)}, bf16[320,2048]{1,0:T(8,128)(2,1)}, u32[]{:S(2)}) copy-start(bf16[320,2048]{1,0:T(8,128)(2,1)} %copy-done.21) | copy-start | bytes 3932164
  464.2 165.4 %copy-start.62 = (s32[320,6]{0,1:T(8,128)S(1)}, s32[320,6]{0,1:T(8,128)}, u32[]{:S(2)}) copy-start(s32[320,6]{0,1:T(8,128)} %param.31) | copy-start | bytes 23044
  629.8 27.4 %copy-start.31 = (f32[320,6]{1,0:T(8,128)}, f32[320,6]{1,0:T(8,128)S(1)}, u32[]{:S(2)}) copy-start(f32[320,6]{1,0:T(8,128)S(1)} %copy.188) | copy-start | bytes 23044
  657.3 121.9 %all-to-all-start.2 = ((bf16[8,8,40,2048]{3,2,1,0:T(8,128)(2,1)}), bf16[8,8,40,2048]{3,2,1,0:T(8,128)(2,1)}, u32[]{:S(2)}, u32[]{:S(2)}) async-start(bf16[8,8,40,2048]{3,2,1,0:T(8,128)(2,1)} %bitcast.226), calls=%async_computation.2 | async-start | bytes 20971520 | tf_op jit(solution)/shard_map/all_to_all | solution.py:257
  779.2 121.7 %all-to-all-start.1 = ((bf16[8,8,40,2048]{3,2,1,0:T(8,128)(2,1)}), bf16[8,8,40,2048]{3,2,1,0:T(8,128)(2,1)}, u32[]{:S(2)}, u32[]{:S(2)}) async-start(bf16[8,8,40,2048]{3,2,1,0:T(8,128)(2,1)} %copy.195), calls=%async_computation.1 | async-start | bytes 20971520 | tf_op jit(solution)/shard_map/all_to_all | solution.py:221
  892.1 14.3 copy-start.17
  892.1 17.2 %copy-start.77 = (s32[1920]{0:T(1024)S(1)}, s32[1920]{0:T(1024)}, u32[]{:S(2)}) copy-start(s32[1920]{0:T(1024)} %fusion.136) | copy-start | bytes 23044
  892.1 17.2 %copy-start.47 = (f32[320,64]{1,0:T(8,128)S(1)}, f32[320,64]{1,0:T(8,128)}, u32[]{:S(2)}) copy-start(f32[320,64]{1,0:T(8,128)} %get-tuple-element.38) | copy-start | bytes 245764
  900.9 121.7 %all-to-all-start.3 = ((bf16[8,8,40,2048]{3,2,1,0:T(8,128)(2,1)}), bf16[8,8,40,2048]{3,2,1,0:T(8,128)(2,1)}, u32[]{:S(2)}, u32[]{:S(2)}) async-start(bf16[8,8,40,2048]{3,2,1,0:T(8,128)(2,1)} %copy.199), calls=%async_computation.3 | async-start | bytes 20971520 | tf_op jit(solution)/shard_map/all_to_all | solution.py:272
  906.1 455.6 %reduce-scatter.9.cloned.1.call-start = ((), (), s32[]{:S(2)}) async-start(), calls=%async_computation.14 | async-start | bytes 737280 | tf_op jit(solution)/shard_map/reduce_scatter | solution.py:341
  932.5 14.3 copy-start.32
  1058.5 12.1 copy-start.63
  1058.5 12.1 copy-start.29
  1058.5 12.1 copy-start.76
  1058.5 12.1 copy-start.83
  1070.6 14.7 copy-start.45
  1101.7 15.8 copy-start.6
  1101.7 15.8 copy-start.44
  1101.7 15.8 copy-start.79
  1234.9 15.1 copy-start.19
  1250.0 11.0 copy-start.38
  1302.4 15.4 copy-start.51
  1302.4 81.5 %reduce-scatter.7.cloned.1.call-start = ((), (), s32[]{:S(2)}) async-start(), calls=%async_computation.13 | async-start | bytes 2949120 | tf_op jit(solution)/shard_map/reduce_scatter | solution.py:338
  1323.1 17.4 %copy-start.9 = (bf16[320,2048]{1,0:T(8,128)(2,1)S(1)}, bf16[320,2048]{1,0:T(8,128)(2,1)}, u32[]{:S(2)}) copy-start(bf16[320,2048]{1,0:T(8,128)(2,1)} %copy-done.8) | copy-start | bytes 3932164
  1323.1 18.4 %copy-start.65 = (bf16[320,16]{0,1:T(8,128)(2,1)S(1)}, bf16[320,16]{0,1:T(8,128)(2,1)}, u32[]{:S(2)}) copy-start(bf16[320,16]{0,1:T(8,128)(2,1)} %copy-done.64) | copy-start | bytes 30724
  1343.9 231.6 %all-reduce.11.cloned.1.call-start = ((), (), s32[]{:S(2)}) async-start(), calls=%async_computation.15 | async-start | bytes 16908288 | tf_op jit(solution)/shard_map/psum | solution.py:378
  1349.6 12.1 copy-start.36
  1349.6 13.2 copy-start.34
  1349.6 34.3 %copy-start.81 = (f32[512]{0:T(512)S(1)}, f32[512]{0:T(512)}, u32[]{:S(2)}) copy-start(f32[512]{0:T(512)} %param.33) | copy-start | bytes 6148
  1360.1 23.9 %copy-start.15 = (f32[320,576]{1,0:T(8,128)S(1)}, f32[320,576]{1,0:T(8,128)}, u32[]{:S(2)}) copy-start(f32[320,576]{1,0:T(8,128)} %copy-done.14) | copy-start | bytes 2211844
  1360.1 25.1 %copy-start.89 = (f32[320]{0:T(512)S(1)}, f32[320]{0:T(512)}, u32[]{:S(2)}) copy-start(f32[320]{0:T(512)} %copy-done.88) | copy-start | bytes 3844
  1360.1 25.1 %copy-start.85 = (f32[320]{0:T(512)S(1)}, f32[320]{0:T(512)}, u32[]{:S(2)}) copy-start(f32[320]{0:T(512)} %copy-done.84) | copy-start | bytes 3844
  1360.1 26.2 %copy-start.71 = (bf16[320,16]{0,1:T(8,128)(2,1)S(1)}, bf16[320,16]{0,1:T(8,128)(2,1)}, u32[]{:S(2)}) copy-start(bf16[320,16]{0,1:T(8,128)(2,1)} %copy-done.70) | copy-start | bytes 30724
  1362.7 27.0 %copy-start.48 = (f32[16,2048]{1,0:T(8,128)S(1)}, f32[16,2048]{1,0:T(8,128)}, u32[]{:S(2)}) copy-start(f32[16,2048]{1,0:T(8,128)} %fusion.71) | copy-start | bytes 393220
  1364.5 25.2 %copy-start.49 = (f32[16,2048]{1,0:T(8,128)S(1)}, f32[16,2048]{1,0:T(8,128)}, u32[]{:S(2)}) copy-start(f32[16,2048]{1,0:T(8,128)} %fusion.183) | copy-start | bytes 393220
  1393.6 8.6 copy-start.7
  1393.6 8.6 copy-start.26
  1402.3 12.1 copy-start.56
  1402.3 12.1 copy-start.68
  1402.3 12.1 copy-start.99
  1575.6 7.6 copy-start.27
  (52 other events, 175.0 us)
Sparse Core Ops, SparseCore 0:
  10.9 60.6 all-gather.8
  77.4 29.0 all-gather.10
  109.3 62.0 all-gather.12
  174.2 94.5 all-gather.14
  271.5 75.7 all-gather.16
  349.9 150.1 all-gather.18
  502.9 141.9 all-gather.20
  1302.5 30.9 reduce-scatter.8
  1344.0 39.8 reduce-scatter.6
  1392.1 183.4 all-reduce.10
where the time goes:
time: 1600 us; the launch traced here: 1590 us
  matrix products  590 us (37%)
  waiting for transfers between devices  408 us (26%)
  local copies, waits for them, and re-layouts  228 us (14%)
  other arithmetic  175 us (11%)
  blocking collectives  154 us (10%)
  starting transfers between devices  21.6 us (1%)
  between operations  17.5 us (1%)
    psum x1, waiting for transfers between devices, body(): lax.psum((place_slot(grad_query_entry), place_slot(grad_query_exit), plac...  155 us
    all_gather x1, blocking collectives, body(): lax.all_gather(router_matrix, ('dp', 'expert'), axis=0, tiled=True)  144 us
    dot_general x15, matrix products, product(): return jnp.dot(left, right, preferred_element_type=jnp.float32)  101 us
    dot_general x15, matrix products, product_t(): lax.dot_general(left, right, (((1,), (1,)), ((), ())), preferred_element_...  81.1 us
    all_to_all x1, waiting for transfers between devices, body(): lax.all_to_all(grad_slot, 'expert', split_axis=0, concat_axis=0, tiled=True)  61 us
    all_gather x1, waiting for transfers between devices, body(): lax.all_gather(latent_down, ('dp', 'expert'), axis=0, tiled=True)  55 us
    dot_general x1, matrix products, body(): jnp.einsum('secf,edf->secd', grad_gate_up, expert_in, preferred_element_t...  51.8 us
    dot_general x1, matrix products, body(): jnp.einsum('secd,edf->secf', lax.all_to_all(sender, 'expert', split_axis=...  49.2 us
  transfers between devices with their start and end apart: 14, of which 8 were waited for; matrix products, arithmetic and copies ran while one was open for 47% of the time, Pallas kernels for 0%

commit v1 on v0

v1 whole, which is shorter than its diff:
```python
import functools

import jax
import jax.numpy as jnp
from jax import lax
from jax.experimental import pallas as pl
from jax.experimental.pallas import tpu as pltpu
from jax.sharding import PartitionSpec as P

D = 2048
HEADS = 16
NOPE = 128
ROPE = 64
VDIM = 128
KVR = 512
TOPK = 6
SEGLEN = 128
TRUNK = 1024
TREE = 2560
LATW = 640
HALF = ROPE // 2
VMEM_LIMIT = 66_000_000
BF = jnp.bfloat16
F32 = jnp.float32


def product(left, right):
    return jnp.dot(left, right, preferred_element_type=F32)


def product_t(left, right):
    return lax.dot_general(left, right, (((1,), (1,)), ((), ())), preferred_element_type=F32)


def product_left(left, right):
    return lax.dot_general(left, right, (((0,), (0,)), ((), ())), preferred_element_type=F32)


def normed(operand, gain):
    return operand * lax.rsqrt(jnp.mean(operand * operand, axis=-1, keepdims=True) + 1e-06) * gain


def rotate(operand, cosine, sine):
    half_width = operand.shape[-1] // 2
    turned = jnp.concatenate([-operand[..., half_width:], operand[..., :half_width]], -1)
    return operand * cosine + turned * sine


def select_slot(bank, chosen):
    return lax.dynamic_index_in_dim(bank, chosen, 0, keepdims=False)


def split_heads(matrix):
    rows = matrix.shape[0]
    three = matrix.reshape(rows, HEADS, NOPE + ROPE)
    nope = three[:, :, :NOPE].reshape(rows, HEADS * NOPE)
    rope = three[:, :, NOPE:].reshape(rows, HEADS // 2, 2, 2, HALF)
    return nope, rope.transpose(0, 1, 3, 2, 4).reshape(rows, HEADS * ROPE)


def join_heads(nope, rope):
    rows = nope.shape[0]
    turned = rope.reshape(rows, HEADS // 2, 2, 2, HALF).transpose(0, 1, 3, 2, 4)
    return jnp.concatenate(
        [nope.reshape(rows, HEADS, NOPE), turned.reshape(rows, HEADS, ROPE)], -1
    ).reshape(rows, HEADS * (NOPE + ROPE))


def lane_iota(shape):
    return lax.broadcasted_iota(jnp.int32, shape, len(shape) - 1)


def row_iota(shape):
    return lax.broadcasted_iota(jnp.int32, shape, len(shape) - 2)


LOG2E = 1.4426950408889634
SCALING = 1.0 / (NOPE + ROPE) ** 0.5


def place_keys(nb, info, lat, latsel):
    latsel[:TRUNK, :] = lat[:TRUNK, :]
    for m in range(nb):
        for side in range(2):
            start = pl.multiple_of(info[side * nb + m] * SEGLEN, SEGLEN)
            at = TRUNK + (2 * m + side) * SEGLEN
            latsel[at : at + SEGLEN, :] = lat[pl.ds(start, SEGLEN), :]


def rotary_keys(tail, kr):
    tail = tail.astype(F32)
    first = jnp.where(lane_iota(tail.shape) % ROPE < HALF, tail, 0.0)
    kr[0] = first.astype(BF)
    kr[1] = pltpu.roll(first, HALF, 1).astype(BF)


def local_limit(nb, info, m, key, row):
    return jnp.where(
        key < SEGLEN,
        (row + 1) * info[2 * nb + m] - 1,
        SEGLEN + SEGLEN * info[3 * nb + m] - 1,
    )


def attend_kernel(
    nb, info, qn, qr, cosp, sinp, qlim, lat, up, upx, out, lse, kv,
    latsel, kr, bias, near, st, sl, pt,
):
    rows_all = qn.shape[0]

    @pl.when(pl.program_id(0) == 0)
    def _():
        place_keys(nb, info, lat, latsel)
        rotary_keys(latsel[:, KVR:], kr)
        bias[...] = jnp.where(row_iota((TRUNK, rows_all)) <= qlim[...], 0.0, -1e30)
        key = row_iota((2 * SEGLEN, SEGLEN))
        row = lane_iota((2 * SEGLEN, SEGLEN))
        for m in range(nb):
            near[m] = jnp.where(key <= local_limit(nb, info, m, key, row), 0.0, -1e30)

    raw = qr[...]
    qrot = (raw * cosp[...] + pltpu.roll(raw, ROPE, 1) * sinp[...]).astype(BF)
    keys = latsel.shape[0]
    rows = keys // 2 if keys % 512 == 0 else keys
    for at in range(0, keys, rows):
        kv[at : at + rows, :] = (
            product(latsel[at : at + rows, :KVR], up[...])
            + product(latsel[at : at + rows, KVR:], upx[...])
        ).astype(BF)
    blocks = [slice(m * SEGLEN, (m + 1) * SEGLEN) for m in range(nb)]
    nears = [slice(TRUNK + 2 * m * SEGLEN, TRUNK + 2 * (m + 1) * SEGLEN) for m in range(nb)]
    chunks = [slice(at, at + 256) for at in range(0, TRUNK, 256)]
    peaks = []
    for a in range(2):
        q = jnp.concatenate([qn[:, a * 128 : a * 128 + 128], qrot], 1)
        k = jnp.concatenate([kv[:, a * 256 : a * 256 + 128], kr[a]], 1)
        peak = None
        for there in chunks:
            scores = product_t(k[there], q) + bias[there, :]
            st[a, there, :] = scores
            top = jnp.max(scores, axis=0, keepdims=True)
            peak = top if peak is None else jnp.maximum(peak, top)
        tops = []
        for m in range(nb):
            scores = product_t(k[nears[m]], q[blocks[m]]) + near[m]
            sl[a, m] = scores
            tops.append(jnp.max(scores, axis=0, keepdims=True))
        peak = jnp.maximum(peak, jnp.concatenate(tops, 1))
        peaks.append(peak * (SCALING * LOG2E))
    levels = []
    for a in range(2):
        v = kv[:, a * 256 + 128 : a * 256 + 256]
        total = None
        for there in chunks:
            e = jnp.exp2(st[a, there, :] * (SCALING * LOG2E) - peaks[a])
            part = jnp.sum(e, axis=0, keepdims=True)
            total = part if total is None else total + part
            pt[a, there, :] = e.astype(BF)
        parts, sums = [], []
        for m in range(nb):
            e = jnp.exp2(sl[a, m] * (SCALING * LOG2E) - peaks[a][:, blocks[m]])
            sums.append(jnp.sum(e, axis=0, keepdims=True))
            parts.append(product_left(e.astype(BF), v[nears[m]]))
        total = total + jnp.concatenate(sums, 1)
        got = product_left(pt[a], v[:TRUNK]) + jnp.concatenate(parts, 0)
        inverse = jnp.broadcast_to(1.0 / total, (128, rows_all)).T
        out[:, a * 128 : a * 128 + 128] = (got * inverse).astype(BF)
        levels.append(peaks[a] + jnp.log(total) * LOG2E)
    lse[0] = jnp.concatenate(levels + [jnp.zeros((6, rows_all), F32)], 0)


def attend_back_kernel(
    nb, info, qn, qr, cosp, sinp, qlim, tails, kv, up, upx, do, stats,
    dqn, dqr, gup, dlat, tail, kr, bias, near, dss, dkv, acc, dkr,
):
    step = pl.program_id(0)
    rows_all = qn.shape[0]

    @pl.when(step == 0)
    def _():
        place_keys(nb, info, tails, tail)
        rotary_keys(tail[...], kr)
        bias[...] = jnp.where(row_iota((TRUNK, rows_all)) <= qlim[...], 0.0, -1e30)
        key = row_iota((2 * SEGLEN, SEGLEN))
        row = lane_iota((2 * SEGLEN, SEGLEN))
        for m in range(nb):
            near[m] = jnp.where(key <= local_limit(nb, info, m, key, row), 0.0, -1e30)
        acc[...] = jnp.zeros_like(acc)
        dkr[...] = jnp.zeros_like(dkr)

    raw = qr[...]
    qrot = (raw * cosp[...] + pltpu.roll(raw, ROPE, 1) * sinp[...]).astype(BF)
    dq_rope = None
    for a in range(2):
        q = jnp.concatenate([qn[:, a * 128 : a * 128 + 128], qrot], 1)
        k = jnp.concatenate([kv[:, a * 256 : a * 256 + 128], kr[a]], 1)
        v = kv[:, a * 256 + 128 : a * 256 + 256]
        g = do[:, a * 128 : a * 128 + 128]
        level = stats[0, a : a + 1, :]
        delta = stats[0, 2 + a : 3 + a, :]
        mine = lane_iota((1, 128)) % ROPE
        mine = (mine < HALF) if a == 0 else (mine >= HALF)

        def block(there, here, hide):
            scores = product_t(k[there], q[here]) + hide
            p = jnp.exp2(scores * (SCALING * LOG2E) - level[:, here])
            ds = (p * (product_t(v[there], g[here]) - delta[:, here])).astype(BF)
            dk = product(ds, q[here]) * SCALING
            dkv[there, a * 256 : a * 256 + 128] = dk[:, :128].astype(BF)
            dkv[there, a * 256 + 128 : a * 256 + 256] = product(p.astype(BF), g[here]).astype(BF)
            dkr[there, :] += jnp.where(mine, dk[:, 128:], 0.0)
            return ds

        for at in range(0, TRUNK, 256):
            there = slice(at, at + 256)
            dss[there, :] = block(there, slice(0, rows_all), bias[there, :])
        parts = []
        for m in range(nb):
            here = slice(m * SEGLEN, (m + 1) * SEGLEN)
            there = slice(TRUNK + 2 * m * SEGLEN, TRUNK + 2 * (m + 1) * SEGLEN)
            parts.append(product_left(block(there, here, near[m]), k[there]))
        dq = (product_left(dss[...], k[:TRUNK]) + jnp.concatenate(parts, 0)) * SCALING
        dqn[:, a * 128 : a * 128 + 128] = dq[:, :128].astype(BF)
        dq_rope = dq[:, 128:] if dq_rope is None else dq_rope + dq[:, 128:]
    dqr[...] = (dq_rope * cosp[...] + pltpu.roll(dq_rope * sinp[...], ROPE, 1)).astype(BF)
    gup[...] = product_left(tail[...], dkv[...])
    for at in range(0, tail.shape[0], 256):
        acc[at : at + 256, :KVR] += product_t(dkv[at : at + 256, :], up[...])
        acc[at : at + 256, KVR:] += product_t(dkv[at : at + 256, :], upx[...])

    @pl.when(step == pl.num_programs(0) - 1)
    def _():
        rope = dkr[...]
        folded = rope + pltpu.roll(rope, 128 - HALF, 1)
        keep = lane_iota(rope.shape) % ROPE < HALF
        acc[:, KVR:] += jnp.where(keep, folded, 0.0)
        dlat[:TRUNK, :] = acc[:TRUNK, :]
        dlat[TRUNK:, :] = jnp.zeros((TREE - TRUNK, LATW), F32)
        for m in range(nb):
            for side in range(2):
                start = pl.multiple_of(info[side * nb + m] * SEGLEN, SEGLEN)
                at = TRUNK + (2 * m + side) * SEGLEN
                dlat[pl.ds(start, SEGLEN), :] += acc[at : at + SEGLEN, :]


def pair_spec(rows, width):
    return pl.BlockSpec((rows, width), lambda i, info: (0, i))


def lead_spec(rows, width):
    return pl.BlockSpec((1, rows, width), lambda i, info: (i, 0, 0))


def whole_spec(shape):
    return pl.BlockSpec(shape, lambda i, info: (0, 0))


def attend(nb, info, qn, qr, cosp, sinp, qlim, lat, up, upx):
    rows, keys = qn.shape[0], TRUNK + 2 * nb * SEGLEN
    return pl.pallas_call(
        functools.partial(attend_kernel, nb),
        out_shape=(
            jax.ShapeDtypeStruct((rows, HEADS * VDIM), BF),
            jax.ShapeDtypeStruct((HEADS // 2, 8, rows), F32),
            jax.ShapeDtypeStruct((keys, HEADS * (NOPE + VDIM)), BF),
        ),
        grid_spec=pltpu.PrefetchScalarGridSpec(
            num_scalar_prefetch=1,
            grid=(HEADS // 2,),
            in_specs=[
                pair_spec(rows, 256),
                pair_spec(rows, 128),
                whole_spec((rows, 128)),
                whole_spec((rows, 128)),
                whole_spec((1, rows)),
                whole_spec((TREE, LATW)),
                pair_spec(KVR, 512),
                pair_spec(LATW - KVR, 512),
            ],
            out_specs=(pair_spec(rows, 256), lead_spec(8, rows), pair_spec(keys, 512)),
            scratch_shapes=[
                pltpu.VMEM((keys, LATW), BF),
                pltpu.VMEM((2, keys, 128), BF),
                pltpu.VMEM((TRUNK, rows), F32),
                pltpu.VMEM((nb, 2 * SEGLEN, SEGLEN), F32),
                pltpu.VMEM((2, TRUNK, rows), F32),
                pltpu.VMEM((2, nb, 2 * SEGLEN, SEGLEN), F32),
                pltpu.VMEM((2, TRUNK, rows), BF),
            ],
        ),
        name="attend",
        **costs(30e9, 25e6),
    )(info, qn, qr, cosp, sinp, qlim[None, :], lat, up, upx)


def attend_back(nb, info, qn, qr, cosp, sinp, qlim, lat, kv, up, upx, do, stats):
    rows, keys = qn.shape[0], TRUNK + 2 * nb * SEGLEN
    return pl.pallas_call(
        functools.partial(attend_back_kernel, nb),
        out_shape=(
            jax.ShapeDtypeStruct((rows, HEADS * NOPE), BF),
            jax.ShapeDtypeStruct((rows, HEADS * ROPE), BF),
            jax.ShapeDtypeStruct((128, HEADS * (NOPE + VDIM)), F32),
            jax.ShapeDtypeStruct((TREE, LATW), F32),
        ),
        grid_spec=pltpu.PrefetchScalarGridSpec(
            num_scalar_prefetch=1,
            grid=(HEADS // 2,),
            in_specs=[
                pair_spec(rows, 256),
                pair_spec(rows, 128),
                whole_spec((rows, 128)),
                whole_spec((rows, 128)),
                whole_spec((1, rows)),
                pl.BlockSpec((TREE, 128), lambda i, info: (0, KVR // 128)),
                pair_spec(keys, 512),
                pair_spec(KVR, 512),
                pair_spec(LATW - KVR, 512),
                pair_spec(rows, 256),
                lead_spec(8, rows),
            ],
            out_specs=(
                pair_spec(rows, 256),
                pair_spec(rows, 128),
                pair_spec(128, 512),
                whole_spec((TREE, LATW)),
            ),
            scratch_shapes=[
                pltpu.VMEM((keys, 128), BF),
                pltpu.VMEM((2, keys, 128), BF),
                pltpu.VMEM((TRUNK, rows), F32),
                pltpu.VMEM((nb, 2 * SEGLEN, SEGLEN), F32),
                pltpu.VMEM((TRUNK, rows), BF),
                pltpu.VMEM((keys, 512), BF),
                pltpu.VMEM((keys, LATW), F32),
                pltpu.VMEM((keys, 128), F32),
            ],
        ),
        name="attend_back",
        **costs(54e9, 30e6),
    )(info, qn, qr, cosp, sinp, qlim[None, :], lat, kv, up, upx, do, stats)


def gated_parts(gate, up):
    sig = 1.0 / (1.0 + jnp.exp(-gate))
    swish = gate * sig
    return swish * up, swish, up * (sig * (1.0 + gate * (1.0 - sig)))


def slot_matrix(slots, owned, cap, rows):
    wanted = row_iota((cap, rows)) + 1
    return [slots[e : e + 1, :] == wanted for e in range(owned)]


def spread_grad_kernel(owned, cap, pay, slots, sh_out, perm, gsh):
    rows = pay.shape[0]
    pick = slot_matrix(slots[0].astype(jnp.int32), owned, cap, rows)
    hot = jnp.concatenate([p.astype(F32) for p in pick], 0).astype(BF)
    values = pay[:, :D]
    got = product(hot, values)
    for e in range(owned):
        perm[e, 0] = got[e * cap : (e + 1) * cap].astype(BF)
    gsh[...] = product_t(values, sh_out[...])


def spread_feed_kernel(owned, cap, pay, slots, probs, gsh, sh_in, perm, gates, inner, gact):
    rows = pay.shape[0]
    pick = slot_matrix(slots[0].astype(jnp.int32), owned, cap, rows)
    hot = jnp.concatenate([p.astype(F32) for p in pick], 0).astype(BF)
    values = pay[:, :D]
    got = product(hot, values)
    for e in range(owned):
        perm[e, 0] = got[e * cap : (e + 1) * cap].astype(BF)
        gate = jnp.sum(jnp.where(pick[e], probs[0, e : e + 1, :], 0.0), axis=1, keepdims=True)
        gates[e, 0] = jnp.broadcast_to(gate, (cap, 128))
    width = gsh.shape[1]
    act = product(values, sh_in[...])
    value, by_up, by_gate = gated_parts(act[:, :width], act[:, width:])
    inner[...] = value.astype(BF)
    gact[:, :width] = (gsh[...] * by_gate).astype(BF)
    gact[:, width:] = (gsh[...] * by_up).astype(BF)


def expert_grad_kernel(g, w_out, back):
    hidden = w_out.shape[1]
    for at in range(0, hidden, 256):
        width = min(256, hidden - at)
        back[0, :, at : at + width] = product_t(g[0], w_out[0, at : at + width, :]).astype(BF)


def expert_kernel(experts, first, x, back, gates, w_in, slot_out, inner, ggu):
    hidden = back.shape[2]
    x_here = x[0]
    gate_here = gates[0][:, :1]
    total = jnp.zeros((x_here.shape[0], 1), F32)
    for at in range(0, hidden, 256):
        width = min(256, hidden - at)
        gate = product(x_here, w_in[0, :, at : at + width])
        up = product(x_here, w_in[0, :, hidden + at : hidden + at + width])
        value, by_up, by_gate = gated_parts(gate, up)
        low = value.astype(BF)
        inner[0, :, at : at + width] = low
        here = back[0, :, at : at + width].astype(F32)
        scaled = here * gate_here
        ggu[:, at : at + width] = (scaled * by_gate).astype(BF)
        ggu[:, hidden + at : hidden + at + width] = (scaled * by_up).astype(BF)
        total = total + jnp.sum(low.astype(F32) * here, axis=1, keepdims=True)
    for at in range(0, D, 256):
        slot_out[0, :, at : at + 256] = product_t(ggu[...], w_in[0, at : at + 256, :]).astype(BF)
    high = total.astype(BF).astype(F32)
    mine = first[0] + pl.program_id(0)
    lane = lane_iota((x_here.shape[0], slot_out.shape[2] - D))
    extra = jnp.where(lane == mine, high, jnp.where(lane == experts + mine, total - high, 0.0))
    slot_out[0, :, D:] = extra.astype(BF)


def expert_rows_kernel(inner, gates, w_out, rows_out):
    gate_here = gates[0][:, :1]
    for at in range(0, D, 256):
        rows = product(inner[0], w_out[0, :, at : at + 256]) * gate_here
        rows_out[0, :, at : at + 256] = rows.astype(BF)


def collect_kernel(owned, cap, rows_perm, slots, inner, weight, out, *, transposed):
    rows = out.shape[0]
    spread = (
        lane_iota((128, owned * cap)) // cap == row_iota((128, owned * cap))
    ).astype(F32).astype(BF)
    named = product(slots[...], spread)
    wanted = (lane_iota((rows, owned * cap)) % cap + 1).astype(F32)
    hot = (named == wanted).astype(F32).astype(BF)
    values = jnp.concatenate([rows_perm[e, 0].astype(F32) for e in range(owned)], 0).astype(BF)
    if transposed:
        shared = product_t(inner[...], weight[...])
    else:
        shared = product(inner[...], weight[...])
    out[:, :D] = (product(hot, values[:, :D]) + shared).astype(BF)
    if out.shape[1] > D:
        out[:, D:] = product(hot, values[:, D:]).astype(BF)


def row_block(rows, width):
    return pl.BlockSpec((rows, width), lambda b: (b, 0))


def fixed(shape):
    return pl.BlockSpec(shape, lambda b: (0,) * len(shape))


def token_block(owned, rows):
    return pl.BlockSpec((1, owned, rows), lambda b: (b, 0, 0))


def perm_block(owned, cap, width):
    return pl.BlockSpec((owned, 1, cap, width), lambda b: (0, b, 0, 0))


def costs(flops, moved):
    return dict(
        compiler_params=pltpu.CompilerParams(
            vmem_limit_bytes=VMEM_LIMIT
        ),
        cost_estimate=pl.CostEstimate(
            flops=int(flops), bytes_accessed=int(moved), transcendentals=0
        ),
    )


def spread_grad(payload, slots, sh_out, cap):
    groups, owned, rows = slots.shape
    width = sh_out.shape[0]
    return pl.pallas_call(
        functools.partial(spread_grad_kernel, owned, cap),
        grid=(groups,),
        out_shape=(
            jax.ShapeDtypeStruct((owned, groups, cap, D), BF),
            jax.ShapeDtypeStruct((groups * rows, width), F32),
        ),
        in_specs=[
            row_block(rows, payload.shape[1]),
            token_block(owned, rows),
            fixed(sh_out.shape),
        ],
        out_specs=(perm_block(owned, cap, D), row_block(rows, width)),
        name="spread_grad",
        **costs(12e9, 28e6),
    )(payload, slots, sh_out)


def spread_feed(payload, slots, probs, gsh, sh_in, cap):
    groups, owned, rows = slots.shape
    width = gsh.shape[1]
    return pl.pallas_call(
        functools.partial(spread_feed_kernel, owned, cap),
        grid=(groups,),
        out_shape=(
            jax.ShapeDtypeStruct((owned, groups, cap, D), BF),
            jax.ShapeDtypeStruct((owned, groups, cap, 128), F32),
            jax.ShapeDtypeStruct((groups * rows, width), BF),
            jax.ShapeDtypeStruct((groups * rows, 2 * width), BF),
        ),
        in_specs=[
            row_block(rows, payload.shape[1]),
            token_block(owned, rows),
            token_block(owned, rows),
            row_block(rows, width),
            fixed(sh_in.shape),
        ],
        out_specs=(
            perm_block(owned, cap, D),
            perm_block(owned, cap, 128),
            row_block(rows, width),
            row_block(rows, 2 * width),
        ),
        name="spread_feed",
        **costs(14e9, 28e6),
    )(payload, slots, probs, gsh, sh_in)


def row_chunk(rows):
    count = 1
    while rows // count > 384 or rows % count or rows // count % 8:
        count += 1
    return rows // count


def expert_specs(owned, rows):
    chunk = row_chunk(rows)

    def at(width):
        return pl.BlockSpec((1, chunk, width), lambda e, i, *_: (e, i, 0))

    def weight(shape):
        return pl.BlockSpec((1,) + shape, lambda e, i, *_: (e, 0, 0))

    return (owned, rows // chunk), chunk, at, weight


def expert_grads(g, w_out):
    owned, rows, _ = g.shape
    hidden = w_out.shape[1]
    grid, _, at, weight = expert_specs(owned, rows)
    return pl.pallas_call(
        expert_grad_kernel,
        out_shape=jax.ShapeDtypeStruct((owned, rows, hidden), BF),
        grid=grid,
        in_specs=[at(D), weight((hidden, D))],
        out_specs=at(hidden),
        name="expert_grads",
        **costs(2 * owned * rows * D * hidden, owned * (D * hidden * 2 + rows * D * 4)),
    )(g, w_out)


def run_experts(first, x, back, gates, w_in, experts):
    owned, rows, _ = x.shape
    hidden = back.shape[2]
    grid, chunk, at, weight = expert_specs(owned, rows)
    return pl.pallas_call(
        functools.partial(expert_kernel, experts),
        out_shape=(
            jax.ShapeDtypeStruct((owned, rows, D + 128), BF),
            jax.ShapeDtypeStruct((owned, rows, hidden), BF),
        ),
        grid_spec=pltpu.PrefetchScalarGridSpec(
            num_scalar_prefetch=1,
            grid=grid,
            in_specs=[at(D), at(hidden), at(128), weight((D, 2 * hidden))],
            out_specs=(at(D + 128), at(hidden)),
            scratch_shapes=[pltpu.VMEM((chunk, 2 * hidden), BF)],
        ),
        name="experts",
        **costs(8 * owned * rows * D * hidden, owned * D * hidden * 4),
    )(first, x, back, gates, w_in)


def expert_rows(inner, gates, w_out):
    owned, rows, hidden = inner.shape
    grid, _, at, weight = expert_specs(owned, rows)
    return pl.pallas_call(
        expert_rows_kernel,
        out_shape=jax.ShapeDtypeStruct((owned, rows, D), BF),
        grid=grid,
        in_specs=[at(hidden), at(128), weight((hidden, D))],
        out_specs=at(D),
        name="expert_rows",
        **costs(2 * owned * rows * D * hidden, owned * (D * hidden * 2 + rows * D * 4)),
    )(inner, gates, w_out)


def collect(rows_perm, slots, inner, weight, transposed):
    owned, groups, cap, width = rows_perm.shape
    rows = slots.shape[0] // groups
    return pl.pallas_call(
        functools.partial(collect_kernel, owned, cap, transposed=transposed),
        grid=(groups,),
        out_shape=jax.ShapeDtypeStruct((groups * rows, width), BF),
        in_specs=[
            perm_block(owned, cap, width),
            row_block(rows, 128),
            row_block(rows, inner.shape[1]),
            fixed(weight.shape),
        ],
        out_specs=row_block(rows, width),
        name="collect_grad" if transposed else "collect_rows",
        **costs(14e9, 28e6),
    )(rows_perm, slots, inner, weight)


MESH = pl.DeviceIdType.MESH
PLANE = 8


def neighbours():
    e = lax.axis_index("expert")
    core, x, y = e % 2, (e // 2) % 2, e // 4
    return e, 1 - 2 * core, 2 - 4 * x, 4 - 8 * y


def remote(src, dst, send_sem, recv_sem, **where):
    return pltpu.make_async_remote_copy(
        src_ref=src,
        dst_ref=dst,
        send_sem=send_sem,
        recv_sem=recv_sem,
        device_id=where,
        device_id_type=MESH,
    )


def greet(plane, levels):
    barrier = pltpu.get_barrier_semaphore()
    for who in plane:
        pl.semaphore_signal(barrier, inc=1, device_id={"expert": who}, device_id_type=MESH)
    for level in levels:
        pl.semaphore_signal(barrier, inc=1, device_id={"dp": level}, device_id_type=MESH)
    pl.semaphore_wait(barrier, len(plane) + len(levels))


class Mail:
    def __init__(self):
        self.sent = []

    def start(self, src, dst, pair, index, **where):
        copy = remote(src, dst, pair[0].at[index], pair[1].at[index], **where)
        copy.start()
        self.sent.append((None, copy))

    def arrived(self, dst, pair, index):
        here = neighbours()[0]
        remote(dst, dst, pair[0].at[index], pair[1].at[index], expert=here).wait_recv()

    def along(self, level, planes, src, dst, pair, index):
        z = lax.axis_index("dp")
        for way, fits, ahead in (
            (0, (level <= z) & (z < planes - 1), z + 1),
            (1, (level >= z) & (z > 0), z - 1),
        ):
            copy = remote(src, dst, pair[0].at[(way, *index)], pair[1].at[index], dp=ahead)
            pl.when(fits)(copy.start)
            self.sent.append((fits, copy))

    def line_arrived(self, dst, pair, index):
        here = neighbours()[0]
        remote(dst, dst, pair[0].at[(0, *index)], pair[1].at[index], expert=here).wait_recv()

    def drain(self):
        for fits, copy in self.sent:
            if fits is None:
                copy.wait_send()
            else:
                pl.when(fits)(copy.wait_send)


def nearest_levels(planes):
    if planes == 1:
        return [0]
    z = lax.axis_index("dp")
    power = 1 + 3 * z + 9 * (z * (z - 1) // 2) + 27 * (z * (z - 1) * (z - 2) // 6)
    order = ((1, 2, 3), (0, 2, 3), (1, 3, 0), (2, 1, 0))
    packed = [sum(order[at][m] * 4**at for at in range(4)) for m in range(3)]
    return [z] + [(code // power) % 4 for code in packed]


def spread_pieces(planes, count, source, place, mail, sems, meanwhile=None):
    line, by_x, by_y, by_far, by_core = [sems[2 * n : 2 * n + 2] for n in range(5)]
    e, to_core, to_x, to_y = neighbours()
    levels = nearest_levels(planes)
    partner, xn, yn, dg = e + to_core, e + to_x, e + to_y, e + to_x + to_y

    def at(k, who, i):
        return place(levels[k], who, i)

    def stage_a(k):
        for i in range(count):
            here = at(k, e, i)
            src = source(i) if k == 0 else here
            if k:
                mail.line_arrived(here, line, (levels[k], i))
            if planes > 1:
                mail.along(levels[k], planes, src, here, line, (levels[k], i))
            if i % 2 == 0:
                mail.start(src, here, by_x, (k, i), expert=xn)
                mail.start(src, here, by_y, (k, i), expert=yn)
            else:
                mail.start(src, here, by_y, (k, i), expert=yn)
                mail.start(src, here, by_x, (k, i), expert=xn)
            mail.start(src, here, by_core, (0, k, i), expert=partner)

    def stage_b(k):
        for i in range(count):
            left, up = at(k, xn, i), at(k, yn, i)
            mail.arrived(left, by_x, (k, i))
            if i % 2 == 0:
                mail.start(left, left, by_far, (k, i), expert=yn)
            mail.start(left, left, by_core, (1, k, i), expert=partner)
            mail.arrived(up, by_y, (k, i))
            if i % 2:
                mail.start(up, up, by_far, (k, i), expert=xn)
            mail.start(up, up, by_core, (2, k, i), expert=partner)

    def stage_c(k):
        for i in range(count):
            here = at(k, dg, i)
            mail.arrived(here, by_far, (k, i))
            mail.start(here, here, by_core, (3, k, i), expert=partner)

    for s in range(planes + 2):
        if s < planes:
            stage_a(s)
        if meanwhile is not None:
            meanwhile(s)
        if 0 <= s - 1 < planes:
            stage_b(s - 1)
        if 0 <= s - 2:
            stage_c(s - 2)
    for k in range(planes):
        for n, who in enumerate((e, xn, yn, dg)):
            for i in range(count):
                mail.arrived(at(k, who + to_core, i), by_core, (n, k, i))


def spread_sems(planes, count):
    dma = pltpu.SemaphoreType.DMA
    each, core = dma((planes, count)), dma((4, planes, count))
    return [dma((2, planes, count)), *([each] * 7), core, core]


def plane_peers(swaps):
    e, to_core, to_x, to_y = neighbours()
    if swaps:
        return [(e + j) % PLANE for j in range(1, PLANE)]
    return [e + to_core, e + to_x, e + to_y]


def other_levels(planes):
    if planes == 1:
        return []
    z = lax.axis_index("dp")
    return [(z + k) % planes for k in range(1, planes)]


def swap_out(mail, src, landing, pair, n):
    e = neighbours()[0]
    for j in range(1, PLANE):
        who = (e + j) % PLANE
        mail.start(src(who), landing(e), pair, (n, j - 1), expert=who)


def swap_in(mail, landing, pair, n):
    e = neighbours()[0]
    for j in range(1, PLANE):
        mail.arrived(landing((e + PLANE - j) % PLANE), pair, (n, j - 1))


def gather_kernel(planes, pieces, count, swaps, lines, *refs):
    total = count + swaps + lines
    shards, outs = refs[:total], refs[total : 2 * total]
    sems = refs[2 * total :]
    own_sem, swap, line = sems[10], sems[11:13], sems[13:15]
    e = neighbours()[0]
    levels = nearest_levels(planes)
    z = levels[0]
    mail = Mail()
    greet(plane_peers(swaps), other_levels(planes))

    def place(level, who, i):
        array, first, rows = pieces[i]
        return outs[array].at[level, who, pl.ds(first, rows)]

    def source(i):
        array, first, rows = pieces[i]
        return shards[array].at[pl.ds(first, rows)]

    mine = [pltpu.make_async_copy(shards[a], outs[a].at[z, e], own_sem.at[a]) for a in range(count)]
    for a in range(count, count + swaps):
        mine.append(pltpu.make_async_copy(shards[a].at[e], outs[a].at[z, e], own_sem.at[a]))
    for a in range(count + swaps, total):
        mine.append(pltpu.make_async_copy(shards[a], outs[a].at[z], own_sem.at[a]))
    for copy in mine:
        copy.start()
    for n in range(swaps):
        a = count + n
        swap_out(
            mail, lambda who: shards[a].at[who], lambda who: outs[a].at[z, who], swap, n
        )
    cuts = []
    for a in range(count, total):
        size = outs[a].shape[1]
        half = size // 2
        cuts += [(a, pl.ds(0, half)), (a, pl.ds(half, size - half))]

    def line_step(k):
        for i, (a, rows) in enumerate(cuts):
            here = outs[a].at[levels[k], rows]
            src = here if k or a < count + swaps else shards[a].at[rows]
            if k:
                mail.line_arrived(here, line, (levels[k], i))
            mail.along(levels[k], planes, src, here, line, (levels[k], i))

    def meanwhile(s):
        if s == planes - 1:
            for n in range(swaps):
                a = count + n
                swap_in(mail, lambda who: outs[a].at[z, who], swap, n)
                mine[a].wait()
            line_step(0)
        if s >= planes:
            line_step(s - planes + 1)

    spread_pieces(
        planes, len(pieces), source, place, mail, sems, meanwhile if cuts else None
    )
    if cuts:
        for k in range(3, planes):
            line_step(k)
    for n, copy in enumerate(mine):
        if not count <= n < count + swaps:
            copy.wait()
    mail.drain()


def gather_blocks(shards, planes, cuts, ident, swaps=(), lines=()):
    dma = pltpu.SemaphoreType.DMA
    pieces = []
    for array, (shard, cut) in enumerate(zip(shards, cuts)):
        rows = shard.shape[0] // cut
        pieces += [(array, at * rows, rows) for at in range(cut)]
    count, total = len(shards), len(shards) + len(swaps) + len(lines)
    shapes = [jax.ShapeDtypeStruct((planes, PLANE) + s.shape, s.dtype) for s in shards]
    shapes += [jax.ShapeDtypeStruct((planes,) + s.shape, s.dtype) for s in [*swaps, *lines]]
    return pl.pallas_call(
        functools.partial(gather_kernel, planes, pieces, count, len(swaps), len(lines)),
        out_shape=shapes,
        in_specs=[pl.BlockSpec(memory_space=pl.ANY)] * total,
        out_specs=[pl.BlockSpec(memory_space=pl.ANY)] * total,
        scratch_shapes=[
            *spread_sems(planes, len(pieces)),
            dma((total,)),
            dma((max(1, len(swaps)), PLANE - 1)),
            dma((max(1, len(swaps)), PLANE - 1)),
            dma((2, planes, max(1, 2 * (total - count)))),
            dma((planes, max(1, 2 * (total - count)))),
        ],
        compiler_params=pltpu.CompilerParams(collective_id=ident, has_side_effects=True),
        name=f"gather{ident}",
    )(*shards, *swaps, *lines)


def bank_kernel(planes, wide, parts, out, landing, part, *sems):
    e = neighbours()[0]
    z = lax.axis_index("dp")
    mail = Mail()
    swap = sems[10:12]
    greet(plane_peers(1), other_levels(planes))

    def chunk(who):
        return pl.ds(pl.multiple_of(who * wide, 128), wide)

    swap_out(mail, lambda who: parts.at[:, chunk(who)], lambda who: landing.at[who], swap, 0)
    total = parts[:, chunk(e)].astype(F32)
    for j in range(1, PLANE):
        who = (e + PLANE - j) % PLANE
        mail.arrived(landing.at[who], swap, (0, j - 1))
        total = total + landing[who].astype(F32)
    low = total.astype(BF)
    part[...] = low
    out[z, e] = low
    spread_pieces(
        planes, 1, lambda i: part, lambda level, who, i: out.at[level, who], mail, sems
    )
    mail.drain()


def exchange_banks(joined, planes, ident):
    rank, width = joined.shape
    wide = width // PLANE
    dma = pltpu.SemaphoreType.DMA
    vmem = pl.BlockSpec(memory_space=pltpu.VMEM)
    return pl.pallas_call(
        functools.partial(bank_kernel, planes, wide),
        out_shape=jax.ShapeDtypeStruct((planes, PLANE, rank, wide), BF),
        in_specs=[vmem],
        out_specs=vmem,
        scratch_shapes=[
            pltpu.VMEM((PLANE, rank, wide), BF),
            pltpu.VMEM((rank, wide), BF),
            *spread_sems(planes, 1),
            dma((1, PLANE - 1)),
            dma((1, PLANE - 1)),
        ],
        compiler_params=pltpu.CompilerParams(
            collective_id=ident, has_side_effects=True, vmem_limit_bytes=VMEM_LIMIT
        ),
        name=f"banks{ident}",
    )(joined)


def place_kernel(trees, offsets, chosen, full, *outs):
    slot = pl.program_id(0)
    wide = full.shape[3]
    for n, (at, width) in enumerate(offsets):
        total = jnp.zeros(outs[n].shape[1:], F32)
        for t in range(trees):
            pick = (chosen[t] == slot).astype(F32)
            columns = []
            while sum(c.shape[1] for c in columns) < width:
                here = at + sum(c.shape[1] for c in columns)
                first = here % wide
                upto = min(wide, first + at + width - here)
                columns.append(full[t, here // wide, :, first:upto].astype(F32))
            total = total + pick * jnp.concatenate(columns, 1)
        outs[n][0] = total


def place_banks(full, adapter_index, offsets, adapters):
    trees, _, rank, _ = full.shape
    return pl.pallas_call(
        functools.partial(place_kernel, trees, offsets),
        out_shape=[jax.ShapeDtypeStruct((adapters, rank, w), F32) for _, w in offsets],
        grid_spec=pltpu.PrefetchScalarGridSpec(
            num_scalar_prefetch=1,
            grid=(adapters,),
            in_specs=[pl.BlockSpec(full.shape, lambda a, chosen: (0, 0, 0, 0))],
            out_specs=[pl.BlockSpec((1, rank, w), lambda a, chosen: (a, 0, 0)) for _, w in offsets],
        ),
        name="place_banks",
        **costs(1e6, 11e6),
    )(adapter_index, full)


def scatter_kernel(parts, blocks, out, core_in, x_in, y_in, chip, total, sends, sems):
    e, to_core, to_x, to_y = neighbours()
    partner, xn, yn, dg = e + to_core, e + to_x, e + to_y, e + to_x + to_y
    rows = out.shape[0] // parts
    half = parts // 2
    greet((partner, xn, yn), [])
    mail, pair = Mail(), (sends, sems)

    def start(src, dst, index, **where):
        mail.start(src, dst, pair, index, **where)

    def arrived(dst, index):
        mail.arrived(dst, pair, index)

    def cut(p):
        return pl.ds(p * rows, rows)

    order = [p // 2 + (p % 2) * half for p in range(parts)]
    whose = (0, to_x, to_y, to_x + to_y)
    for p in order:
        for b in (3, 1, 2, 0):
            start(
                blocks.at[partner + whose[b], cut(p)],
                core_in.at[b, cut(p)],
                (b, p),
                expert=partner,
            )

    def add_chip(p):
        for b in (3, 1, 2, 0):
            arrived(core_in.at[b, cut(p)], (b, p))
            chip[b, cut(p), :] = (
                blocks[e + whose[b], cut(p), :].astype(F32) + core_in[b, cut(p), :].astype(F32)
            ).astype(BF)

    def first_hop(p):
        if p < half:
            start(chip.at[3, cut(p)], x_in.at[1, cut(p)], (5, p), expert=xn)
            start(chip.at[1, cut(p)], x_in.at[0, cut(p)], (4, p), expert=xn)
        else:
            start(chip.at[3, cut(p)], x_in.at[1, cut(p)], (5, p), expert=yn)
            start(chip.at[2, cut(p)], x_in.at[0, cut(p)], (4, p), expert=yn)

    def add_first(p):
        passed = 2 if p < half else 1
        arrived(x_in.at[1, cut(p)], (5, p))
        chip[passed, cut(p), :] = (
            chip[passed, cut(p), :].astype(F32) + x_in[1, cut(p), :].astype(F32)
        ).astype(BF)
        arrived(x_in.at[0, cut(p)], (4, p))
        total[cut(p), :] = chip[0, cut(p), :].astype(F32) + x_in[0, cut(p), :].astype(F32)

    def second_hop(p):
        if p < half:
            start(chip.at[2, cut(p)], y_in.at[cut(p)], (6, p), expert=yn)
        else:
            start(chip.at[1, cut(p)], y_in.at[cut(p)], (6, p), expert=xn)

    def finish(p):
        arrived(y_in.at[cut(p)], (6, p))
        out[cut(p), :] = (total[cut(p), :] + y_in[cut(p), :].astype(F32)).astype(out.dtype)

    for n, p in enumerate(order):
        add_chip(p)
        if n:
            first_hop(order[n - 1])
    first_hop(order[-1])
    for n, p in enumerate(order):
        add_first(p)
        if n:
            second_hop(order[n - 1])
    second_hop(order[-1])
    for p in order:
        finish(p)
    mail.drain()


def scatter_blocks(blocks, parts, ident, dtype):
    _, rows, width = blocks.shape
    dma = pltpu.SemaphoreType.DMA
    vmem = pl.BlockSpec(memory_space=pltpu.VMEM)
    return pl.pallas_call(
        functools.partial(scatter_kernel, parts),
        out_shape=jax.ShapeDtypeStruct((rows, width), dtype),
        in_specs=[vmem],
        out_specs=vmem,
        scratch_shapes=[
            pltpu.VMEM((4, rows, width), BF),
            pltpu.VMEM((2, rows, width), BF),
            pltpu.VMEM((rows, width), BF),
            pltpu.VMEM((4, rows, width), BF),
            pltpu.VMEM((rows, width), F32),
            dma((7, parts)),
            dma((7, parts)),
        ],
        compiler_params=pltpu.CompilerParams(
            collective_id=ident, has_side_effects=True, vmem_limit_bytes=VMEM_LIMIT
        ),
        name=f"scatter{ident}",
    )(blocks)


def gather_dp(shard):
    size = lax.axis_size("dp")
    me = lax.axis_index("dp")
    pieces = [shard]
    for k in range(1, size):
        pieces.append(lax.ppermute(shard, "dp", [(i, (i + k) % size) for i in range(size)]))
    stacked = jnp.stack(pieces)
    return jnp.concatenate(
        [lax.dynamic_index_in_dim(stacked, (me - s) % size, 0, keepdims=True) for s in range(size)], 0
    )


def gather_plane(value):
    groups = lax.axis_size("expert")
    spread = jnp.broadcast_to(value[None], (groups,) + value.shape)
    return lax.all_to_all(spread, "expert", split_axis=0, concat_axis=0, tiled=True)


def reduce_banks(gradients, local_tree, trees_here, adapter_index, adapters):
    groups = lax.axis_size("expert")
    rank = gradients[0].shape[0]
    widths = [g.shape[1] for g in gradients]
    joined = jnp.concatenate(gradients, 1).astype(BF)
    if trees_here > 1:
        joined = jnp.where(
            (jnp.arange(trees_here) == local_tree)[:, None, None], joined[None], 0.0
        ).astype(BF)
    joined = joined.reshape(groups, -1)
    parts = lax.all_to_all(joined, "expert", split_axis=0, concat_axis=0, tiled=True)
    part = jnp.sum(parts.astype(F32), axis=0).astype(BF)
    lanes = gather_dp(part)
    full = gather_plane(lanes)
    trees = lax.axis_size("dp") * trees_here
    full = full.transpose(1, 0, 2).reshape(trees, rank, sum(widths))
    outs, at = [], 0
    for width in widths:
        piece = full[:, :, at : at + width].astype(F32)
        at += width
        outs.append(
            sum(
                jnp.where(
                    (jnp.arange(adapters) == adapter_index[t])[:, None, None], piece[t][None], 0.0
                )
                for t in range(trees)
            )
        )
    return outs


def body(
    tokens_in,
    cotangent,
    segment_id,
    parent_id,
    adapter_index,
    routes,
    mixer_gain,
    latent_gain,
    feed_gain,
    query_matrix,
    latent_down,
    latent_up,
    output_matrix,
    router_matrix,
    shared_in,
    shared_out,
    expert_in,
    expert_out,
    query_entry,
    query_exit,
    lower_entry,
    lower_exit,
    upper_entry,
    upper_exit,
    output_entry,
    output_exit,
):
    rows_here = tokens_in.shape[0]
    groups = lax.axis_size("expert")
    planes = lax.axis_size("dp")
    group_pos = lax.axis_index("expert")
    trees_here = segment_id.shape[0] // TREE
    local_tree = group_pos * rows_here // TREE
    tree_offset = group_pos * rows_here - local_tree * TREE
    chosen = adapter_index[lax.axis_index("dp") * trees_here + local_tree]
    query_in = select_slot(query_entry, chosen)
    qn_out, qr_out = split_heads(select_slot(query_exit, chosen))
    lower_in = select_slot(lower_entry, chosen)
    lower_out = select_slot(lower_exit, chosen)
    upper_in = select_slot(upper_entry, chosen)
    upper_out = select_slot(upper_exit, chosen)
    output_in = select_slot(output_entry, chosen)
    output_out = select_slot(output_exit, chosen)
    experts_all = router_matrix.shape[1]
    owned = expert_in.shape[0]
    capacity = max(2, 4 * rows_here * TOPK // (3 * experts_all))
    cap = -(-capacity // 8) * 8
    hidden_shared = shared_out.shape[0]
    both = ("dp", "expert")
    fast = groups == PLANE and planes == 4 and groups * rows_here == TREE and hidden_shared % 8 == 0

    weight_rows = query_matrix.shape[0]
    qn_here, qr_here = split_heads(query_matrix)
    front = jnp.concatenate([qn_here, qr_here, latent_down, router_matrix], 1)
    padded_shared = -(-planes * hidden_shared // 128) * 128
    fill = padded_shared - planes * hidden_shared
    cut = shared_in.reshape(weight_rows, 2, planes, groups, hidden_shared)
    cut = cut.transpose(3, 0, 1, 2, 4).reshape(groups, weight_rows, 2, planes * hidden_shared)
    cut = jnp.pad(cut, ((0, 0), (0, 0), (0, 0), (0, fill)))
    cut = cut.reshape(groups, weight_rows, 2 * padded_shared)
    if fast:
        lines = shared_out.reshape(hidden_shared // 8, 8, D)
        front, mix_up, mix_out, sh_in, sh_out = gather_blocks(
            [front, latent_up, output_matrix], planes, (4, 2, 2), 1, [cut], [lines]
        )
        front = front.reshape(D, -1)
        mix_up = mix_up.reshape(KVR, -1)
        mix_out = mix_out.reshape(-1, D)
    else:
        front = lax.all_gather(front, both, axis=0, tiled=True)
        mix_up = lax.all_gather(latent_up, both, axis=0, tiled=True)
        mix_out = lax.all_gather(output_matrix, both, axis=0, tiled=True)
        cut = lax.all_to_all(cut, "expert", split_axis=0, concat_axis=0, tiled=True)
        sh_in = gather_dp(cut.reshape(groups * weight_rows, -1))
        sh_out = gather_dp(shared_out)
    wide = HEADS * (NOPE + ROPE)
    feed_router = front[:, wide + KVR + ROPE :]

    sh_in = sh_in.reshape(D, 2 * padded_shared)
    sh_out = sh_out.reshape(planes * hidden_shared, D)
    sh_out = jnp.pad(sh_out, ((0, fill), (0, 0)))

    seg_tree = lax.dynamic_slice_in_dim(segment_id, local_tree * TREE, TREE)
    par_tree = lax.dynamic_slice_in_dim(parent_id, local_tree * TREE, TREE)
    key_index = jnp.arange(TREE, dtype=jnp.int32)
    start_pos = jnp.where(par_tree == 0, TRUNK, TRUNK + SEGLEN)
    key_pos = jnp.where(seg_tree == 0, key_index, start_pos + key_index % SEGLEN)
    row_pos = lax.dynamic_slice_in_dim(key_pos, tree_offset, rows_here)
    row_seg = lax.dynamic_slice_in_dim(seg_tree, tree_offset, rows_here)
    step = 128
    while rows_here % step:
        step //= 2
    nb = -(-(rows_here - step) // SEGLEN) + 1
    first_block = tree_offset // SEGLEN
    shift = tree_offset - first_block * SEGLEN
    seg_blocks = seg_tree.reshape(TREE // SEGLEN, SEGLEN)[:, 0]
    par_blocks = par_tree.reshape(TREE // SEGLEN, SEGLEN)[:, 0]
    own = jnp.minimum(first_block + jnp.arange(nb, dtype=jnp.int32), TREE // SEGLEN - 1)
    own_seg = seg_blocks[own]
    own_par = par_blocks[own]
    is_leaf = ((own_seg != 0) & (own_par != 0)).astype(jnp.int32)
    match = (seg_blocks[None, :] == own_par[:, None]) & (is_leaf[:, None] > 0)
    par_block = jnp.sum(
        jnp.where(match, jnp.arange(TREE // SEGLEN, dtype=jnp.int32)[None, :], 0), axis=1
    )
    info = jnp.concatenate([own, par_block, (own_seg != 0).astype(jnp.int32), is_leaf])
    query_limit = jnp.where(
        row_seg == 0, tree_offset + jnp.arange(rows_here, dtype=jnp.int32), TRUNK - 1
    )

    def pad_rows(value):
        empty = jnp.zeros((nb * SEGLEN,) + value.shape[1:], value.dtype)
        return lax.dynamic_update_slice_in_dim(empty, value, shift, 0)

    def cut_rows(value):
        return lax.dynamic_slice_in_dim(value, shift, rows_here, 0)

    inverse = 10000.0 ** (-(jnp.arange(HALF, dtype=F32) * 2.0 / ROPE))
    angles = row_pos.astype(F32)[:, None] * inverse[None, :]
    cos_half, sin_half = jnp.cos(angles), jnp.sin(angles)
    cosine = jnp.concatenate([cos_half, cos_half], -1)
    sine = jnp.concatenate([sin_half, sin_half], -1)
    cos_pair = pad_rows(jnp.concatenate([cos_half] * 4, -1))
    sin_pair = pad_rows(jnp.concatenate([-sin_half, -sin_half, sin_half, sin_half], -1))
    limit_rows = pad_rows(query_limit)

    mask = jnp.sum(
        (routes[:, :, None] == jnp.arange(experts_all, dtype=jnp.int32)).astype(F32), axis=1
    )
    lower = (
        jnp.arange(rows_here)[:, None] >= jnp.arange(rows_here)[None, :]
    ).astype(BF)
    slots_here = product(lower, mask.astype(BF)) * mask

    inputs = tokens_in.astype(F32)
    hidden = normed(inputs, mixer_gain).astype(BF)
    query_mid = product_t(hidden, query_in).astype(BF)
    lower_mid = product_t(hidden, lower_in).astype(BF)
    front_lin = product(hidden, front)
    latent_full = front_lin[:, wide : wide + KVR + ROPE] + product(lower_mid, lower_out)
    latent_raw = latent_full[:, :KVR]
    rope_raw = latent_full[:, KVR:]
    latent_norm = normed(latent_raw, latent_gain).astype(BF)
    key_rope = rotate(rope_raw, cosine, sine).astype(BF)
    upper_mid = product_t(latent_norm, upper_in).astype(BF)
    rank = upper_mid.shape[1]
    latent_ext = jnp.concatenate(
        [
            latent_norm,
            key_rope[:, :HALF],
            upper_mid,
            jnp.zeros((rows_here, HALF - rank), BF),
            key_rope[:, HALF:],
            jnp.zeros((rows_here, HALF), BF),
        ],
        1,
    )
    if fast:
        all_latent = gather_blocks([latent_ext], 1, (2,), 2)[0].reshape(TREE, LATW)
    else:
        all_latent = lax.all_gather(latent_ext, "expert", axis=0, tiled=True)
    tree_latent = lax.dynamic_slice_in_dim(all_latent, local_tree * TREE, TREE, 0)
    up_extra = jnp.concatenate(
        [
            jnp.zeros((HALF, mix_up.shape[1]), BF),
            upper_out,
            jnp.zeros((LATW - KVR - HALF - rank, mix_up.shape[1]), BF),
        ],
        0,
    )
    q_nope = pad_rows(
        (front_lin[:, : HEADS * NOPE] + product(query_mid, qn_out)).astype(BF)
    )
    q_rope = pad_rows(front_lin[:, HEADS * NOPE : wide] + product(query_mid, qr_out))
    grad_payload = jnp.concatenate(
        [cotangent, slots_here.astype(BF), jnp.zeros((rows_here, 128 - experts_all), BF)], 1
    )
    grad_payload, tree_latent = lax.optimization_barrier((grad_payload, tree_latent))
    all_grad = lax.all_gather(grad_payload, "expert", axis=0, tiled=True)

    attended, level, keys_values = attend(
        nb, info, q_nope, q_rope, cos_pair, sin_pair, limit_rows, tree_latent, mix_up, up_extra
    )
    attended = cut_rows(attended)
    output_mid = product_t(attended, output_in).astype(BF)
    mixed_state = inputs + product(attended, mix_out) + product(output_mid, output_out)
    feed_hidden = normed(mixed_state, feed_gain).astype(BF)
    logits = product(feed_hidden, feed_router)
    logit_peak = jnp.max(logits, axis=1, keepdims=True)
    logit_exp = jnp.exp(logits - logit_peak)
    router_probs = logit_exp / jnp.sum(logit_exp, axis=1, keepdims=True)

    my_slots = lax.dynamic_slice(all_grad, (0, D + group_pos * owned), (groups * rows_here, owned))
    slot_rows = jnp.pad(my_slots, ((0, 0), (0, 128 - owned)))
    slot_cols = my_slots.reshape(groups, rows_here, owned).transpose(0, 2, 1).astype(F32)
    grad_perm, grad_shared = spread_grad(all_grad, slot_cols, sh_out, cap)
    flat = (owned, groups * cap)
    grad_inner = expert_grads(grad_perm.reshape(*flat, D), expert_out)

    high = lax.reduce_precision(router_probs, 8, 7)
    feed_payload = jnp.concatenate(
        [feed_hidden, high.astype(BF), (router_probs - high).astype(BF)], 1
    )
    all_feed = lax.all_gather(feed_payload, "expert", axis=0, tiled=True)

    all_feed, grad_inner = lax.optimization_barrier((all_feed, grad_inner))

    def my_columns(start):
        return lax.dynamic_slice(
            all_feed, (0, start + group_pos * owned), (groups * rows_here, owned)
        ).astype(F32)

    my_probs = my_columns(D) + my_columns(D + experts_all)
    prob_cols = my_probs.reshape(groups, rows_here, owned).transpose(0, 2, 1)
    feed_perm, gates, inner_shared, gact_shared = spread_feed(
        all_feed, slot_cols, prob_cols, grad_shared, sh_in, cap
    )
    gates = gates.reshape(*flat, 128)
    slot_perm, inner = run_experts(
        (group_pos * owned).astype(jnp.int32).reshape(1),
        feed_perm.reshape(*flat, D),
        grad_inner,
        gates,
        expert_in,
        experts_all,
    )
    grad_part = collect(
        slot_perm.reshape(owned, groups, cap, D + 128), slot_rows, gact_shared, sh_in, True
    )
    grad_sum = lax.psum_scatter(grad_part, "expert", scatter_dimension=0, tiled=True)
    inner, grad_part = lax.optimization_barrier((inner, grad_part))
    rows_perm = expert_rows(inner, gates, expert_out)
    row_part = collect(
        rows_perm.reshape(owned, groups, cap, D), slot_rows, inner_shared, sh_out, False
    )
    row_sum = lax.psum_scatter(row_part, "expert", scatter_dimension=0, tiled=True)

    grad_output = cotangent.astype(F32)
    grad_sum = grad_sum.astype(F32)
    grad_probs = grad_sum[:, D : D + experts_all] + grad_sum[:, D + experts_all :]
    grad_logits = router_probs * (
        grad_probs - jnp.sum(router_probs * grad_probs, axis=1, keepdims=True)
    )
    grad_feed = grad_sum[:, :D] + product_t(grad_logits.astype(BF), feed_router)
    _, norm_two_back = jax.vjp(lambda operand: normed(operand, feed_gain), mixed_state)
    grad_mixed = grad_output + norm_two_back(grad_feed)[0]
    grad_attn = grad_mixed.astype(BF)
    grad_output_mid = product_t(grad_attn, output_out).astype(BF)
    grad_output_exit = product_left(output_mid, grad_attn)
    grad_output_entry = product_left(grad_output_mid, attended)
    grad_attended = (product_t(grad_attn, mix_out) + product(grad_output_mid, output_in)).astype(BF)

    delta = jnp.sum(
        (grad_attended.astype(F32) * attended.astype(F32)).reshape(rows_here, HEADS, VDIM), axis=2
    )
    padded = nb * SEGLEN
    stats = jnp.concatenate(
        [
            level[:, :2],
            pad_rows(delta).T.reshape(HEADS // 2, 2, padded),
            jnp.zeros((HEADS // 2, 4, padded), F32),
        ],
        1,
    )
    dq_nope, dq_rope, grad_up, grad_lat = attend_back(
        nb,
        info,
        q_nope,
        q_rope,
        cos_pair,
        sin_pair,
        limit_rows,
        tree_latent,
        keys_values,
        mix_up,
        up_extra,
        pad_rows(grad_attended),
        stats,
    )
    row_sum, dq_nope = lax.optimization_barrier((row_sum, dq_nope))
    block_output = (mixed_state + row_sum.astype(F32)).astype(BF)
    dq_nope, dq_rope = cut_rows(dq_nope), cut_rows(dq_rope)
    grad_upper_exit = grad_up[HALF : HALF + rank]
    grad_upper_mid = grad_lat[:, KVR + HALF : KVR + HALF + rank].astype(BF)
    grad_upper_entry = product_left(grad_upper_mid, tree_latent[:, :KVR])
    grad_tree = grad_lat[:, :KVR] + product(grad_upper_mid, upper_in)
    grad_tree = jnp.concatenate(
        [
            grad_tree,
            grad_lat[:, KVR : KVR + HALF],
            grad_lat[:, KVR + ROPE : KVR + ROPE + HALF],
            jnp.zeros((TREE, ROPE), F32),
        ],
        1,
    ).astype(BF)
    if trees_here > 1:
        grad_tree = lax.dynamic_update_slice_in_dim(
            jnp.zeros((groups * rows_here, grad_tree.shape[1]), BF), grad_tree, local_tree * TREE, 0
        )
    if fast:
        grad_latent = scatter_blocks(grad_tree.reshape(groups, rows_here, -1), 4, 5, F32)
    else:
        grad_latent = lax.psum_scatter(
            grad_tree, "expert", scatter_dimension=0, tiled=True
        ).astype(F32)
    _, latent_back = jax.vjp(lambda operand: normed(operand, latent_gain), latent_raw)
    _, key_back = jax.vjp(lambda operand: rotate(operand, cosine, sine), rope_raw)
    grad_latent_full = jnp.concatenate(
        [latent_back(grad_latent[:, :KVR])[0], key_back(grad_latent[:, KVR : KVR + ROPE])[0]], -1
    ).astype(BF)
    grad_lower_mid = product_t(grad_latent_full, lower_out).astype(BF)
    grad_lower_exit = product_left(lower_mid, grad_latent_full)
    grad_lower_entry = product_left(grad_lower_mid, hidden)
    dq_all = jnp.concatenate([dq_nope, dq_rope], 1)
    q_out = jnp.concatenate([qn_out, qr_out], 1)
    grad_query_mid = product_t(dq_all, q_out).astype(BF)
    grad_query_exit = product_left(query_mid, dq_all)
    grad_query_exit = join_heads(
        grad_query_exit[:, : HEADS * NOPE], grad_query_exit[:, HEADS * NOPE :]
    )
    grad_query_entry = product_left(grad_query_mid, hidden)
    grad_front = jnp.concatenate(
        [dq_all, grad_latent_full, jnp.zeros((rows_here, experts_all), BF)], 1
    )
    grad_hidden = (
        product_t(grad_front, front)
        + product(grad_query_mid, query_in)
        + product(grad_lower_mid, lower_in)
    )
    _, norm_one_back = jax.vjp(lambda operand: normed(operand, mixer_gain), inputs)
    grad_input = (grad_mixed + norm_one_back(grad_hidden)[0]).astype(BF)

    adapters = query_entry.shape[0]
    gradients = [
        grad_query_entry,
        grad_query_exit,
        grad_lower_entry,
        grad_lower_exit,
        grad_upper_entry,
        grad_upper_exit,
        grad_output_entry,
        grad_output_exit,
    ]
    if fast:
        offsets, pieces, at = [], [], 0
        for gradient in gradients:
            width = gradient.shape[1]
            offsets.append((at, width))
            pieces.append(jnp.pad(gradient, ((0, 0), (0, -width % 128))))
            at += width + -width % 128
        pieces.append(jnp.zeros((rank, -at % (128 * PLANE)), F32))
        joined = jnp.concatenate(pieces, 1).astype(BF)
        full = exchange_banks(joined, planes, 6)
        banks = place_banks(full, adapter_index, tuple(offsets), adapters)
    else:
        banks = reduce_banks(gradients, local_tree, trees_here, adapter_index, adapters)
    return (block_output, grad_input, *banks)


def solution(mesh):
    tokens = P(("dp", "expert"), None)
    in_specs = (
        tokens,
        tokens,
        P("dp"),
        P("dp"),
        P(),
        tokens,
        P(),
        P(),
        P(),
        *([tokens] * 7),
        P("expert", None, None),
        P("expert", None, None),
        *([P()] * 8),
    )
    out_specs = (tokens, tokens, *([P()] * 8))
    return jax.shard_map(body, mesh=mesh, in_specs=in_specs, out_specs=out_specs, check_vma=False)
```

time: 1600 us -> 792 us (0.49)
  Pallas kernels: 0 us -> 557 us
  matrix products: 590 us -> 59.6 us
  waiting for transfers between devices: 408 us -> 54.9 us
  local copies, waits for them, and re-layouts: 228 us -> 66.1 us
  blocking collectives: 154 us -> 0 us
  other arithmetic: 175 us -> 26.1 us
  starting transfers between devices: 21.6 us -> 0.16 us
    pallas_call x0 -> x14, Pallas kernels: none -> 557 us  [the longest x2 194 us: gather_blocks(): pl.pallas_call(functools.partial(gather_kernel, planes, pieces, count, le...]
    dot_general x28 -> x12, matrix products: 490 us -> 30.3 us  [product(): return jnp.dot(left, right, preferred_element_type=F32)]
    psum x1 -> x0, waiting for transfers between devices: 155 us -> none  [body(): lax.psum((place_slot(grad_query_entry), place_slot(grad_query_exit), plac...]
    all_gather x2 -> x0, blocking collectives: 154 us -> none  [the longest x1 144 us: body(): lax.all_gather(router_matrix, ('dp', 'expert'), axis=0, tiled=True)]
    all_gather x7 -> x2, waiting for transfers between devices: 133 us -> 19.1 us  [the longest x1 19.1 us: body(): all_feed = lax.all_gather(feed_payload, 'expert', axis=0, tiled=True)]
    all_to_all x4 -> x0, waiting for transfers between devices: 96.6 us -> none  [the longest x1 61 us: body(): lax.all_to_all(grad_slot, 'expert', split_axis=0, concat_axis=0, tiled=True)]
    dot_general x15 -> x10, matrix products: 81.1 us -> 25.1 us  [product_t(): lax.dot_general(left, right, (((1,), (1,)), ((), ())), preferred_element_...]
    convert_element_type x11 -> x7, other arithmetic: 60 us -> 6.68 us  [the longest x1 2.52 us: body(): grad_input = (grad_mixed + norm_one_back(grad_hidden)[0]).astype(BF)]
  transfers between devices with their start and end apart: 14 -> 4, of which waited for: 8 -> 2; matrix products, arithmetic and copies ran while one was open for 47% -> 7% of each run, Pallas kernels for 0% -> 27%
where the time goes in v1:
time: 792 us; the launch traced here: 782 us
  Pallas kernels  557 us (70%)
  local copies, waits for them, and re-layouts  66.1 us (8%)
  matrix products  59.6 us (8%)
  waiting for transfers between devices  54.9 us (7%)
  other arithmetic  26.1 us (3%)
  between operations  17.6 us (2%)
    pallas_call x2, Pallas kernels, gather_blocks(): pl.pallas_call(functools.partial(gather_kernel, planes, pieces, count, le...  194 us
    pallas_call x1, Pallas kernels, run_experts(): pl.pallas_call(functools.partial(expert_kernel, experts), out_shape=(jax....  72.8 us
    pallas_call x1, Pallas kernels, attend_back(): pl.pallas_call(functools.partial(attend_back_kernel, nb), out_shape=(jax....  58.8 us
    pallas_call x2, Pallas kernels, collect(): pl.pallas_call(functools.partial(collect_kernel, owned, cap, transposed=t...  36.9 us
    reduce_scatter x1, waiting for transfers between devices, body(): lax.psum_scatter(grad_part, 'expert', scatter_dimension=0, tiled=True)  35.7 us
    pallas_call x1, Pallas kernels, attend(): pl.pallas_call(functools.partial(attend_kernel, nb), out_shape=(jax.Shape...  33.9 us
    pallas_call x1, Pallas kernels, exchange_banks(): pl.pallas_call(functools.partial(bank_kernel, planes, wide), out_shape=ja...  33.5 us
    dot_general x12, matrix products, product(): return jnp.dot(left, right, preferred_element_type=F32)  30.3 us
  transfers between devices with their start and end apart: 4, of which 2 were waited for; matrix products, arithmetic and copies ran while one was open for 7% of the time, Pallas kernels for 27%

profile of v1, /device:TPU:0, one launch (start us, length us, event | category | flops | bytes accessed | tf_op | source)
XLA Modules:
  0.0 781.9 jit_solution(16714332445067557955)
XLA Ops:
  7.3 1.5 copy.97
  12.0 1.9 copy.110
  14.1 4.3 reshape.236
  18.4 2.6 copy.101
  21.0 3.5 reshape.237
  24.5 1.6 pad.23
  26.1 3.1 reshape.238.refs_3_
  30.8 173.9 %gather1.1 = (bf16[4,8,64,3712]{3,2,1,0:T(8,128)(2,1)}, bf16[4,8,16,4096]{3,2,1,0:T(8,128)(2,1)}, bf16[4,8,64,2048]{3,2,1,0:T(8,128)(2,1)}, bf16[4,8,64,768]{3,2,1,0:T(8,128)(2,1)}, bf16[4,11,8,2048]{3,2,1,0:T(8,128)(2,1)}) custom-call(bf16[64,3712]{1,0:T(8,128)(2,1)} %concatenate.71.refs_0_, bf16[16,4096]{1,0:T(8,128)(2,1)} %refs_1_.1, ...), custom_call_target="tpu_custom_call" | custom-call | tf_op jit(solution)/shard_map/gather1/pallas_call | solution.py:851
  204.7 9.6 %fusion.110 = f32[320,3712]{1,0:T(8,128)S(1)} fusion(bf16[2048,3712]{1,0:T(8,128)(2,1)} %bitcast.138, bf16[320,2048]{1,0:T(8,128)(2,1)S(1)} %copy-done.11, f32[2048]{0:T(1024)S(1)} %copy-done.79, f32[320]{0:T(512)S(1)} %fusion.93), kind=kOutput, calls=%fused_computation.204 | convolution fusion | flops 4868014080 | bytes 21275904 | tf_op jit(solution)/shard_map/dot_general | solution.py:28
  214.3 1.4 convolution_convert_fusion.8
  218.6 1.4 add_select_fusion.1
  220.7 1.3 fusion.62
  222.0 1.3 fusion.38
  227.7 1.8 concatenate.78.refs_0_
  229.5 20.1 %gather2.1 = bf16[1,8,320,640]{3,2,1,0:T(8,128)(2,1)} custom-call(bf16[320,640]{1,0:T(8,128)(2,1)} %concatenate.78.refs_0_), custom_call_target="tpu_custom_call" | custom-call | tf_op jit(solution)/shard_map/gather2/pallas_call | solution.py:851
  250.1 3.2 concatenate.74
  254.1 1.2 reshape.241
  258.8 1.5 convolution_convert_fusion.9
  260.6 1.8 fusion.18.qr
  262.4 1.1 copy-done.33
  264.3 1.1 copy-done.32
  267.5 33.9 %attend.1 = (bf16[384,2048]{1,0:T(8,128)(2,1)}, f32[8,8,384]{2,1,0:T(8,128)}, bf16[1792,4096]{1,0:T(8,128)(2,1)}) custom-call(s32[12]{0:T(128)} %pad_add_fusion.info, bf16[384,2048]{1,0:T(8,128)(2,1)} %copy-done.32, f32[384,1024]{1,0:T(8,128)} %copy-done.33, f32[384,128]{1,0:T(8,128)} %copy-done.45, f32[384,128]{1,0:T(8,128)} %copy-done.44, ...), custom_call_target="tpu_custom_call" | custom-call | flops 30000001024 | bytes 25000000 | tf_op jit(solution)/shard_map/attend/pallas_call | solution.py:260
  301.4 1.8 convolution_convert_fusion.7
  303.2 7.0 convert_add_fusion
  310.3 1.5 multiply_reduce_fusion.1
  312.1 2.2 fusion.115
  315.5 2.0 concatenate.80
  317.5 1.3 pad.24.sh_out.weight
  318.8 1.3 constant_dynamic-slice_fusion.2
  321.0 17.4 %spread_grad.1 = (bf16[8,8,40,2048]{3,2,1,0:T(8,128)(2,1)}, f32[2560,384]{1,0:T(8,128)}) custom-call(bf16[2560,2176]{1,0:T(8,128)(2,1)} %all-gather.5.cloned.1.call-done.pay, f32[8,8,320]{2,1,0:T(8,128)} %bitcast.135, bf16[384,2048]{1,0:T(8,128)(2,1)} %pad.24.sh_out.weight), custom_call_target="tpu_custom_call" | custom-call | flops 12000000000 | bytes 28000000 | tf_op jit(solution)/shard_map/spread_grad/pallas_call | solution.py:472
  338.4 27.8 %expert_grads.1.back = bf16[8,320,1408]{2,1,0:T(8,128)(2,1)} custom-call(bf16[8,320,2048]{2,1,0:T(8,128)(2,1)} %bitcast.112, bf16[8,1408,2048]{2,1,0:T(8,128)(2,1)} %w_out.3), custom_call_target="tpu_custom_call" | custom-call | flops 14763950080 | bytes 67108864 | tf_op jit(solution)/shard_map/expert_grads/pallas_call | solution.py:543
  366.2 19.1 %all-gather.3.cloned.1.call-done.pay = bf16[2560,2176]{1,0:T(8,128)(2,1)} async-done(((bf16[320,2176]{1,0:T(8,128)(2,1)}), bf16[2560,2176]{1,0:T(8,128)(2,1)}) %all-gather.3.cloned.1.call-update) | async-done | bytes 11141136 | tf_op jit(solution)/shard_map/all_gather | solution.py:1306
  385.3 1.9 convert_add_fusion.1
  389.3 21.1 %spread_feed.1 = (bf16[8,8,40,2048]{3,2,1,0:T(8,128)(2,1)}, f32[8,8,40,128]{3,2,1,0:T(8,128)}, bf16[2560,384]{1,0:T(8,128)(2,1)}, bf16[2560,768]{1,0:T(8,128)(2,1)}) custom-call(bf16[2560,2176]{1,0:T(8,128)(2,1)} %all-gather.3.cloned.1.call-done.pay, f32[8,8,320]{2,1,0:T(8,128)} %bitcast.136, f32[8,8,320]{2,1,0:T(8,128)} %bitcast.137, ...), custom_call_target="tpu_custom_call" | custom-call | flops 14000000000 | bytes 28000000 | tf_op jit(solution)/shard_map/spread_feed/pallas_call | solution.py:493
  410.4 72.8 %experts.1 = (bf16[8,320,2176]{2,1,0:T(8,128)(2,1)}, bf16[8,320,1408]{2,1,0:T(8,128)(2,1)}) custom-call(s32[1]{0:T(128)} %bitcast.23.first, bf16[8,320,2048]{2,1,0:T(8,128)(2,1)} %bitcast.154, bf16[8,320,1408]{2,1,0:T(8,128)(2,1)} %expert_grads.1.back, f32[8,320,128]{2,1,0:T(8,128)} %bitcast.124, bf16[8,2048,2816]{2,1,0:T(8,128)(2,1)} %w_in.1), custom_call_target="tpu_custom_call" | custom-call | flops 59055800320 | bytes 92274688 | tf_op jit(solution)/shard_map/experts/pallas_call | solution.py:558
  483.2 20.1 %collect_grad.1 = bf16[2560,2176]{1,0:T(8,128)(2,1)} custom-call(bf16[8,8,40,2176]{3,2,1,0:T(8,128)(2,1)} %bitcast.153, bf16[2560,128]{1,0:T(8,128)(2,1)} %pad.25.slots, bf16[2560,768]{1,0:T(8,128)(2,1)} %get-tuple-element.61.inner, bf16[2048,768]{1,0:T(8,128)(2,1)} %bitcast.152), custom_call_target="tpu_custom_call" | custom-call | flops 14000000000 | bytes 28000000 | tf_op jit(solution)/shard_map/collect_grad/pallas_call | solution.py:593
  503.4 29.4 %expert_rows.1 = bf16[8,320,2048]{2,1,0:T(8,128)(2,1)} custom-call(bf16[8,320,1408]{2,1,0:T(8,128)(2,1)} %get-tuple-element.62.inner, f32[8,320,128]{2,1,0:T(8,128)} %bitcast.125, bf16[8,1408,2048]{2,1,0:T(8,128)(2,1)} %w_out.3), custom_call_target="tpu_custom_call" | custom-call | flops 14763950080 | bytes 67108864 | tf_op jit(solution)/shard_map/expert_rows/pallas_call | solution.py:579
  532.8 16.8 %collect_rows.1 = bf16[2560,2048]{1,0:T(8,128)(2,1)} custom-call(bf16[8,8,40,2048]{3,2,1,0:T(8,128)(2,1)} %bitcast.109, bf16[2560,128]{1,0:T(8,128)(2,1)} %pad.25.slots, bf16[2560,384]{1,0:T(8,128)(2,1)} %get-tuple-element.63.inner, bf16[384,2048]{1,0:T(8,128)(2,1)} %pad.24.sh_out.weight), custom_call_target="tpu_custom_call" | custom-call | flops 14000000000 | bytes 28000000 | tf_op jit(solution)/shard_map/collect_rows/pallas_call | solution.py:593
  551.1 1.2 slice.117
  552.4 35.7 %reduce-scatter.5.cloned.1.call-done = bf16[320,2176]{1,0:T(8,128)(2,1)} async-done(((bf16[2560,2176]{1,0:T(8,128)(2,1)}), bf16[320,2176]{1,0:T(8,128)(2,1)}) %reduce-scatter.5.cloned.1.call-update) | async-done | bytes 1392656 | tf_op jit(solution)/shard_map/reduce_scatter | solution.py:1332
  588.2 1.5 convert_element_type.148
  590.1 2.1 multiply_reduce_fusion
  592.8 2.3 convolution_convert_fusion.6
  595.5 2.9 fusion.103
  598.6 1.5 constant_dynamic-update-slice_fusion.2
  600.1 1.2 copy-done.31
  604.2 58.8 %attend_back.1 = (bf16[384,2048]{1,0:T(8,128)(2,1)}, bf16[384,1024]{1,0:T(8,128)(2,1)}, f32[128,4096]{1,0:T(8,128)}, f32[2560,640]{1,0:T(8,128)}) custom-call(s32[12]{0:T(128)} %pad_add_fusion.info, bf16[384,2048]{1,0:T(8,128)(2,1)} %copy-done.32, f32[384,1024]{1,0:T(8,128)} %copy-done.33, f32[384,128]{1,0:T(8,128)} %copy-done.45, f32[384,128]{1,0:T(8,128)} %copy-done.44, ...), custom_call_target="tpu_custom_call" | custom-call | flops 54000001024 | bytes 30000000 | tf_op jit(solution)/shard_map/attend_back/pallas_call | solution.py:298
  663.0 3.4 convert.61
  666.4 1.5 copy-done.8
  667.9 1.6 add_convert_fusion
  669.9 2.7 maximum_maximum_fusion.blocks
  672.6 24.1 %scatter5.1 = f32[320,640]{1,0:T(8,128)} custom-call(bf16[8,320,640]{2,1,0:T(8,128)(2,1)} %maximum_maximum_fusion.blocks), custom_call_target="tpu_custom_call" | custom-call | tf_op jit(solution)/shard_map/scatter5/pallas_call | solution.py:1032
  696.7 2.0 constant_dynamic-slice_fusion
  698.8 1.3 multiply_reduce_fusion.2
  700.2 1.5 constant_dynamic-slice_fusion.1
  704.3 4.4 concatenate.86
  709.3 1.9 fusion.26
  713.3 2.1 fusion.23
  717.8 33.5 %banks6.1.full = bf16[4,8,16,2176]{3,2,1,0:T(8,128)(2,1)} custom-call(bf16[16,17408]{1,0:T(8,128)(2,1)} %copy-done.43), custom_call_target="tpu_custom_call" | custom-call | tf_op jit(solution)/shard_map/banks6/pallas_call | solution.py:899
  751.3 7.7 place_banks.1
  758.9 9.3 %fusion.116 = f32[320,2048]{1,0:T(8,128)S(1)} fusion(bf16[320,3712]{1,0:T(8,128)(2,1)} %concatenate.86, bf16[2048,3712]{1,0:T(8,128)(2,1)} %bitcast.141), kind=kOutput, calls=%fused_computation.209 | convolution fusion | flops 4865392640 | bytes 20201472 | tf_op jit(solution)/shard_map/dot_general | solution.py:32
  768.3 1.5 convolution_add_fusion.1
  769.8 1.8 fusion.11
  772.7 2.5 fusion.7
  (298 shorter events, 37.5 us)
Async XLA Ops:
  7.2 246.2 %copy-start = (bf16[8,16,3072]{2,1,0:T(8,128)(2,1)S(1)}, bf16[8,16,3072]{2,1,0:T(8,128)(2,1)}, u32[]{:S(2)}) copy-start(bf16[8,16,3072]{2,1,0:T(8,128)(2,1)} %param.45) | copy-start | bytes 2359300
  7.2 4.4 copy-start.11
  7.2 311.6 %all-gather.5.cloned.1.call-start = ((), (), s32[]{:S(2)}) async-start(), calls=%async_computation.3 | async-start | bytes 12533760 | tf_op jit(solution)/shard_map/all_gather | solution.py:1281
  12.0 6.4 copy-start.65
  12.0 202.4 %copy-start.81 = (f32[320]{0:T(512)}, f32[320]{0:T(512)S(1)}, u32[]{:S(2)}) copy-start(f32[320]{0:T(512)S(1)} %fusion.93) | copy-start | bytes 3844
  21.0 8.9 %copy-start.37 = (bf16[64,2048]{1,0:T(8,128)(2,1)S(1)}, bf16[64,2048]{1,0:T(8,128)(2,1)}, u32[]{:S(2)}) copy-start(bf16[64,2048]{1,0:T(8,128)(2,1)} %copy.110) | copy-start | bytes 786436
  21.0 8.9 %copy-start.51 = (bf16[64,576]{1,0:T(8,128)(2,1)S(1)}, bf16[64,576]{1,0:T(8,128)(2,1)}, u32[]{:S(2)}) copy-start(bf16[64,576]{1,0:T(8,128)(2,1)} %param.36) | copy-start | bytes 221188
  21.0 8.9 %copy-start.75 = (bf16[64,64]{1,0:T(8,128)(2,1)S(1)}, bf16[64,64]{1,0:T(8,128)(2,1)}, u32[]{:S(2)}) copy-start(bf16[64,64]{1,0:T(8,128)(2,1)} %param.39) | copy-start | bytes 24580
  26.1 178.6 %copy-start.79 = (f32[2048]{0:T(1024)S(1)}, f32[2048]{0:T(1024)}, u32[]{:S(2)}) copy-start(f32[2048]{0:T(1024)} %param.32) | copy-start | bytes 24580
  216.4 8.1 %copy-start.61 = (f32[512]{0:T(512)S(1)}, f32[512]{0:T(512)}, u32[]{:S(2)}) copy-start(f32[512]{0:T(512)} %param.33) | copy-start | bytes 6148
  217.5 11.9 %copy-start.9 = (f32[320,576]{1,0:T(8,128)}, f32[320,576]{1,0:T(8,128)S(1)}, u32[]{:S(2)}) copy-start(f32[320,576]{1,0:T(8,128)S(1)} %convolution_add_fusion.7) | copy-start | bytes 2211844
  218.6 5.5 copy-start.67
  222.0 36.3 %copy-start.26 = (f32[320,32]{1,0:T(8,128)}, f32[320,32]{1,0:T(8,128)S(1)}, u32[]{:S(2)}) copy-start(f32[320,32]{1,0:T(8,128)S(1)} %get-tuple-element.96) | copy-start | bytes 122884
  225.6 24.0 %copy-start.78 = (s32[320,6]{0,1:T(8,128)S(1)}, s32[320,6]{0,1:T(8,128)}, u32[]{:S(2)}) copy-start(s32[320,6]{0,1:T(8,128)} %param.31) | copy-start | bytes 23044
  250.0 5.5 copy-start.38
  250.1 5.7 copy-start.73
  250.1 6.4 copy-start.74
  253.3 4.0 copy-start.84
  253.3 5.3 copy-start.29
  253.3 5.3 copy-start.40
  253.3 5.5 copy-start.82
  253.3 132.0 %all-gather.3.cloned.1.call-start = ((), (), s32[]{:S(2)}) async-start(), calls=%async_computation.2 | async-start | bytes 12533760 | tf_op jit(solution)/shard_map/all_gather | solution.py:1306
  254.1 9.7 %slice-start = ((s8[4751360]{0:T(1024)(128)(4,1)}), s8[557056]{0:T(1024)(128)(4,1)S(1)}, s32[]{:S(2)}) async-start(s8[4751360]{0:T(1024)(128)(4,1)} %bitcast.115), calls=%async_computation.6 | async-start | bytes 1114112
  255.3 8.5 %copy-start.41 = (bf16[16,16,128]{2,1,0:T(8,128)(2,1)}, bf16[16,16,128]{2,1,0:T(8,128)(2,1)S(1)}, u32[]{:S(2)}) copy-start(bf16[16,16,128]{2,1,0:T(8,128)(2,1)S(1)} %slice.137) | copy-start | bytes 196612
  255.7 4.9 copy-start.46
  257.5 3.1 copy-start.85
  258.5 3.9 copy-start.45
  258.8 3.6 copy-start.44
  258.8 5.0 slice-start.1
  260.3 3.4 copy-start.55
  303.2 7.0 copy-start.49
  311.7 2.6 copy-start.2
  311.7 2.6 copy-start.69
  314.3 4.5 copy-start.53
  314.3 3.2 copy-start.34
  314.4 4.4 copy-start.22
  317.4 270.7 %reduce-scatter.5.cloned.1.call-start = ((), (), s32[]{:S(2)}) async-start(), calls=%async_computation.5 | async-start | bytes 12533760 | tf_op jit(solution)/shard_map/reduce_scatter | solution.py:1332
  503.3 196.9 %reduce-scatter.3.cloned.1.call-start = ((), (), s32[]{:S(2)}) async-start(), calls=%async_computation.4 | async-start | bytes 11796480 | tf_op jit(solution)/shard_map/reduce_scatter | solution.py:1338
  550.5 39.2 %copy-start.23 = (f32[320,64]{1,0:T(8,128)S(1)}, f32[320,64]{1,0:T(8,128)}, u32[]{:S(2)}) copy-start(f32[320,64]{1,0:T(8,128)} %copy-done.22) | copy-start | bytes 245764
  550.5 39.2 %copy-start.54 = (f32[320]{0:T(512)S(1)}, f32[320]{0:T(512)}, u32[]{:S(2)}) copy-start(f32[320]{0:T(512)} %copy-done.53) | copy-start | bytes 3844
  550.5 39.3 %copy-start.60 = (f32[320]{0:T(512)S(1)}, f32[320]{0:T(512)}, u32[]{:S(2)}) copy-start(f32[320]{0:T(512)} %copy-done.59) | copy-start | bytes 3844
  550.5 39.6 %copy-start.3 = (f32[320,2048]{1,0:T(8,128)S(1)}, f32[320,2048]{1,0:T(8,128)}, u32[]{:S(2)}) copy-start(f32[320,2048]{1,0:T(8,128)} %copy-done.2) | copy-start | bytes 7864324
  550.5 39.6 %copy-start.58 = (f32[2048]{0:T(1024)S(1)}, f32[2048]{0:T(1024)}, u32[]{:S(2)}) copy-start(f32[2048]{0:T(1024)} %param.34) | copy-start | bytes 24580
  590.1 5.1 slice-start.3
  592.2 3.3 slice-start.4
  592.8 5.6 copy-start.5
  598.6 2.7 copy-start.16
  663.0 4.9 copy-start.8
  672.6 26.2 %copy-start.10 = (f32[320,576]{1,0:T(8,128)S(1)}, f32[320,576]{1,0:T(8,128)}, u32[]{:S(2)}) copy-start(f32[320,576]{1,0:T(8,128)} %copy-done.9) | copy-start | bytes 2211844
  672.6 26.2 %copy-start.62 = (f32[512]{0:T(512)S(1)}, f32[512]{0:T(512)}, u32[]{:S(2)}) copy-start(f32[512]{0:T(512)} %param.33) | copy-start | bytes 6148
  672.6 27.5 %copy-start.30 = (f32[320,32]{1,0:T(8,128)S(1)}, f32[320,32]{1,0:T(8,128)}, u32[]{:S(2)}) copy-start(f32[320,32]{1,0:T(8,128)} %copy-done.28) | copy-start | bytes 122884
  696.7 3.4 copy-start.18
  696.7 5.0 copy-start.56
  704.2 4.5 slice-start.2
  704.2 5.1 copy-start.25
  704.2 5.1 copy-start.47
  704.3 5.1 copy-start.52
  708.7 2.6 copy-start.12
  708.7 2.6 copy-start.80
  708.7 2.6 copy-start.83
  711.8 4.5 copy-start.17
  712.3 4.3 copy-start.6
  712.3 4.3 copy-start.50
  769.8 2.9 copy-start.36
  (32 other events, 52.5 us)
Sparse Core Ops, SparseCore 0:
  253.5 63.2 all-gather.4
  319.2 66.0 all-gather.2
  503.4 84.6 reduce-scatter.4
  591.9 81.5 reduce-scatter.2

commit v2 on v1

--- a/solution.py
+++ b/solution.py
@@ -170,8 +170,8 @@
 
 
 def attend_back_kernel(
-    nb, info, qn, qr, cosp, sinp, qlim, tails, kv, up, upx, do, stats,
-    dqn, dqr, gup, dlat, tail, kr, bias, near, dss, dkv, acc, dkr,
+    nb, info, qn, qr, cosp, sinp, qlim, tails, kv, up, upx, do, att, stats, upper,
+    dqn, dqr, gup, dlow, tail, kr, bias, near, dss, dkv, acc, dkr, dlat,
 ):
     step = pl.program_id(0)
     rows_all = qn.shape[0]
@@ -197,7 +197,11 @@
         v = kv[:, a * 256 + 128 : a * 256 + 256]
         g = do[:, a * 128 : a * 128 + 128]
         level = stats[0, a : a + 1, :]
-        delta = stats[0, 2 + a : 3 + a, :]
+        shares = g.astype(F32) * att[:, a * 128 : a * 128 + 128].astype(F32)
+        main = shares.astype(BF)
+        ones = jnp.ones((8, 128), BF)
+        delta = product_t(ones, main) + product_t(ones, (shares - main.astype(F32)).astype(BF))
+        delta = delta[:1]
         mine = lane_iota((1, 128)) % ROPE
         mine = (mine < HALF) if a == 0 else (mine >= HALF)
 
@@ -241,6 +245,9 @@
                 start = pl.multiple_of(info[side * nb + m] * SEGLEN, SEGLEN)
                 at = TRUNK + (2 * m + side) * SEGLEN
                 dlat[pl.ds(start, SEGLEN), :] += acc[at : at + SEGLEN, :]
+        low = dlat[:, KVR:].astype(BF)
+        dlow[:, KVR:] = low
+        dlow[:, :KVR] = (dlat[:, :KVR] + product(low, upper[...])).astype(BF)
 
 
 def pair_spec(rows, width):
@@ -293,7 +300,7 @@
     )(info, qn, qr, cosp, sinp, qlim[None, :], lat, up, upx)
 
 
-def attend_back(nb, info, qn, qr, cosp, sinp, qlim, lat, kv, up, upx, do, stats):
+def attend_back(nb, info, qn, qr, cosp, sinp, qlim, lat, kv, up, upx, do, att, stats, upper):
     rows, keys = qn.shape[0], TRUNK + 2 * nb * SEGLEN
     return pl.pallas_call(
         functools.partial(attend_back_kernel, nb),
@@ -301,7 +308,7 @@
             jax.ShapeDtypeStruct((rows, HEADS * NOPE), BF),
             jax.ShapeDtypeStruct((rows, HEADS * ROPE), BF),
             jax.ShapeDtypeStruct((128, HEADS * (NOPE + VDIM)), F32),
-            jax.ShapeDtypeStruct((TREE, LATW), F32),
+            jax.ShapeDtypeStruct((TREE, LATW), BF),
         ),
         grid_spec=pltpu.PrefetchScalarGridSpec(
             num_scalar_prefetch=1,
@@ -317,7 +324,9 @@
                 pair_spec(KVR, 512),
                 pair_spec(LATW - KVR, 512),
                 pair_spec(rows, 256),
+                pair_spec(rows, 256),
                 lead_spec(8, rows),
+                whole_spec((LATW - KVR, KVR)),
             ],
             out_specs=(
                 pair_spec(rows, 256),
@@ -334,11 +343,363 @@
                 pltpu.VMEM((keys, 512), BF),
                 pltpu.VMEM((keys, LATW), F32),
                 pltpu.VMEM((keys, 128), F32),
+                pltpu.VMEM((TREE, LATW), F32),
             ],
         ),
         name="attend_back",
         **costs(54e9, 30e6),
-    )(info, qn, qr, cosp, sinp, qlim[None, :], lat, kv, up, upx, do, stats)
+    )(info, qn, qr, cosp, sinp, qlim[None, :], lat, kv, up, upx, do, att, stats, upper)
+
+
+def prepare_kernel(planes, query, down, router, shared, front, cut):
+    wide = query[...].astype(F32)
+    nope, rope = [], []
+    for pair in range(HEADS // 2):
+        starts = [(2 * pair + a) * (NOPE + ROPE) for a in range(2)]
+        for at in starts:
+            nope.append(wide[:, at : at + NOPE])
+        for half in range(2):
+            for at in starts:
+                first = at + NOPE + half * HALF
+                rope.append(wide[:, first : first + HALF])
+    rest = [down[...].astype(F32), router[...].astype(F32)]
+    front[...] = jnp.concatenate(nope + rope + rest, 1).astype(BF)
+    whole = shared[...].astype(F32)
+    groups, _, width = cut.shape
+    hidden = whole.shape[1] // 2
+    each = hidden // (planes * groups)
+    blank = jnp.zeros((whole.shape[0], width // 2 - planes * each), F32)
+    for j in range(groups):
+        columns = []
+        for part in range(2):
+            for i in range(planes):
+                at = part * hidden + (i * groups + j) * each
+                columns.append(whole[:, at : at + each])
+            columns.append(blank)
+        cut[j] = jnp.concatenate(columns, 1).astype(BF)
+
+
+def prepare(query, down, router, shared, planes, groups, padded):
+    rows = query.shape[0]
+    width = query.shape[1] + down.shape[1] + router.shape[1]
+    return pl.pallas_call(
+        functools.partial(prepare_kernel, planes),
+        out_shape=(
+            jax.ShapeDtypeStruct((rows, width), BF),
+            jax.ShapeDtypeStruct((groups, rows, 2 * padded), BF),
+        ),
+        name="prepare",
+        **costs(1e6, 3e6),
+    )(query, down, router, shared)
+
+
+def project_kernel(
+    info, tokens, front, query_in, query_out, lower_in, lower_out, upper_in, mixer, gain, cos, sin,
+    qn, qr, ext, raw, hidden, query_mid, lower_mid, acc,
+):
+    step = pl.program_id(0)
+
+    @pl.when(step == 0)
+    def _():
+        hidden[...] = normed(tokens[...].astype(F32), mixer[...]).astype(BF)
+        query_mid[...] = product_t(hidden[...], query_in[...]).astype(BF)
+        lower_mid[...] = product_t(hidden[...], lower_in[...]).astype(BF)
+
+    depth = front.shape[0]
+    part = product(hidden[:, pl.ds(pl.multiple_of(step * depth, depth), depth)], front[...])
+
+    @pl.when(step == 0)
+    def _():
+        acc[...] = part
+
+    @pl.when(step > 0)
+    def _():
+        acc[...] += part
+
+    @pl.when(step == pl.num_programs(0) - 1)
+    def _():
+        rows = hidden.shape[0]
+        wide = HEADS * (NOPE + ROPE)
+        middle = HEADS * NOPE
+        here = pl.ds(pl.multiple_of(info[0], 16), rows)
+        qn[...] = jnp.zeros_like(qn)
+        qr[...] = jnp.zeros_like(qr)
+        mid = query_mid[...]
+        qn[here, :] = (acc[:, :middle] + product(mid, query_out[:, :middle])).astype(BF)
+        qr[here, :] = acc[:, middle:wide] + product(mid, query_out[:, middle:])
+        low = product(lower_mid[...], lower_out[...])
+        latent = acc[:, wide : wide + KVR] + low[:, :KVR]
+        raw[...] = latent
+        norm = normed(latent, gain[...]).astype(BF)
+        upper = product_t(norm, upper_in[...])
+        key = acc[:, wide + KVR : wide + KVR + ROPE] + low[:, KVR:]
+        first, second = key[:, :HALF], key[:, HALF:]
+        c, s = cos[...], sin[...]
+        ext[:, :KVR] = norm
+        ext[:, KVR:] = jnp.concatenate(
+            [
+                first * c - second * s,
+                upper,
+                jnp.zeros((rows, HALF - upper.shape[1]), F32),
+                second * c + first * s,
+                jnp.zeros((rows, HALF), F32),
+            ],
+            1,
+        ).astype(BF)
+
+
+def fixed_at(value):
+    return pl.BlockSpec(value.shape, lambda i, info: (0,) * value.ndim)
+
+
+def whole_out(shape):
+    return pl.BlockSpec(shape, lambda i, info: (0,) * len(shape))
+
+
+def project(nb, shift, tokens, front, small):
+    rows, depth = tokens.shape
+    padded, step, rank = nb * SEGLEN, 512, small[0].shape[0]
+    shapes = [
+        ((padded, HEADS * NOPE), BF),
+        ((padded, HEADS * ROPE), F32),
+        ((rows, LATW), BF),
+        ((rows, KVR), F32),
+        ((rows, depth), BF),
+        ((rows, rank), BF),
+        ((rows, rank), BF),
+    ]
+    return pl.pallas_call(
+        project_kernel,
+        out_shape=[jax.ShapeDtypeStruct(shape, kind) for shape, kind in shapes],
+        grid_spec=pltpu.PrefetchScalarGridSpec(
+            num_scalar_prefetch=1,
+            grid=(depth // step,),
+            in_specs=[
+                fixed_at(tokens),
+                pl.BlockSpec((step, front.shape[1]), lambda i, info: (i, 0)),
+                *[fixed_at(v) for v in small],
+            ],
+            out_specs=[whole_out(shape) for shape, _ in shapes],
+            scratch_shapes=[pltpu.VMEM((rows, front.shape[1]), F32)],
+        ),
+        name="project",
+        **costs(5e9, 20e6),
+    )(shift, tokens, front, *small)
+
+
+def mix_kernel(
+    info, attended, tokens, matrix, router, out_in, out_out, gain,
+    mixed, payload, probs, out_mid, acc,
+):
+    step = pl.program_id(0)
+    rows = tokens.shape[0]
+    here = pl.ds(pl.multiple_of(info[0], 16), rows)
+
+    @pl.when(step == 0)
+    def _():
+        out_mid[...] = product_t(attended[here, :], out_in[...]).astype(BF)
+
+    depth = matrix.shape[0]
+    columns = pl.ds(pl.multiple_of(step * depth, depth), depth)
+    part = product(attended[here, columns], matrix[...])
+
+    @pl.when(step == 0)
+    def _():
+        acc[...] = part
+
+    @pl.when(step > 0)
+    def _():
+        acc[...] += part
+
+    @pl.when(step == pl.num_programs(0) - 1)
+    def _():
+        state = tokens[...].astype(F32) + (acc[...] + product(out_mid[...], out_out[...]))
+        mixed[...] = state
+        feed = normed(state, gain[...]).astype(BF)
+        experts = probs.shape[1]
+        logits = product(feed, router[...])[:, 128 - experts :]
+        powers = jnp.exp(logits - jnp.max(logits, axis=1, keepdims=True))
+        chance = powers / jnp.sum(powers, axis=1, keepdims=True)
+        probs[...] = chance
+        high = chance.astype(BF).astype(F32)
+        payload[:, :D] = feed
+        payload[:, D:] = jnp.concatenate([high, chance - high], 1).astype(BF)
+
+
+def mix(shift, attended, tokens, matrix, front, out_in, out_out, gain, experts):
+    rows = tokens.shape[0]
+    step, rank = 512, out_in.shape[0]
+    last = front.shape[1] // 128 - 1
+    shapes = [((rows, D), F32), ((rows, D + 128), BF), ((rows, experts), F32), ((rows, rank), BF)]
+    return pl.pallas_call(
+        mix_kernel,
+        out_shape=[jax.ShapeDtypeStruct(shape, kind) for shape, kind in shapes],
+        grid_spec=pltpu.PrefetchScalarGridSpec(
+            num_scalar_prefetch=1,
+            grid=(D // step,),
+            in_specs=[
+                fixed_at(attended),
+                fixed_at(tokens),
+                pl.BlockSpec((step, D), lambda i, info: (i, 0)),
+                pl.BlockSpec((D, 128), lambda i, info: (0, last)),
+                fixed_at(out_in),
+                fixed_at(out_out),
+                fixed_at(gain),
+            ],
+            out_specs=[whole_out(shape) for shape, _ in shapes],
+            scratch_shapes=[pltpu.VMEM((rows, D), F32)],
+        ),
+        name="mix",
+        **costs(3e9, 14e6),
+    )(shift, attended, tokens, matrix, front, out_in, out_out, gain)
+
+
+def turn_kernel(
+    info, sums, probs, mixed, cotangent, gain, router, out_in, out_out, matrix,
+    grad_mixed, out_mid, do, low,
+):
+    rows = mixed.shape[0]
+
+    @pl.when(pl.program_id(0) == 0)
+    def _():
+        experts = probs.shape[1]
+        both = sums[:, D:].astype(F32)
+        direct = both[:, :experts] + both[:, experts:]
+        chance = probs[...]
+        logits = chance * (direct - jnp.sum(chance * direct, axis=1, keepdims=True))
+        spread = jnp.concatenate([jnp.zeros((rows, 128 - experts), F32), logits], 1).astype(BF)
+        keep = jnp.where(lane_iota(router.shape) >= 128 - experts, router[...].astype(F32), 0.0)
+        feed = sums[:, :D].astype(F32) + product_t(spread, keep.astype(BF))
+        state = mixed[...]
+        inverse = lax.rsqrt(jnp.mean(state * state, axis=-1, keepdims=True) + 1e-06)
+        scaled = feed * gain[...]
+        along = jnp.mean(scaled * state, axis=-1, keepdims=True)
+        back = inverse * scaled - state * (inverse * inverse * inverse * along)
+        total = cotangent[...].astype(F32) + back
+        grad_mixed[...] = total
+        low[...] = total.astype(BF)
+        out_mid[...] = product_t(low[...], out_out[...]).astype(BF)
+
+    here = pl.ds(pl.multiple_of(info[0], 16), rows)
+    do[...] = jnp.zeros_like(do)
+    do[here, :] = (
+        product_t(low[...], matrix[...]) + product(out_mid[...], out_in[...])
+    ).astype(BF)
+
+
+def turn(nb, shift, sums, probs, mixed, cotangent, gain, front, out_in, out_out, matrix):
+    rows, experts = probs.shape
+    step, rank = 512, out_in.shape[0]
+    last = front.shape[1] // 128 - 1
+    padded = nb * SEGLEN
+    return pl.pallas_call(
+        turn_kernel,
+        out_shape=[
+            jax.ShapeDtypeStruct((rows, D), F32),
+            jax.ShapeDtypeStruct((rows, rank), BF),
+            jax.ShapeDtypeStruct((padded, D), BF),
+        ],
+        grid_spec=pltpu.PrefetchScalarGridSpec(
+            num_scalar_prefetch=1,
+            grid=(D // step,),
+            in_specs=[
+                fixed_at(sums),
+                fixed_at(probs),
+                fixed_at(mixed),
+                fixed_at(cotangent),
+                fixed_at(gain),
+                pl.BlockSpec((D, 128), lambda i, info: (0, last)),
+                pl.BlockSpec((rank, step), lambda i, info: (0, i)),
+                fixed_at(out_out),
+                pl.BlockSpec((step, D), lambda i, info: (i, 0)),
+            ],
+            out_specs=[
+                whole_out((rows, D)),
+                whole_out((rows, rank)),
+                pl.BlockSpec((padded, step), lambda i, info: (0, i)),
+            ],
+            scratch_shapes=[pltpu.VMEM((rows, D), BF)],
+        ),
+        name="turn",
+        **costs(3e9, 18e6),
+    )(shift, sums, probs, mixed, cotangent, gain, front, out_in, out_out, matrix)
+
+
+def join_kernel(
+    offsets, info, dqn, dqr, query_out, query_mid, hidden, sums, raw, gain, cos, sin, lower_out,
+    lower_mid, tree, lat, upper_exit, out_mid, mixed, grad_out_mid, attended,
+    grads, joined, grad_query_mid, grad_lower_mid,
+):
+    rows = hidden.shape[0]
+    here = pl.ds(pl.multiple_of(info[0], 16), rows)
+    nope, rope = dqn[here, :], dqr[here, :]
+    middle, wide = HEADS * NOPE, HEADS * (NOPE + ROPE)
+    values = raw[...]
+    inverse = lax.rsqrt(jnp.mean(values * values, axis=-1, keepdims=True) + 1e-06)
+    scaled = sums[:, :KVR] * gain[...]
+    along = jnp.mean(scaled * values, axis=-1, keepdims=True)
+    latent = inverse * scaled - values * (inverse * inverse * inverse * along)
+    first = sums[:, KVR : KVR + HALF]
+    second = sums[:, KVR + ROPE : KVR + ROPE + HALF]
+    c, s = cos[...], sin[...]
+    key = jnp.concatenate(
+        [first * c + second * s, second * c - first * s, jnp.zeros((rows, ROPE), F32)], 1
+    )
+    low = jnp.concatenate([latent, key], 1).astype(BF)
+    grads[:, :middle] = nope
+    grads[:, middle:wide] = rope
+    grads[:, wide:] = low
+    back_low = product_t(low[:, : KVR + ROPE], lower_out[...]).astype(BF)
+    back_query = (
+        product_t(nope, query_out[:, :middle]) + product_t(rope, query_out[:, middle:])
+    ).astype(BF)
+    grad_lower_mid[...] = back_low
+    grad_query_mid[...] = back_query
+    exit_nope = product_left(query_mid[...], nope)
+    exit_rope = product_left(query_mid[...], rope)
+    heads = []
+    for head in range(HEADS):
+        at = (head // 2) * 128 + (head % 2) * HALF
+        heads += [
+            exit_nope[:, head * NOPE : (head + 1) * NOPE],
+            exit_rope[:, at : at + HALF],
+            exit_rope[:, at + ROPE : at + ROPE + HALF],
+        ]
+    rank = back_low.shape[1]
+    pieces = (
+        product_left(back_query, hidden[...]),
+        jnp.concatenate(heads, 1),
+        product_left(back_low, hidden[...]),
+        product_left(lower_mid[...], low),
+        product_left(tree[:, KVR:], lat[:, :KVR])[HALF : HALF + rank],
+        upper_exit[HALF : HALF + rank, :],
+        product_left(grad_out_mid[...], attended[here, :]),
+        product_left(out_mid[...], mixed[...].astype(BF)),
+    )
+    end = 0
+    for (at, _), piece in zip(offsets, pieces):
+        end = at + piece.shape[1]
+        joined[:, at:end] = piece.astype(BF)
+    joined[:, end:] = jnp.zeros((rank, joined.shape[1] - end), BF)
+
+
+def join(offsets, total, shift, operands):
+    hidden, query_mid = operands[4], operands[3]
+    rows, rank = query_mid.shape
+    wide = HEADS * (NOPE + ROPE) + KVR + 2 * ROPE
+    shapes = [((rows, wide), BF), ((rank, total), BF), ((rows, rank), BF), ((rows, rank), BF)]
+    return pl.pallas_call(
+        functools.partial(join_kernel, offsets),
+        out_shape=[jax.ShapeDtypeStruct(shape, kind) for shape, kind in shapes],
+        grid_spec=pltpu.PrefetchScalarGridSpec(
+            num_scalar_prefetch=1,
+            grid=(1,),
+            in_specs=[fixed_at(v) for v in operands],
+            out_specs=[whole_out(shape) for shape, _ in shapes],
+        ),
+        name="join",
+        **costs(3e9, 25e6),
+    )(shift, *operands)
 
 
 def gated_parts(gate, up):
@@ -772,16 +1133,17 @@
         mail.arrived(landing((e + PLANE - j) % PLANE), pair, (n, j - 1))
 
 
-def gather_kernel(planes, pieces, count, swaps, lines, *refs):
+def gather_kernel(planes, depth, pieces, count, swaps, lines, *refs):
     total = count + swaps + lines
     shards, outs = refs[:total], refs[total : 2 * total]
     sems = refs[2 * total :]
     own_sem, swap, line = sems[10], sems[11:13], sems[13:15]
     e = neighbours()[0]
-    levels = nearest_levels(planes)
+    levels = nearest_levels(depth)
     z = levels[0]
     mail = Mail()
-    greet(plane_peers(swaps), other_levels(planes))
+    greet(plane_peers(swaps), other_levels(depth))
+    home = z if planes > 1 else 0
 
     def place(level, who, i):
         array, first, rows = pieces[i]
@@ -791,7 +1153,7 @@
         array, first, rows = pieces[i]
         return shards[array].at[pl.ds(first, rows)]
 
-    mine = [pltpu.make_async_copy(shards[a], outs[a].at[z, e], own_sem.at[a]) for a in range(count)]
+    mine = [pltpu.make_async_copy(shards[a], outs[a].at[home, e], own_sem.at[a]) for a in range(count)]
     for a in range(count, count + swaps):
         mine.append(pltpu.make_async_copy(shards[a].at[e], outs[a].at[z, e], own_sem.at[a]))
     for a in range(count + swaps, total):
@@ -815,23 +1177,24 @@
             src = here if k or a < count + swaps else shards[a].at[rows]
             if k:
                 mail.line_arrived(here, line, (levels[k], i))
-            mail.along(levels[k], planes, src, here, line, (levels[k], i))
+            mail.along(levels[k], depth, src, here, line, (levels[k], i))
+
+    first = 2 if planes > 1 else 0
 
     def meanwhile(s):
-        if s == planes - 1:
+        if s == 1:
             for n in range(swaps):
                 a = count + n
                 swap_in(mail, lambda who: outs[a].at[z, who], swap, n)
                 mine[a].wait()
-            line_step(0)
-        if s >= planes:
-            line_step(s - planes + 1)
+        if 0 <= s - first < depth:
+            line_step(s - first)
 
     spread_pieces(
         planes, len(pieces), source, place, mail, sems, meanwhile if cuts else None
     )
     if cuts:
-        for k in range(3, planes):
+        for k in range(planes + 2 - first, depth):
             line_step(k)
     for n, copy in enumerate(mine):
         if not count <= n < count + swaps:
@@ -839,17 +1202,20 @@
     mail.drain()
 
 
-def gather_blocks(shards, planes, cuts, ident, swaps=(), lines=()):
+def gather_blocks(shards, planes, cuts, ident, swaps=(), lines=(), depth=None):
     dma = pltpu.SemaphoreType.DMA
+    depth = planes if depth is None else depth
     pieces = []
     for array, (shard, cut) in enumerate(zip(shards, cuts)):
         rows = shard.shape[0] // cut
         pieces += [(array, at * rows, rows) for at in range(cut)]
     count, total = len(shards), len(shards) + len(swaps) + len(lines)
     shapes = [jax.ShapeDtypeStruct((planes, PLANE) + s.shape, s.dtype) for s in shards]
-    shapes += [jax.ShapeDtypeStruct((planes,) + s.shape, s.dtype) for s in [*swaps, *lines]]
+    shapes += [jax.ShapeDtypeStruct((depth,) + s.shape, s.dtype) for s in [*swaps, *lines]]
     return pl.pallas_call(
-        functools.partial(gather_kernel, planes, pieces, count, len(swaps), len(lines)),
+        functools.partial(
+            gather_kernel, planes, depth, pieces, count, len(swaps), len(lines)
+        ),
         out_shape=shapes,
         in_specs=[pl.BlockSpec(memory_space=pl.ANY)] * total,
         out_specs=[pl.BlockSpec(memory_space=pl.ANY)] * total,
@@ -858,25 +1224,60 @@
             dma((total,)),
             dma((max(1, len(swaps)), PLANE - 1)),
             dma((max(1, len(swaps)), PLANE - 1)),
-            dma((2, planes, max(1, 2 * (total - count)))),
-            dma((planes, max(1, 2 * (total - count)))),
+            dma((2, depth, max(1, 2 * (total - count)))),
+            dma((depth, max(1, 2 * (total - count)))),
         ],
         compiler_params=pltpu.CompilerParams(collective_id=ident, has_side_effects=True),
         name=f"gather{ident}",
     )(*shards, *swaps, *lines)
 
 
-def bank_kernel(planes, wide, parts, out, landing, part, *sems):
+def bank_kernel(
+    planes, wide, parts, front, grads, query_mid, lower_mid, query_in, lower_in, tokens, gain, mixed,
+    out, result, landing, part, hold, back, hold_sem, *sems,
+):
     e = neighbours()[0]
     z = lax.axis_index("dp")
     mail = Mail()
     swap = sems[10:12]
+    step = hold.shape[1]
+    steps = D // step
+
+    def fetch(n):
+        return pltpu.make_async_copy(
+            front.at[pl.ds(n * step, step)], hold.at[n % 2], hold_sem.at[n % 2]
+        )
+
+    def multiply(n):
+        fetch(n).wait()
+        columns = slice(n * step, (n + 1) * step)
+        back[:, columns] = (
+            product_t(grads[...], hold[n % 2])
+            + product(query_mid[...], query_in[:, columns])
+            + product(lower_mid[...], lower_in[:, columns])
+        )
+        if n + 2 < steps:
+            fetch(n + 2).start()
+
+    def finish():
+        values = tokens[...].astype(F32)
+        inverse = lax.rsqrt(jnp.mean(values * values, axis=-1, keepdims=True) + 1e-06)
+        scaled = back[...] * gain[...]
+        along = jnp.mean(scaled * values, axis=-1, keepdims=True)
+        change = inverse * scaled - values * (inverse * inverse * inverse * along)
+        result[...] = (mixed[...] + change).astype(BF)
+
+    for n in range(2):
+        fetch(n).start()
     greet(plane_peers(1), other_levels(planes))
 
     def chunk(who):
         return pl.ds(pl.multiple_of(who * wide, 128), wide)
 
     swap_out(mail, lambda who: parts.at[:, chunk(who)], lambda who: landing.at[who], swap, 0)
+    early = steps - planes
+    for n in range(early):
+        multiply(n)
     total = parts[:, chunk(e)].astype(F32)
     for j in range(1, PLANE):
         who = (e + PLANE - j) % PLANE
@@ -885,25 +1286,39 @@
     low = total.astype(BF)
     part[...] = low
     out[z, e] = low
+
+    def meanwhile(s):
+        if s < planes:
+            multiply(early + s)
+        if s == planes:
+            finish()
+
     spread_pieces(
-        planes, 1, lambda i: part, lambda level, who, i: out.at[level, who], mail, sems
+        planes, 1, lambda i: part, lambda level, who, i: out.at[level, who], mail, sems, meanwhile
     )
     mail.drain()
 
 
-def exchange_banks(joined, planes, ident):
+def exchange_banks(joined, planes, ident, front, operands):
     rank, width = joined.shape
     wide = width // PLANE
+    rows = operands[0].shape[0]
     dma = pltpu.SemaphoreType.DMA
     vmem = pl.BlockSpec(memory_space=pltpu.VMEM)
     return pl.pallas_call(
         functools.partial(bank_kernel, planes, wide),
-        out_shape=jax.ShapeDtypeStruct((planes, PLANE, rank, wide), BF),
-        in_specs=[vmem],
-        out_specs=vmem,
+        out_shape=[
+            jax.ShapeDtypeStruct((planes, PLANE, rank, wide), BF),
+            jax.ShapeDtypeStruct((rows, D), BF),
+        ],
+        in_specs=[vmem, pl.BlockSpec(memory_space=pl.ANY), *([vmem] * len(operands))],
+        out_specs=[vmem, vmem],
         scratch_shapes=[
             pltpu.VMEM((PLANE, rank, wide), BF),
             pltpu.VMEM((rank, wide), BF),
+            pltpu.VMEM((2, 256, front.shape[1]), BF),
+            pltpu.VMEM((rows, D), F32),
+            dma((2,)),
             *spread_sems(planes, 1),
             dma((1, PLANE - 1)),
             dma((1, PLANE - 1)),
@@ -912,7 +1327,7 @@
             collective_id=ident, has_side_effects=True, vmem_limit_bytes=VMEM_LIMIT
         ),
         name=f"banks{ident}",
-    )(joined)
+    )(joined, front, *operands)
 
 
 def place_kernel(trees, offsets, chosen, full, *outs):
@@ -1152,18 +1567,14 @@
     fast = groups == PLANE and planes == 4 and groups * rows_here == TREE and hidden_shared % 8 == 0
 
     weight_rows = query_matrix.shape[0]
-    qn_here, qr_here = split_heads(query_matrix)
-    front = jnp.concatenate([qn_here, qr_here, latent_down, router_matrix], 1)
     padded_shared = -(-planes * hidden_shared // 128) * 128
     fill = padded_shared - planes * hidden_shared
-    cut = shared_in.reshape(weight_rows, 2, planes, groups, hidden_shared)
-    cut = cut.transpose(3, 0, 1, 2, 4).reshape(groups, weight_rows, 2, planes * hidden_shared)
-    cut = jnp.pad(cut, ((0, 0), (0, 0), (0, 0), (0, fill)))
-    cut = cut.reshape(groups, weight_rows, 2 * padded_shared)
+    front, cut = prepare(
+        query_matrix, latent_down, router_matrix, shared_in, planes, groups, padded_shared
+    )
     if fast:
-        lines = shared_out.reshape(hidden_shared // 8, 8, D)
-        front, mix_up, mix_out, sh_in, sh_out = gather_blocks(
-            [front, latent_up, output_matrix], planes, (4, 2, 2), 1, [cut], [lines]
+        front, mix_up, mix_out, sh_in = gather_blocks(
+            [front, latent_up, output_matrix], planes, (4, 2, 2), 1, [cut]
         )
         front = front.reshape(D, -1)
         mix_up = mix_up.reshape(KVR, -1)
@@ -1174,13 +1585,8 @@
         mix_out = lax.all_gather(output_matrix, both, axis=0, tiled=True)
         cut = lax.all_to_all(cut, "expert", split_axis=0, concat_axis=0, tiled=True)
         sh_in = gather_dp(cut.reshape(groups * weight_rows, -1))
-        sh_out = gather_dp(shared_out)
     wide = HEADS * (NOPE + ROPE)
     feed_router = front[:, wide + KVR + ROPE :]
-
-    sh_in = sh_in.reshape(D, 2 * padded_shared)
-    sh_out = sh_out.reshape(planes * hidden_shared, D)
-    sh_out = jnp.pad(sh_out, ((0, fill), (0, 0)))
 
     seg_tree = lax.dynamic_slice_in_dim(segment_id, local_tree * TREE, TREE)
     par_tree = lax.dynamic_slice_in_dim(parent_id, local_tree * TREE, TREE)
@@ -1234,34 +1640,40 @@
     ).astype(BF)
     slots_here = product(lower, mask.astype(BF)) * mask
 
-    inputs = tokens_in.astype(F32)
-    hidden = normed(inputs, mixer_gain).astype(BF)
-    query_mid = product_t(hidden, query_in).astype(BF)
-    lower_mid = product_t(hidden, lower_in).astype(BF)
-    front_lin = product(hidden, front)
-    latent_full = front_lin[:, wide : wide + KVR + ROPE] + product(lower_mid, lower_out)
-    latent_raw = latent_full[:, :KVR]
-    rope_raw = latent_full[:, KVR:]
-    latent_norm = normed(latent_raw, latent_gain).astype(BF)
-    key_rope = rotate(rope_raw, cosine, sine).astype(BF)
-    upper_mid = product_t(latent_norm, upper_in).astype(BF)
-    rank = upper_mid.shape[1]
-    latent_ext = jnp.concatenate(
-        [
-            latent_norm,
-            key_rope[:, :HALF],
-            upper_mid,
-            jnp.zeros((rows_here, HALF - rank), BF),
-            key_rope[:, HALF:],
-            jnp.zeros((rows_here, HALF), BF),
-        ],
-        1,
-    )
+    offset = shift.astype(jnp.int32).reshape(1)
+    q_nope, q_rope, latent_ext, latent_raw, hidden, query_mid, lower_mid = project(
+        nb,
+        offset,
+        tokens_in,
+        front,
+        (
+            query_in,
+            jnp.concatenate([qn_out, qr_out], 1),
+            lower_in,
+            lower_out,
+            upper_in,
+            mixer_gain[None, :],
+            latent_gain[None, :],
+            cos_half,
+            sin_half,
+        ),
+    )
+    grad_payload = jnp.concatenate(
+        [cotangent, slots_here.astype(BF), jnp.zeros((rows_here, 128 - experts_all), BF)], 1
+    )
+    grad_payload, latent_ext, out_rows = lax.optimization_barrier(
+        (grad_payload, latent_ext, shared_out)
+    )
+    sh_out = gather_dp(out_rows).reshape(planes * hidden_shared, D)
+    sh_out = jnp.pad(sh_out, ((0, fill), (0, 0)))
+    all_grad = lax.all_gather(grad_payload, "expert", axis=0, tiled=True)
+    rank = query_mid.shape[1]
     if fast:
         all_latent = gather_blocks([latent_ext], 1, (2,), 2)[0].reshape(TREE, LATW)
     else:
         all_latent = lax.all_gather(latent_ext, "expert", axis=0, tiled=True)
     tree_latent = lax.dynamic_slice_in_dim(all_latent, local_tree * TREE, TREE, 0)
+    sh_in = sh_in.reshape(D, 2 * padded_shared)
     up_extra = jnp.concatenate(
         [
             jnp.zeros((HALF, mix_up.shape[1]), BF),
@@ -1270,27 +1682,21 @@
         ],
         0,
     )
-    q_nope = pad_rows(
-        (front_lin[:, : HEADS * NOPE] + product(query_mid, qn_out)).astype(BF)
-    )
-    q_rope = pad_rows(front_lin[:, HEADS * NOPE : wide] + product(query_mid, qr_out))
-    grad_payload = jnp.concatenate(
-        [cotangent, slots_here.astype(BF), jnp.zeros((rows_here, 128 - experts_all), BF)], 1
-    )
-    grad_payload, tree_latent = lax.optimization_barrier((grad_payload, tree_latent))
-    all_grad = lax.all_gather(grad_payload, "expert", axis=0, tiled=True)
-
     attended, level, keys_values = attend(
         nb, info, q_nope, q_rope, cos_pair, sin_pair, limit_rows, tree_latent, mix_up, up_extra
     )
-    attended = cut_rows(attended)
-    output_mid = product_t(attended, output_in).astype(BF)
-    mixed_state = inputs + product(attended, mix_out) + product(output_mid, output_out)
-    feed_hidden = normed(mixed_state, feed_gain).astype(BF)
-    logits = product(feed_hidden, feed_router)
-    logit_peak = jnp.max(logits, axis=1, keepdims=True)
-    logit_exp = jnp.exp(logits - logit_peak)
-    router_probs = logit_exp / jnp.sum(logit_exp, axis=1, keepdims=True)
+    attended, sh_out = lax.optimization_barrier((attended, sh_out))
+    mixed_state, feed_payload, router_probs, output_mid = mix(
+        offset,
+        attended,
+        tokens_in,
+        mix_out,
+        front,
+        output_in,
+        output_out,
+        feed_gain[None, :],
+        experts_all,
+    )
 
     my_slots = lax.dynamic_slice(all_grad, (0, D + group_pos * owned), (groups * rows_here, owned))
     slot_rows = jnp.pad(my_slots, ((0, 0), (0, 128 - owned)))
@@ -1299,10 +1705,6 @@
     flat = (owned, groups * cap)
     grad_inner = expert_grads(grad_perm.reshape(*flat, D), expert_out)
 
-    high = lax.reduce_precision(router_probs, 8, 7)
-    feed_payload = jnp.concatenate(
-        [feed_hidden, high.astype(BF), (router_probs - high).astype(BF)], 1
-    )
     all_feed = lax.all_gather(feed_payload, "expert", axis=0, tiled=True)
 
     all_feed, grad_inner = lax.optimization_barrier((all_feed, grad_inner))
@@ -1337,34 +1739,21 @@
     )
     row_sum = lax.psum_scatter(row_part, "expert", scatter_dimension=0, tiled=True)
 
-    grad_output = cotangent.astype(F32)
-    grad_sum = grad_sum.astype(F32)
-    grad_probs = grad_sum[:, D : D + experts_all] + grad_sum[:, D + experts_all :]
-    grad_logits = router_probs * (
-        grad_probs - jnp.sum(router_probs * grad_probs, axis=1, keepdims=True)
-    )
-    grad_feed = grad_sum[:, :D] + product_t(grad_logits.astype(BF), feed_router)
-    _, norm_two_back = jax.vjp(lambda operand: normed(operand, feed_gain), mixed_state)
-    grad_mixed = grad_output + norm_two_back(grad_feed)[0]
-    grad_attn = grad_mixed.astype(BF)
-    grad_output_mid = product_t(grad_attn, output_out).astype(BF)
-    grad_output_exit = product_left(output_mid, grad_attn)
-    grad_output_entry = product_left(grad_output_mid, attended)
-    grad_attended = (product_t(grad_attn, mix_out) + product(grad_output_mid, output_in)).astype(BF)
-
-    delta = jnp.sum(
-        (grad_attended.astype(F32) * attended.astype(F32)).reshape(rows_here, HEADS, VDIM), axis=2
-    )
-    padded = nb * SEGLEN
-    stats = jnp.concatenate(
-        [
-            level[:, :2],
-            pad_rows(delta).T.reshape(HEADS // 2, 2, padded),
-            jnp.zeros((HEADS // 2, 4, padded), F32),
-        ],
-        1,
-    )
-    dq_nope, dq_rope, grad_up, grad_lat = attend_back(
+    grad_mixed, grad_output_mid, grad_attended = turn(
+        nb,
+        offset,
+        grad_sum,
+        router_probs,
+        mixed_state,
+        cotangent,
+        feed_gain[None, :],
+        front,
+        output_in,
+        output_out,
+        mix_out,
+    )
+
+    dq_nope, dq_rope, grad_up, grad_tree = attend_back(
         nb,
         info,
         q_nope,
@@ -1376,25 +1765,12 @@
         keys_values,
         mix_up,
         up_extra,
-        pad_rows(grad_attended),
-        stats,
-    )
-    row_sum, dq_nope = lax.optimization_barrier((row_sum, dq_nope))
-    block_output = (mixed_state + row_sum.astype(F32)).astype(BF)
-    dq_nope, dq_rope = cut_rows(dq_nope), cut_rows(dq_rope)
-    grad_upper_exit = grad_up[HALF : HALF + rank]
-    grad_upper_mid = grad_lat[:, KVR + HALF : KVR + HALF + rank].astype(BF)
-    grad_upper_entry = product_left(grad_upper_mid, tree_latent[:, :KVR])
-    grad_tree = grad_lat[:, :KVR] + product(grad_upper_mid, upper_in)
-    grad_tree = jnp.concatenate(
-        [
-            grad_tree,
-            grad_lat[:, KVR : KVR + HALF],
-            grad_lat[:, KVR + ROPE : KVR + ROPE + HALF],
-            jnp.zeros((TREE, ROPE), F32),
-        ],
-        1,
-    ).astype(BF)
+        grad_attended,
+        attended,
+        level,
+        jnp.pad(upper_in, ((HALF, LATW - KVR - HALF - rank), (0, 0))),
+    )
+    own_tree = grad_tree
     if trees_here > 1:
         grad_tree = lax.dynamic_update_slice_in_dim(
             jnp.zeros((groups * rows_here, grad_tree.shape[1]), BF), grad_tree, local_tree * TREE, 0
@@ -1405,56 +1781,78 @@
         grad_latent = lax.psum_scatter(
             grad_tree, "expert", scatter_dimension=0, tiled=True
         ).astype(F32)
-    _, latent_back = jax.vjp(lambda operand: normed(operand, latent_gain), latent_raw)
-    _, key_back = jax.vjp(lambda operand: rotate(operand, cosine, sine), rope_raw)
-    grad_latent_full = jnp.concatenate(
-        [latent_back(grad_latent[:, :KVR])[0], key_back(grad_latent[:, KVR : KVR + ROPE])[0]], -1
-    ).astype(BF)
-    grad_lower_mid = product_t(grad_latent_full, lower_out).astype(BF)
-    grad_lower_exit = product_left(lower_mid, grad_latent_full)
-    grad_lower_entry = product_left(grad_lower_mid, hidden)
-    dq_all = jnp.concatenate([dq_nope, dq_rope], 1)
-    q_out = jnp.concatenate([qn_out, qr_out], 1)
-    grad_query_mid = product_t(dq_all, q_out).astype(BF)
-    grad_query_exit = product_left(query_mid, dq_all)
-    grad_query_exit = join_heads(
-        grad_query_exit[:, : HEADS * NOPE], grad_query_exit[:, HEADS * NOPE :]
-    )
-    grad_query_entry = product_left(grad_query_mid, hidden)
-    grad_front = jnp.concatenate(
-        [dq_all, grad_latent_full, jnp.zeros((rows_here, experts_all), BF)], 1
-    )
-    grad_hidden = (
-        product_t(grad_front, front)
-        + product(grad_query_mid, query_in)
-        + product(grad_lower_mid, lower_in)
-    )
-    _, norm_one_back = jax.vjp(lambda operand: normed(operand, mixer_gain), inputs)
-    grad_input = (grad_mixed + norm_one_back(grad_hidden)[0]).astype(BF)
+    row_sum, grad_latent = lax.optimization_barrier((row_sum, grad_latent))
+    block_output = (mixed_state + row_sum.astype(F32)).astype(BF)
+    offsets, end = [], 0
+    for width in (
+        query_entry.shape[2],
+        query_exit.shape[2],
+        lower_entry.shape[2],
+        lower_exit.shape[2],
+        upper_entry.shape[2],
+        upper_exit.shape[2],
+        output_entry.shape[2],
+        output_exit.shape[2],
+    ):
+        offsets.append((end, width))
+        end += -(-width // 128) * 128
+    total = -(-end // (128 * PLANE)) * 128 * PLANE
+    grad_front, joined, grad_query_mid, grad_lower_mid = join(
+        tuple(offsets),
+        total,
+        offset,
+        [
+            dq_nope,
+            dq_rope,
+            jnp.concatenate([qn_out, qr_out], 1),
+            query_mid,
+            hidden,
+            grad_latent.astype(F32),
+            latent_raw,
+            latent_gain[None, :],
+            cos_half,
+            sin_half,
+            lower_out,
+            lower_mid,
+            own_tree,
+            tree_latent,
+            grad_up,
+            output_mid,
+            grad_mixed,
+            grad_output_mid,
+            attended,
+        ],
+    )
 
     adapters = query_entry.shape[0]
-    gradients = [
-        grad_query_entry,
-        grad_query_exit,
-        grad_lower_entry,
-        grad_lower_exit,
-        grad_upper_entry,
-        grad_upper_exit,
-        grad_output_entry,
-        grad_output_exit,
-    ]
     if fast:
-        offsets, pieces, at = [], [], 0
-        for gradient in gradients:
-            width = gradient.shape[1]
-            offsets.append((at, width))
-            pieces.append(jnp.pad(gradient, ((0, 0), (0, -width % 128))))
-            at += width + -width % 128
-        pieces.append(jnp.zeros((rank, -at % (128 * PLANE)), F32))
-        joined = jnp.concatenate(pieces, 1).astype(BF)
-        full = exchange_banks(joined, planes, 6)
+        full, grad_input = exchange_banks(
+            joined,
+            planes,
+            6,
+            front,
+            [
+                grad_front,
+                grad_query_mid,
+                grad_lower_mid,
+                query_in,
+                lower_in,
+                tokens_in,
+                mixer_gain[None, :],
+                grad_mixed,
+            ],
+        )
         banks = place_banks(full, adapter_index, tuple(offsets), adapters)
     else:
+        grad_hidden = (
+            product_t(grad_front, front)
+            + product(grad_query_mid, query_in)
+            + product(grad_lower_mid, lower_in)
+        )
+        inputs = tokens_in.astype(F32)
+        _, norm_one_back = jax.vjp(lambda operand: normed(operand, mixer_gain), inputs)
+        grad_input = (grad_mixed + norm_one_back(grad_hidden)[0]).astype(BF)
+        gradients = [joined[:, at : at + width] for at, width in offsets]
         banks = reduce_banks(gradients, local_tree, trees_here, adapter_index, adapters)
     return (block_output, grad_input, *banks)
 

time: 792 us -> 715 us (0.903)
  matrix products: 59.6 us -> 0.2 us
  local copies, waits for them, and re-layouts: 66.1 us -> 20.9 us
  Pallas kernels: 557 us -> 598 us
  other arithmetic: 26.1 us -> 11.2 us
    pallas_call x3 -> x8, Pallas kernels: 228 us -> 264 us  [the longest x2 175 us: gather_blocks(): pl.pallas_call(functools.partial(gather_kernel, planes, depth, pieces, co...]
    dot_general x12 -> x1, matrix products: 30.3 us -> 0.2 us  [product(): return jnp.dot(left, right, preferred_element_type=F32)]
    dot_general x17 -> x0, matrix products: 29.3 us -> none  [the longest x10 25.1 us: product_t(): lax.dot_general(left, right, (((1,), (1,)), ((), ())), preferred_element_...]
    unnamed x190 -> x30, local copies, waits for them, and re-layouts: 15.2 us -> 1.83 us
    reshape x8 -> x0, local copies, waits for them, and re-layouts: 13.3 us -> none  [the longest x1 4.3 us: body(): cut = shared_in.reshape(weight_rows, 2, planes, groups, hidden_shared)]
    concatenate x7 -> x1, local copies, waits for them, and re-layouts: 9.22 us -> 0.01 us  [body(): jnp.concatenate([qn_out, qr_out], 1)]
  transfers between devices with their start and end apart: 4 -> 7, of which waited for: 2 -> 2; matrix products, arithmetic and copies ran while one was open for 7% -> 2% of each run, Pallas kernels for 27% -> 38%
where the time goes in v2:
time: 715 us; the launch traced here: 706 us
  Pallas kernels  598 us (84%)
  waiting for transfers between devices  54.7 us (8%)
  local copies, waits for them, and re-layouts  20.9 us (3%)
  between operations  16.4 us (2%)
  other arithmetic  11.2 us (2%)
    pallas_call x2, Pallas kernels, gather_blocks(): pl.pallas_call(functools.partial(gather_kernel, planes, depth, pieces, co...  175 us
    pallas_call x1, Pallas kernels, run_experts(): pl.pallas_call(functools.partial(expert_kernel, experts), out_shape=(jax....  72.9 us
    pallas_call x1, Pallas kernels, attend_back(): pl.pallas_call(functools.partial(attend_back_kernel, nb), out_shape=(jax....  60 us
    reduce_scatter x1, waiting for transfers between devices, body(): lax.psum_scatter(grad_part, 'expert', scatter_dimension=0, tiled=True)  37.1 us
    pallas_call x1, Pallas kernels, exchange_banks(): pl.pallas_call(functools.partial(bank_kernel, planes, wide), out_shape=[j...  36.9 us
    pallas_call x2, Pallas kernels, collect(): pl.pallas_call(functools.partial(collect_kernel, owned, cap, transposed=t...  36.9 us
    pallas_call x1, Pallas kernels, attend(): pl.pallas_call(functools.partial(attend_kernel, nb), out_shape=(jax.Shape...  33.9 us
    pallas_call x1, Pallas kernels, expert_rows(): pl.pallas_call(expert_rows_kernel, out_shape=jax.ShapeDtypeStruct((owned,...  29.4 us
  transfers between devices with their start and end apart: 7, of which 2 were waited for; matrix products, arithmetic and copies ran while one was open for 2% of the time, Pallas kernels for 38%

profile of v2, /device:TPU:0, one launch (start us, length us, event | category | flops | bytes accessed | tf_op | source)
XLA Modules:
  0.0 706.1 jit_solution(2484964467558376603)
XLA Ops:
  7.3 1.4 dynamic_slice.63
  10.7 0.2 reshape.132
  10.9 0.1 reshape.134
  11.0 0.1 copy.57
  11.1 0.2 reshape.135
  11.4 1.3 dynamic-slice_bitcast_fusion.5.lower_out
  12.7 1.3 dynamic-slice_bitcast_fusion.6.upper_in
  14.1 0.2 convolution_multiply_fusion
  14.3 0.1 copy.58
  14.4 1.6 dynamic-slice_bitcast_fusion.3
  16.0 0.1 add_select_fusion.1
  16.1 0.1 fusion.4
  16.2 1.4 fusion
  17.6 2.0 concatenate.26
  19.6 2.9 prepare.1
  22.5 143.3 %gather1.1 = (bf16[4,8,64,3712]{3,2,1,0:T(8,128)(2,1)}, bf16[4,8,16,4096]{3,2,1,0:T(8,128)(2,1)}, bf16[4,8,64,2048]{3,2,1,0:T(8,128)(2,1)}, bf16[4,8,64,768]{3,2,1,0:T(8,128)(2,1)}) custom-call(bf16[64,3712]{1,0:T(8,128)(2,1)} %get-tuple-element.69.refs_0_, bf16[16,4096]{1,0:T(8,128)(2,1)} %refs_1_.1, bf16[64,2048]{1,0:T(8,128)(2,1)} %refs_2_.1, ...), custom_call_target="tpu_custom_call" | custom-call | tf_op jit(solution)/shard_map/gather1/pallas_call | solution.py:1215
  165.8 15.3 %project.1 = (bf16[384,2048]{1,0:T(8,128)(2,1)}, f32[384,1024]{1,0:T(8,128)}, bf16[320,640]{1,0:T(8,128)(2,1)}, f32[320,512]{1,0:T(8,128)}, bf16[320,2048]{1,0:T...) custom-call(s32[1]{0:T(128)} %bitcast.info, bf16[320,2048]{1,0:T(8,128)(2,1)} %tokens.5, ...), custom_call_target="tpu_custom_call" | custom-call | flops 5000000000 | bytes 20000000 | tf_op jit(solution)/shard_map/project/pallas_call | solution.py:471
  181.3 3.1 collective-permute-start.1
  184.4 1.2 collective-permute-start.2
  185.5 32.1 %gather2.1 = bf16[1,8,320,640]{3,2,1,0:T(8,128)(2,1)} custom-call(bf16[320,640]{1,0:T(8,128)(2,1)} %get-tuple-element.75.refs_0_), custom_call_target="tpu_custom_call" | custom-call | tf_op jit(solution)/shard_map/gather2/pallas_call | solution.py:1215
  217.7 0.1 slice_reduce_fusion
  217.8 0.6 gather_fusion
  218.4 0.1 slice_reduce_fusion.1
  218.6 0.6 gather_fusion.1
  219.2 0.1 pad.25.clone
  219.3 0.1 dynamic_update_slice.12.qlim
  219.4 0.2 select_reduce_fusion
  219.6 0.7 pad_add_fusion.info
  220.3 0.2 maximum_dynamic-update-slice_fusion.cosp
  220.6 0.2 maximum_dynamic-update-slice_fusion.1.sinp
  220.8 1.0 dynamic-slice_bitcast_fusion
  221.8 1.1 maximum_maximum_fusion.upx
  222.9 33.9 %attend.1 = (bf16[384,2048]{1,0:T(8,128)(2,1)}, f32[8,8,384]{2,1,0:T(8,128)}, bf16[1792,4096]{1,0:T(8,128)(2,1)}) custom-call(s32[12]{0:T(128)} %pad_add_fusion.info, bf16[384,2048]{1,0:T(8,128)(2,1)} %get-tuple-element.72.qn, f32[384,1024]{1,0:T(8,128)} %get-tuple-element.73.qr, f32[384,128]{1,0:T(8,128)} %copy-done.8, f32[384,128]{1,0:T(8,128)} %copy-done.7, ...), custom_call_target="tpu_custom_call" | custom-call | flops 30000001024 | bytes 25000000 | tf_op jit(solution)/shard_map/attend/pallas_call | solution.py:267
  256.9 1.5 dynamic-slice_bitcast_fusion.1
  258.5 1.5 pad_maximum_fusion
  260.0 0.1 constant_dynamic-slice_fusion.4
  260.1 0.2 pad_maximum_fusion.1
  260.3 1.3 pad.12.sh_out.weight
  261.6 12.0 %mix.1 = (f32[320,2048]{1,0:T(8,128)}, bf16[320,2176]{1,0:T(8,128)(2,1)}, f32[320,64]{1,0:T(8,128)}, bf16[320,16]{1,0:T(8,128)(2,1)}) custom-call(s32[1]{0:T(128)} %bitcast.info, bf16[384,2048]{1,0:T(8,128)(2,1)} %get-tuple-element.79.attended.att, bf16[320,2048]{1,0:T(8,128)(2,1)} %tokens.5, bf16[2048,2048]{1,0:T(8,128)(2,1)} %bitcast.53, ...), custom_call_target="tpu_custom_call" | custom-call | flops 3000000000 | bytes 14000000 | tf_op jit(solution)/shard_map/mix/pallas_call | solution.py:534
  273.7 0.2 reduce-scatter.5.cloned.1.call-start
  273.9 1.3 constant_dynamic-slice_fusion
  275.2 1.0 pad.13.slots
  276.2 0.9 copy.59
  277.1 17.2 %spread_grad.1 = (bf16[8,8,40,2048]{3,2,1,0:T(8,128)(2,1)}, f32[2560,384]{1,0:T(8,128)}) custom-call(bf16[2560,2176]{1,0:T(8,128)(2,1)} %all-gather.5.cloned.1.call-done.pay, f32[8,8,320]{2,1,0:T(8,128)} %bitcast.68, bf16[384,2048]{1,0:T(8,128)(2,1)} %pad.12.sh_out.weight), custom_call_target="tpu_custom_call" | custom-call | flops 12000000000 | bytes 28000000 | tf_op jit(solution)/shard_map/spread_grad/pallas_call | solution.py:833
  294.3 26.8 %expert_grads.1.back = bf16[8,320,1408]{2,1,0:T(8,128)(2,1)} custom-call(bf16[8,320,2048]{2,1,0:T(8,128)(2,1)} %bitcast.60, bf16[8,1408,2048]{2,1,0:T(8,128)(2,1)} %w_out.3), custom_call_target="tpu_custom_call" | custom-call | flops 14763950080 | bytes 67108864 | tf_op jit(solution)/shard_map/expert_grads/pallas_call | solution.py:904
  321.0 17.5 %all-gather.3.cloned.1.call-done.pay = bf16[2560,2176]{1,0:T(8,128)(2,1)} async-done(((bf16[320,2176]{1,0:T(8,128)(2,1)}), bf16[2560,2176]{1,0:T(8,128)(2,1)}) %all-gather.3.cloned.1.call-update) | async-done | bytes 11141136 | tf_op jit(solution)/shard_map/all_gather | solution.py:1708
  338.5 1.8 convert_add_fusion
  340.3 1.1 copy.61
  341.4 21.0 %spread_feed.1 = (bf16[8,8,40,2048]{3,2,1,0:T(8,128)(2,1)}, f32[8,8,40,128]{3,2,1,0:T(8,128)}, bf16[2560,384]{1,0:T(8,128)(2,1)}, bf16[2560,768]{1,0:T(8,128)(2,1)}) custom-call(bf16[2560,2176]{1,0:T(8,128)(2,1)} %all-gather.3.cloned.1.call-done.pay, f32[8,8,320]{2,1,0:T(8,128)} %bitcast.69, f32[8,8,320]{2,1,0:T(8,128)} %bitcast.70, ...), custom_call_target="tpu_custom_call" | custom-call | flops 14000000000 | bytes 28000000 | tf_op jit(solution)/shard_map/spread_feed/pallas_call | solution.py:854
  362.4 72.9 %experts.1 = (bf16[8,320,2176]{2,1,0:T(8,128)(2,1)}, bf16[8,320,1408]{2,1,0:T(8,128)(2,1)}) custom-call(s32[1]{0:T(128)} %bitcast.25.first, bf16[8,320,2048]{2,1,0:T(8,128)(2,1)} %bitcast.84, bf16[8,320,1408]{2,1,0:T(8,128)(2,1)} %expert_grads.1.back, f32[8,320,128]{2,1,0:T(8,128)} %bitcast.64, bf16[8,2048,2816]{2,1,0:T(8,128)(2,1)} %w_in.1), custom_call_target="tpu_custom_call" | custom-call | flops 59055800320 | bytes 92274688 | tf_op jit(solution)/shard_map/experts/pallas_call | solution.py:919
  435.3 20.0 %collect_grad.1 = bf16[2560,2176]{1,0:T(8,128)(2,1)} custom-call(bf16[8,8,40,2176]{3,2,1,0:T(8,128)(2,1)} %bitcast.83, bf16[2560,128]{1,0:T(8,128)(2,1)} %pad.13.slots, bf16[2560,768]{1,0:T(8,128)(2,1)} %get-tuple-element.94.inner, bf16[2048,768]{1,0:T(8,128)(2,1)} %bitcast.82), custom_call_target="tpu_custom_call" | custom-call | flops 14000000000 | bytes 28000000 | tf_op jit(solution)/shard_map/collect_grad/pallas_call | solution.py:954
  455.4 29.4 %expert_rows.1 = bf16[8,320,2048]{2,1,0:T(8,128)(2,1)} custom-call(bf16[8,320,1408]{2,1,0:T(8,128)(2,1)} %get-tuple-element.95.inner, f32[8,320,128]{2,1,0:T(8,128)} %bitcast.65, bf16[8,1408,2048]{2,1,0:T(8,128)(2,1)} %w_out.3), custom_call_target="tpu_custom_call" | custom-call | flops 14763950080 | bytes 67108864 | tf_op jit(solution)/shard_map/expert_rows/pallas_call | solution.py:940
  484.7 16.8 %collect_rows.1 = bf16[2560,2048]{1,0:T(8,128)(2,1)} custom-call(bf16[8,8,40,2048]{3,2,1,0:T(8,128)(2,1)} %bitcast.59, bf16[2560,128]{1,0:T(8,128)(2,1)} %pad.13.slots, bf16[2560,384]{1,0:T(8,128)(2,1)} %get-tuple-element.96.inner, bf16[384,2048]{1,0:T(8,128)(2,1)} %pad.12.sh_out.weight), custom_call_target="tpu_custom_call" | custom-call | flops 14000000000 | bytes 28000000 | tf_op jit(solution)/shard_map/collect_rows/pallas_call | solution.py:954
  501.6 0.7 copy-done.9
  502.3 0.7 pad.14.upper
  503.0 37.1 %reduce-scatter.5.cloned.1.call-done.sums = bf16[320,2176]{1,0:T(8,128)(2,1)} async-done(((bf16[2560,2176]{1,0:T(8,128)(2,1)}), bf16[320,2176]{1,0:T(8,128)(2,1)}) %reduce-scatter.5.cloned.1.call-update) | async-done | bytes 1392656 | tf_op jit(solution)/shard_map/reduce_scatter | solution.py:1734
  540.1 11.1 %turn.1 = (f32[320,2048]{1,0:T(8,128)}, bf16[320,16]{1,0:T(8,128)(2,1)}, bf16[384,2048]{1,0:T(8,128)(2,1)}) custom-call(s32[1]{0:T(128)} %bitcast.info, bf16[320,2176]{1,0:T(8,128)(2,1)} %reduce-scatter.5.cloned.1.call-done.sums, f32[320,64]{1,0:T(8,128)} %get-tuple-element.98.probs, f32[320,2048]{1,0:T(8,128)} %get-tuple-element.81.mixed, ...), custom_call_target="tpu_custom_call" | custom-call | flops 3000000000 | bytes 18000000 | tf_op jit(solution)/shard_map/turn/pallas_call | solution.py:595
  551.3 60.0 %attend_back.1 = (bf16[384,2048]{1,0:T(8,128)(2,1)}, bf16[384,1024]{1,0:T(8,128)(2,1)}, f32[128,4096]{1,0:T(8,128)}, bf16[2560,640]{1,0:T(8,128)(2,1)}) custom-call(s32[12]{0:T(128)} %pad_add_fusion.info, bf16[384,2048]{1,0:T(8,128)(2,1)} %get-tuple-element.72.qn, f32[384,1024]{1,0:T(8,128)} %get-tuple-element.73.qr, f32[384,128]{1,0:T(8,128)} %copy-done.8, ...), custom_call_target="tpu_custom_call" | custom-call | flops 54000001024 | bytes 30000000 | tf_op jit(solution)/shard_map/attend_back/pallas_call | solution.py:305
  611.3 28.4 %scatter5.1.sums = f32[320,640]{1,0:T(8,128)} custom-call(bf16[8,320,640]{2,1,0:T(8,128)(2,1)} %bitcast.58), custom_call_target="tpu_custom_call" | custom-call | tf_op jit(solution)/shard_map/scatter5/pallas_call | solution.py:1447
  639.7 10.3 %join.1 = (bf16[320,3712]{1,0:T(8,128)(2,1)}, bf16[16,17408]{1,0:T(8,128)(2,1)}, bf16[320,16]{1,0:T(8,128)(2,1)}, bf16[320,16]{1,0:T(8,128)(2,1)}) custom-call(s32[1]{0:T(128)} %bitcast.info, bf16[384,2048]{1,0:T(8,128)(2,1)} %get-tuple-element.103.dqn, bf16[384,1024]{1,0:T(8,128)(2,1)} %get-tuple-element.104.dqr, bf16[16,3072]{1,0:T(8,128)(2,1)} %copy-done.6, ...), custom_call_target="tpu_custom_call" | custom-call | flops 3000000000 | bytes 25000000 | tf_op jit(solution)/shard_map/join/pallas_call | solution.py:691
  650.0 36.9 %banks6.1 = (bf16[4,8,16,2176]{3,2,1,0:T(8,128)(2,1)}, bf16[320,2048]{1,0:T(8,128)(2,1)}) custom-call(bf16[16,17408]{1,0:T(8,128)(2,1)} %get-tuple-element.114.parts, bf16[2048,3712]{1,0:T(8,128)(2,1)} %bitcast.52, bf16[320,3712]{1,0:T(8,128)(2,1)} %get-tuple-element.115.grads, bf16[320,16]{1,0:T(8,128)(2,1)} %get-tuple-element.116.query_mid, ...), custom_call_target="tpu_custom_call" | custom-call | tf_op jit(solution)/shard_map/banks6/pallas_call | solution.py:1308
  686.9 7.7 %place_banks.1 = (f32[8,16,2048]{2,1,0:T(8,128)}, f32[8,16,3072]{2,1,0:T(8,128)}, f32[8,16,2048]{2,1,0:T(8,128)}, f32[8,16,576]{2,1,0:T(8,128)}, f32[8,16,512]{2...) custom-call(s32[4]{0:T(128)} %chosen.1, ...), custom_call_target="tpu_custom_call" | custom-call | flops 1000000 | bytes 11000000 | tf_op jit(solution)/shard_map/place_banks/pallas_call | solution.py:1352
  694.6 3.7 add_convert_fusion
  698.3 1.1 copy.71
  (59 shorter events, 0.6 us)
Async XLA Ops:
  7.2 3.5 copy-start
  7.2 6.8 copy-start.12
  7.2 8.8 %copy-start.11 = (s32[2560]{0:T(1024)S(1)}, s32[2560]{0:T(1024)}, u32[]{:S(2)}) copy-start(s32[2560]{0:T(1024)} %param.28) | copy-start | bytes 30724
  7.2 8.9 %copy-start.10 = (s32[2560]{0:T(1024)S(1)}, s32[2560]{0:T(1024)}, u32[]{:S(2)}) copy-start(s32[2560]{0:T(1024)} %param.29) | copy-start | bytes 30724
  7.2 10.3 %copy-start.2 = (bf16[320,2048]{1,0:T(8,128)(2,1)S(1)}, bf16[320,2048]{1,0:T(8,128)(2,1)}, u32[]{:S(2)}) copy-start(bf16[320,2048]{1,0:T(8,128)(2,1)} %cotangent.1) | copy-start | bytes 3932164
  7.2 266.7 %all-gather.5.cloned.1.call-start = ((), (), s32[]{:S(2)}) async-start(), calls=%async_computation.3 | async-start | bytes 12533760 | tf_op jit(solution)/shard_map/all_gather | solution.py:1669
  14.4 5.2 copy-start.6
  181.2 157.3 %all-gather.3.cloned.1.call-start = ((), (), s32[]{:S(2)}) async-start(), calls=%async_computation.2 | async-start | bytes 12533760 | tf_op jit(solution)/shard_map/all_gather | solution.py:1708
  181.2 77.3 %collective-permute-start = (bf16[88,2048]{1,0:T(8,128)(2,1)}, bf16[88,2048]{1,0:T(8,128)(2,1)}, u32[]{:S(2)}, u32[]{:S(2)}) collective-permute-start(bf16[88,2048]{1,0:T(8,128)(2,1)} %param.41), channel_id=1, source_target_pairs={{0,8},{8,16},{16,24},{24,0},{1,9},{9,17},{17,25},{25,1},{2,10},{10... | collective-permute-start | bytes 1081352 | tf_op jit(solution)/shard_map/ppermute | solution.py:1473
  181.3 77.2 %collective-permute-start.1 = (bf16[88,2048]{1,0:T(8,128)(2,1)}, bf16[88,2048]{1,0:T(8,128)(2,1)}, u32[]{:S(2)}, u32[]{:S(2)}) collective-permute-start(bf16[88,2048]{1,0:T(8,128)(2,1)} %param.41), channel_id=1, source_target_pairs={{0,16},{8,24},{16,0},{24,8},{1,17},{9,25},{17,1},{25,9},{2,18},{10... | collective-permute-start | bytes 1081352 | tf_op jit(solution)/shard_map/ppermute | solution.py:1473
  184.4 74.1 %collective-permute-start.2 = (bf16[88,2048]{1,0:T(8,128)(2,1)}, bf16[88,2048]{1,0:T(8,128)(2,1)}, u32[]{:S(2)}, u32[]{:S(2)}) collective-permute-start(bf16[88,2048]{1,0:T(8,128)(2,1)} %param.41), channel_id=1, source_target_pairs={{0,24},{8,0},{16,8},{24,16},{1,25},{9,1},{17,9},{25,17},{2,26},{10... | collective-permute-start | bytes 1081352 | tf_op jit(solution)/shard_map/ppermute | solution.py:1473
  185.5 34.8 %copy-start.4 = (f32[320,32]{1,0:T(8,128)S(1)}, f32[320,32]{1,0:T(8,128)}, u32[]{:S(2)}) copy-start(f32[320,32]{1,0:T(8,128)} %get-tuple-element.138.cos) | copy-start | bytes 122884
  217.6 2.9 copy-start.3
  219.4 3.5 copy-start.13
  220.5 2.4 copy-start.8
  220.8 2.2 copy-start.7
  273.7 266.5 %reduce-scatter.5.cloned.1.call-start = ((), (), s32[]{:S(2)}) async-start(), calls=%async_computation.5 | async-start | bytes 12533760 | tf_op jit(solution)/shard_map/reduce_scatter | solution.py:1734
  455.3 184.4 %reduce-scatter.3.cloned.1.call-start = ((), (), s32[]{:S(2)}) async-start(), calls=%async_computation.4 | async-start | bytes 11796480 | tf_op jit(solution)/shard_map/reduce_scatter | solution.py:1740
  501.6 0.7 copy-start.9
  694.6 3.7 copy-start.5
  694.6 4.8 copy-start.1
Sparse Core Ops, SparseCore 0:
  181.3 73.7 all-gather.4
  273.8 64.6 all-gather.2
  455.4 84.6 reduce-scatter.4
  543.9 86.8 reduce-scatter.2

commit v3 on v2

--- a/solution.py
+++ b/solution.py
@@ -44,26 +44,6 @@
     half_width = operand.shape[-1] // 2
     turned = jnp.concatenate([-operand[..., half_width:], operand[..., :half_width]], -1)
     return operand * cosine + turned * sine
-
-
-def select_slot(bank, chosen):
-    return lax.dynamic_index_in_dim(bank, chosen, 0, keepdims=False)
-
-
-def split_heads(matrix):
-    rows = matrix.shape[0]
-    three = matrix.reshape(rows, HEADS, NOPE + ROPE)
-    nope = three[:, :, :NOPE].reshape(rows, HEADS * NOPE)
-    rope = three[:, :, NOPE:].reshape(rows, HEADS // 2, 2, 2, HALF)
-    return nope, rope.transpose(0, 1, 3, 2, 4).reshape(rows, HEADS * ROPE)
-
-
-def join_heads(nope, rope):
-    rows = nope.shape[0]
-    turned = rope.reshape(rows, HEADS // 2, 2, 2, HALF).transpose(0, 1, 3, 2, 4)
-    return jnp.concatenate(
-        [nope.reshape(rows, HEADS, NOPE), turned.reshape(rows, HEADS, ROPE)], -1
-    ).reshape(rows, HEADS * (NOPE + ROPE))
 
 
 def lane_iota(shape):
@@ -169,14 +149,12 @@
     lse[0] = jnp.concatenate(levels + [jnp.zeros((6, rows_all), F32)], 0)
 
 
-def attend_back_kernel(
-    nb, info, qn, qr, cosp, sinp, qlim, tails, kv, up, upx, do, att, stats, upper,
-    dqn, dqr, gup, dlow, tail, kr, bias, near, dss, dkv, acc, dkr, dlat,
+def chance_kernel(
+    nb, info, qn, qr, cosp, sinp, qlim, tails, kv, stats, pt, pn, tail, kr, bias, near
 ):
-    step = pl.program_id(0)
     rows_all = qn.shape[0]
 
-    @pl.when(step == 0)
+    @pl.when(pl.program_id(0) == 0)
     def _():
         place_keys(nb, info, tails, tail)
         rotary_keys(tail[...], kr)
@@ -185,6 +163,35 @@
         row = lane_iota((2 * SEGLEN, SEGLEN))
         for m in range(nb):
             near[m] = jnp.where(key <= local_limit(nb, info, m, key, row), 0.0, -1e30)
+
+    raw = qr[...]
+    qrot = (raw * cosp[...] + pltpu.roll(raw, ROPE, 1) * sinp[...]).astype(BF)
+    for a in range(2):
+        q = jnp.concatenate([qn[:, a * 128 : a * 128 + 128], qrot], 1)
+        k = jnp.concatenate([kv[:, a * 256 : a * 256 + 128], kr[a]], 1)
+        level = stats[0, a : a + 1, :]
+        for at in range(0, TRUNK, 256):
+            there = slice(at, at + 256)
+            scores = product_t(k[there], q) + bias[there, :]
+            pt[0, a, there, :] = jnp.exp2(scores * (SCALING * LOG2E) - level).astype(BF)
+        for m in range(nb):
+            here = slice(m * SEGLEN, (m + 1) * SEGLEN)
+            there = slice(TRUNK + 2 * m * SEGLEN, TRUNK + 2 * (m + 1) * SEGLEN)
+            scores = product_t(k[there], q[here]) + near[m]
+            pn[0, a, m] = jnp.exp2(scores * (SCALING * LOG2E) - level[:, here]).astype(BF)
+
+
+def attend_back_kernel(
+    nb, info, qn, qr, cosp, sinp, tails, kv, up, upx, do, att, pt, pn, upper,
+    dqn, dqr, gup, dlow, tail, kr, dss, dkv, acc, dkr, dlat,
+):
+    step = pl.program_id(0)
+    rows_all = qn.shape[0]
+
+    @pl.when(step == 0)
+    def _():
+        place_keys(nb, info, tails, tail)
+        rotary_keys(tail[...], kr)
         acc[...] = jnp.zeros_like(acc)
         dkr[...] = jnp.zeros_like(dkr)
 
@@ -196,7 +203,6 @@
         k = jnp.concatenate([kv[:, a * 256 : a * 256 + 128], kr[a]], 1)
         v = kv[:, a * 256 + 128 : a * 256 + 256]
         g = do[:, a * 128 : a * 128 + 128]
-        level = stats[0, a : a + 1, :]
         shares = g.astype(F32) * att[:, a * 128 : a * 128 + 128].astype(F32)
         main = shares.astype(BF)
         ones = jnp.ones((8, 128), BF)
@@ -205,24 +211,23 @@
         mine = lane_iota((1, 128)) % ROPE
         mine = (mine < HALF) if a == 0 else (mine >= HALF)
 
-        def block(there, here, hide):
-            scores = product_t(k[there], q[here]) + hide
-            p = jnp.exp2(scores * (SCALING * LOG2E) - level[:, here])
-            ds = (p * (product_t(v[there], g[here]) - delta[:, here])).astype(BF)
+        def block(there, here, p):
+            dp = product_t(v[there], g[here])
+            ds = (p.astype(F32) * (dp - delta[:, here])).astype(BF)
             dk = product(ds, q[here]) * SCALING
             dkv[there, a * 256 : a * 256 + 128] = dk[:, :128].astype(BF)
-            dkv[there, a * 256 + 128 : a * 256 + 256] = product(p.astype(BF), g[here]).astype(BF)
+            dkv[there, a * 256 + 128 : a * 256 + 256] = product(p, g[here]).astype(BF)
             dkr[there, :] += jnp.where(mine, dk[:, 128:], 0.0)
             return ds
 
         for at in range(0, TRUNK, 256):
             there = slice(at, at + 256)
-            dss[there, :] = block(there, slice(0, rows_all), bias[there, :])
+            dss[there, :] = block(there, slice(0, rows_all), pt[0, a, there, :])
         parts = []
         for m in range(nb):
             here = slice(m * SEGLEN, (m + 1) * SEGLEN)
             there = slice(TRUNK + 2 * m * SEGLEN, TRUNK + 2 * (m + 1) * SEGLEN)
-            parts.append(product_left(block(there, here, near[m]), k[there]))
+            parts.append(product_left(block(there, here, pn[0, a, m]), k[there]))
         dq = (product_left(dss[...], k[:TRUNK]) + jnp.concatenate(parts, 0)) * SCALING
         dqn[:, a * 128 : a * 128 + 128] = dq[:, :128].astype(BF)
         dq_rope = dq[:, 128:] if dq_rope is None else dq_rope + dq[:, 128:]
@@ -300,15 +305,21 @@
     )(info, qn, qr, cosp, sinp, qlim[None, :], lat, up, upx)
 
 
-def attend_back(nb, info, qn, qr, cosp, sinp, qlim, lat, kv, up, upx, do, att, stats, upper):
+def far_spec(keys, rows):
+    return pl.BlockSpec((1, 2, keys, rows), lambda i, info: (i, 0, 0, 0))
+
+
+def near_spec(nb):
+    return pl.BlockSpec((1, 2, nb, 2 * SEGLEN, SEGLEN), lambda i, info: (i, 0, 0, 0, 0))
+
+
+def chances(nb, info, qn, qr, cosp, sinp, qlim, lat, kv, stats):
     rows, keys = qn.shape[0], TRUNK + 2 * nb * SEGLEN
     return pl.pallas_call(
-        functools.partial(attend_back_kernel, nb),
+        functools.partial(chance_kernel, nb),
         out_shape=(
-            jax.ShapeDtypeStruct((rows, HEADS * NOPE), BF),
-            jax.ShapeDtypeStruct((rows, HEADS * ROPE), BF),
-            jax.ShapeDtypeStruct((128, HEADS * (NOPE + VDIM)), F32),
-            jax.ShapeDtypeStruct((TREE, LATW), BF),
+            jax.ShapeDtypeStruct((HEADS // 2, 2, TRUNK, rows), BF),
+            jax.ShapeDtypeStruct((HEADS // 2, 2, nb, 2 * SEGLEN, SEGLEN), BF),
         ),
         grid_spec=pltpu.PrefetchScalarGridSpec(
             num_scalar_prefetch=1,
@@ -321,11 +332,47 @@
                 whole_spec((1, rows)),
                 pl.BlockSpec((TREE, 128), lambda i, info: (0, KVR // 128)),
                 pair_spec(keys, 512),
+                lead_spec(8, rows),
+            ],
+            out_specs=(far_spec(TRUNK, rows), near_spec(nb)),
+            scratch_shapes=[
+                pltpu.VMEM((keys, 128), BF),
+                pltpu.VMEM((2, keys, 128), BF),
+                pltpu.VMEM((TRUNK, rows), F32),
+                pltpu.VMEM((nb, 2 * SEGLEN, SEGLEN), F32),
+            ],
+        ),
+        name="chances",
+        **costs(6e9, 32e6),
+    )(info, qn, qr, cosp, sinp, qlim[None, :], lat, kv, stats)
+
+
+def attend_back(nb, info, qn, qr, cosp, sinp, lat, kv, up, upx, do, att, pt, pn, upper):
+    rows, keys = qn.shape[0], TRUNK + 2 * nb * SEGLEN
+    return pl.pallas_call(
+        functools.partial(attend_back_kernel, nb),
+        out_shape=(
+            jax.ShapeDtypeStruct((rows, HEADS * NOPE), BF),
+            jax.ShapeDtypeStruct((rows, HEADS * ROPE), BF),
+            jax.ShapeDtypeStruct((128, HEADS * (NOPE + VDIM)), F32),
+            jax.ShapeDtypeStruct((TREE, LATW), BF),
+        ),
+        grid_spec=pltpu.PrefetchScalarGridSpec(
+            num_scalar_prefetch=1,
+            grid=(HEADS // 2,),
+            in_specs=[
+                pair_spec(rows, 256),
+                pair_spec(rows, 128),
+                whole_spec((rows, 128)),
+                whole_spec((rows, 128)),
+                pl.BlockSpec((TREE, 128), lambda i, info: (0, KVR // 128)),
+                pair_spec(keys, 512),
                 pair_spec(KVR, 512),
                 pair_spec(LATW - KVR, 512),
                 pair_spec(rows, 256),
                 pair_spec(rows, 256),
-                lead_spec(8, rows),
+                far_spec(TRUNK, rows),
+                near_spec(nb),
                 whole_spec((LATW - KVR, KVR)),
             ],
             out_specs=(
@@ -337,8 +384,6 @@
             scratch_shapes=[
                 pltpu.VMEM((keys, 128), BF),
                 pltpu.VMEM((2, keys, 128), BF),
-                pltpu.VMEM((TRUNK, rows), F32),
-                pltpu.VMEM((nb, 2 * SEGLEN, SEGLEN), F32),
                 pltpu.VMEM((TRUNK, rows), BF),
                 pltpu.VMEM((keys, 512), BF),
                 pltpu.VMEM((keys, LATW), F32),
@@ -348,11 +393,10 @@
         ),
         name="attend_back",
         **costs(54e9, 30e6),
-    )(info, qn, qr, cosp, sinp, qlim[None, :], lat, kv, up, upx, do, att, stats, upper)
-
-
-def prepare_kernel(planes, query, down, router, shared, front, cut):
-    wide = query[...].astype(F32)
+    )(info, qn, qr, cosp, sinp, lat, kv, up, upx, do, att, pt, pn, upper)
+
+
+def head_columns(wide):
     nope, rope = [], []
     for pair in range(HEADS // 2):
         starts = [(2 * pair + a) * (NOPE + ROPE) for a in range(2)]
@@ -362,8 +406,14 @@
             for at in starts:
                 first = at + NOPE + half * HALF
                 rope.append(wide[:, first : first + HALF])
+    return nope + rope
+
+
+def prepare_kernel(planes, picked, info, *refs):
+    query, down, router, shared = refs[:4]
+    banks, (front, cut), chosen = refs[4 : 4 + picked], refs[4 + picked : 6 + picked], refs[6 + picked :]
     rest = [down[...].astype(F32), router[...].astype(F32)]
-    front[...] = jnp.concatenate(nope + rope + rest, 1).astype(BF)
+    front[...] = jnp.concatenate(head_columns(query[...].astype(F32)) + rest, 1).astype(BF)
     whole = shared[...].astype(F32)
     groups, _, width = cut.shape
     hidden = whole.shape[1] // 2
@@ -377,20 +427,51 @@
                 columns.append(whole[:, at : at + each])
             columns.append(blank)
         cut[j] = jnp.concatenate(columns, 1).astype(BF)
-
-
-def prepare(query, down, router, shared, planes, groups, padded):
-    rows = query.shape[0]
+    rank = banks[0].shape[1]
+    for n in range(picked):
+        if n == 1:
+            chosen[n][...] = jnp.concatenate(head_columns(banks[n][0].astype(F32)), 1).astype(BF)
+        elif n in (4, 5):
+            columns = banks[n].shape[2]
+            chosen[n][...] = jnp.concatenate(
+                [
+                    jnp.zeros((HALF, columns), F32),
+                    banks[n][0].astype(F32),
+                    jnp.zeros((LATW - KVR - HALF - rank, columns), F32),
+                ],
+                0,
+            ).astype(BF)
+        else:
+            chosen[n][...] = banks[n][0]
+    chosen[picked][...] = banks[4][0]
+
+
+def prepare(chosen, matrices, banks, planes, groups, padded):
+    query, down, router, shared = matrices
+    rows, rank = query.shape[0], banks[0].shape[1]
     width = query.shape[1] + down.shape[1] + router.shape[1]
+    shapes = [(rows, width), (groups, rows, 2 * padded)]
+    for n, bank in enumerate(banks):
+        shapes.append((LATW - KVR if n in (4, 5) else rank, bank.shape[2]))
+    shapes.append((rank, banks[4].shape[2]))
     return pl.pallas_call(
-        functools.partial(prepare_kernel, planes),
-        out_shape=(
-            jax.ShapeDtypeStruct((rows, width), BF),
-            jax.ShapeDtypeStruct((groups, rows, 2 * padded), BF),
+        functools.partial(prepare_kernel, planes, len(banks)),
+        out_shape=[jax.ShapeDtypeStruct(shape, BF) for shape in shapes],
+        grid_spec=pltpu.PrefetchScalarGridSpec(
+            num_scalar_prefetch=1,
+            grid=(1,),
+            in_specs=[
+                *[fixed_at(m) for m in matrices],
+                *[
+                    pl.BlockSpec((1, rank, bank.shape[2]), lambda i, info: (info[0], 0, 0))
+                    for bank in banks
+                ],
+            ],
+            out_specs=[whole_out(shape) for shape in shapes],
         ),
         name="prepare",
-        **costs(1e6, 3e6),
-    )(query, down, router, shared)
+        **costs(1e6, 4e6),
+    )(chosen.reshape(1), *matrices, *banks)
 
 
 def project_kernel(
@@ -713,9 +794,17 @@
     return [slots[e : e + 1, :] == wanted for e in range(owned)]
 
 
-def spread_grad_kernel(owned, cap, pay, slots, sh_out, perm, gsh):
+def my_columns(first, extra, owned, offsets):
+    shape = (max(8, owned), extra.shape[1])
+    lane, row = lane_iota(shape), row_iota(shape) + first[0]
+    pick = sum((lane == row + at).astype(F32) for at in offsets)
+    return product_t(pick.astype(BF), extra)
+
+
+def spread_grad_kernel(owned, cap, first, pay, sh_out, perm, gsh):
     rows = pay.shape[0]
-    pick = slot_matrix(slots[0].astype(jnp.int32), owned, cap, rows)
+    slots = my_columns(first, pay[:, D:], owned, (0,)).astype(jnp.int32)
+    pick = slot_matrix(slots, owned, cap, rows)
     hot = jnp.concatenate([p.astype(F32) for p in pick], 0).astype(BF)
     values = pay[:, :D]
     got = product(hot, values)
@@ -724,15 +813,19 @@
     gsh[...] = product_t(values, sh_out[...])
 
 
-def spread_feed_kernel(owned, cap, pay, slots, probs, gsh, sh_in, perm, gates, inner, gact):
+def spread_feed_kernel(
+    owned, cap, experts, first, pay, marks, gsh, sh_in, perm, gates, inner, gact
+):
     rows = pay.shape[0]
-    pick = slot_matrix(slots[0].astype(jnp.int32), owned, cap, rows)
+    slots = my_columns(first, marks[...], owned, (0,)).astype(jnp.int32)
+    probs = my_columns(first, pay[:, D:], owned, (0, experts))
+    pick = slot_matrix(slots, owned, cap, rows)
     hot = jnp.concatenate([p.astype(F32) for p in pick], 0).astype(BF)
     values = pay[:, :D]
     got = product(hot, values)
     for e in range(owned):
         perm[e, 0] = got[e * cap : (e + 1) * cap].astype(BF)
-        gate = jnp.sum(jnp.where(pick[e], probs[0, e : e + 1, :], 0.0), axis=1, keepdims=True)
+        gate = jnp.sum(jnp.where(pick[e], probs[e : e + 1, :], 0.0), axis=1, keepdims=True)
         gates[e, 0] = jnp.broadcast_to(gate, (cap, 128))
     width = gsh.shape[1]
     act = product(values, sh_in[...])
@@ -782,10 +875,10 @@
         rows_out[0, :, at : at + 256] = rows.astype(BF)
 
 
-def collect_kernel(owned, cap, rows_perm, slots, inner, weight, out, *, transposed):
-    rows = out.shape[0]
+def collect_kernel(owned, cap, first, rows_perm, slots, inner, weight, *outs, transposed):
+    rows = slots.shape[0]
     spread = (
-        lane_iota((128, owned * cap)) // cap == row_iota((128, owned * cap))
+        lane_iota((128, owned * cap)) // cap + first[0] == row_iota((128, owned * cap))
     ).astype(F32).astype(BF)
     named = product(slots[...], spread)
     wanted = (lane_iota((rows, owned * cap)) % cap + 1).astype(F32)
@@ -795,25 +888,31 @@
         shared = product_t(inner[...], weight[...])
     else:
         shared = product(inner[...], weight[...])
-    out[:, :D] = (product(hot, values[:, :D]) + shared).astype(BF)
-    if out.shape[1] > D:
-        out[:, D:] = product(hot, values[:, D:]).astype(BF)
+    whole = (product(hot, values[:, :D]) + shared).astype(BF)
+    if transposed:
+        outs[0][:, :D] = whole
+        outs[0][:, D:] = product(hot, values[:, D:]).astype(BF)
+    else:
+        at = 0
+        for out in outs:
+            out[...] = whole[:, at : at + out.shape[1]]
+            at += out.shape[1]
 
 
 def row_block(rows, width):
-    return pl.BlockSpec((rows, width), lambda b: (b, 0))
+    return pl.BlockSpec((rows, width), lambda b, *_: (b, 0))
 
 
 def fixed(shape):
-    return pl.BlockSpec(shape, lambda b: (0,) * len(shape))
-
-
-def token_block(owned, rows):
-    return pl.BlockSpec((1, owned, rows), lambda b: (b, 0, 0))
+    return pl.BlockSpec(shape, lambda b, *_: (0,) * len(shape))
+
+
+def extra_block(rows):
+    return pl.BlockSpec((rows, 128), lambda b, *_: (b, D // 128))
 
 
 def perm_block(owned, cap, width):
-    return pl.BlockSpec((owned, 1, cap, width), lambda b: (0, b, 0, 0))
+    return pl.BlockSpec((owned, 1, cap, width), lambda b, *_: (0, b, 0, 0))
 
 
 def costs(flops, moved):
@@ -827,55 +926,54 @@
     )
 
 
-def spread_grad(payload, slots, sh_out, cap):
-    groups, owned, rows = slots.shape
-    width = sh_out.shape[0]
+def spread_grad(first, payload, sh_out, groups, owned, cap):
+    rows, width = payload.shape[0] // groups, sh_out.shape[0]
     return pl.pallas_call(
         functools.partial(spread_grad_kernel, owned, cap),
-        grid=(groups,),
         out_shape=(
             jax.ShapeDtypeStruct((owned, groups, cap, D), BF),
             jax.ShapeDtypeStruct((groups * rows, width), F32),
         ),
-        in_specs=[
-            row_block(rows, payload.shape[1]),
-            token_block(owned, rows),
-            fixed(sh_out.shape),
-        ],
-        out_specs=(perm_block(owned, cap, D), row_block(rows, width)),
+        grid_spec=pltpu.PrefetchScalarGridSpec(
+            num_scalar_prefetch=1,
+            grid=(groups,),
+            in_specs=[row_block(rows, payload.shape[1]), fixed(sh_out.shape)],
+            out_specs=(perm_block(owned, cap, D), row_block(rows, width)),
+        ),
         name="spread_grad",
         **costs(12e9, 28e6),
-    )(payload, slots, sh_out)
-
-
-def spread_feed(payload, slots, probs, gsh, sh_in, cap):
-    groups, owned, rows = slots.shape
-    width = gsh.shape[1]
+    )(first, payload, sh_out)
+
+
+def spread_feed(first, payload, marks, gsh, sh_in, groups, owned, cap, experts):
+    rows, width = payload.shape[0] // groups, gsh.shape[1]
     return pl.pallas_call(
-        functools.partial(spread_feed_kernel, owned, cap),
-        grid=(groups,),
+        functools.partial(spread_feed_kernel, owned, cap, experts),
         out_shape=(
             jax.ShapeDtypeStruct((owned, groups, cap, D), BF),
             jax.ShapeDtypeStruct((owned, groups, cap, 128), F32),
             jax.ShapeDtypeStruct((groups * rows, width), BF),
             jax.ShapeDtypeStruct((groups * rows, 2 * width), BF),
         ),
-        in_specs=[
-            row_block(rows, payload.shape[1]),
-            token_block(owned, rows),
-            token_block(owned, rows),
-            row_block(rows, width),
-            fixed(sh_in.shape),
-        ],
-        out_specs=(
-            perm_block(owned, cap, D),
-            perm_block(owned, cap, 128),
-            row_block(rows, width),
-            row_block(rows, 2 * width),
+        grid_spec=pltpu.PrefetchScalarGridSpec(
+            num_scalar_prefetch=1,
+            grid=(groups,),
+            in_specs=[
+                row_block(rows, payload.shape[1]),
+                extra_block(rows),
+                row_block(rows, width),
+                fixed(sh_in.shape),
+            ],
+            out_specs=(
+                perm_block(owned, cap, D),
+                perm_block(owned, cap, 128),
+                row_block(rows, width),
+                row_block(rows, 2 * width),
+            ),
         ),
         name="spread_feed",
         **costs(14e9, 28e6),
-    )(payload, slots, probs, gsh, sh_in)
+    )(first, payload, marks, gsh, sh_in)
 
 
 def row_chunk(rows):
@@ -948,23 +1046,26 @@
     )(inner, gates, w_out)
 
 
-def collect(rows_perm, slots, inner, weight, transposed):
+def collect(first, rows_perm, marks, inner, weight, widths, transposed):
     owned, groups, cap, width = rows_perm.shape
-    rows = slots.shape[0] // groups
+    rows = marks.shape[0] // groups
     return pl.pallas_call(
         functools.partial(collect_kernel, owned, cap, transposed=transposed),
-        grid=(groups,),
-        out_shape=jax.ShapeDtypeStruct((groups * rows, width), BF),
-        in_specs=[
-            perm_block(owned, cap, width),
-            row_block(rows, 128),
-            row_block(rows, inner.shape[1]),
-            fixed(weight.shape),
-        ],
-        out_specs=row_block(rows, width),
+        out_shape=[jax.ShapeDtypeStruct((groups * rows, w), BF) for w in widths],
+        grid_spec=pltpu.PrefetchScalarGridSpec(
+            num_scalar_prefetch=1,
+            grid=(groups,),
+            in_specs=[
+                perm_block(owned, cap, width),
+                extra_block(rows),
+                row_block(rows, inner.shape[1]),
+                fixed(weight.shape),
+            ],
+            out_specs=[row_block(rows, w) for w in widths],
+        ),
         name="collect_grad" if transposed else "collect_rows",
         **costs(14e9, 28e6),
-    )(rows_perm, slots, inner, weight)
+    )(first, rows_perm, marks, inner, weight)
 
 
 MESH = pl.DeviceIdType.MESH
@@ -1550,14 +1651,6 @@
     local_tree = group_pos * rows_here // TREE
     tree_offset = group_pos * rows_here - local_tree * TREE
     chosen = adapter_index[lax.axis_index("dp") * trees_here + local_tree]
-    query_in = select_slot(query_entry, chosen)
-    qn_out, qr_out = split_heads(select_slot(query_exit, chosen))
-    lower_in = select_slot(lower_entry, chosen)
-    lower_out = select_slot(lower_exit, chosen)
-    upper_in = select_slot(upper_entry, chosen)
-    upper_out = select_slot(upper_exit, chosen)
-    output_in = select_slot(output_entry, chosen)
-    output_out = select_slot(output_exit, chosen)
     experts_all = router_matrix.shape[1]
     owned = expert_in.shape[0]
     capacity = max(2, 4 * rows_here * TOPK // (3 * experts_all))
@@ -1569,8 +1662,34 @@
     weight_rows = query_matrix.shape[0]
     padded_shared = -(-planes * hidden_shared // 128) * 128
     fill = padded_shared - planes * hidden_shared
-    front, cut = prepare(
-        query_matrix, latent_down, router_matrix, shared_in, planes, groups, padded_shared
+    (
+        front,
+        cut,
+        query_in,
+        query_out,
+        lower_in,
+        lower_out,
+        upper_extra,
+        up_extra,
+        output_in,
+        output_out,
+        upper_in,
+    ) = prepare(
+        chosen,
+        (query_matrix, latent_down, router_matrix, shared_in),
+        (
+            query_entry,
+            query_exit,
+            lower_entry,
+            lower_exit,
+            upper_entry,
+            upper_exit,
+            output_entry,
+            output_exit,
+        ),
+        planes,
+        groups,
+        padded_shared,
     )
     if fast:
         front, mix_up, mix_out, sh_in = gather_blocks(
@@ -1648,7 +1767,7 @@
         front,
         (
             query_in,
-            jnp.concatenate([qn_out, qr_out], 1),
+            query_out,
             lower_in,
             lower_out,
             upper_in,
@@ -1674,14 +1793,6 @@
         all_latent = lax.all_gather(latent_ext, "expert", axis=0, tiled=True)
     tree_latent = lax.dynamic_slice_in_dim(all_latent, local_tree * TREE, TREE, 0)
     sh_in = sh_in.reshape(D, 2 * padded_shared)
-    up_extra = jnp.concatenate(
-        [
-            jnp.zeros((HALF, mix_up.shape[1]), BF),
-            upper_out,
-            jnp.zeros((LATW - KVR - HALF - rank, mix_up.shape[1]), BF),
-        ],
-        0,
-    )
     attended, level, keys_values = attend(
         nb, info, q_nope, q_rope, cos_pair, sin_pair, limit_rows, tree_latent, mix_up, up_extra
     )
@@ -1698,10 +1809,8 @@
         experts_all,
     )
 
-    my_slots = lax.dynamic_slice(all_grad, (0, D + group_pos * owned), (groups * rows_here, owned))
-    slot_rows = jnp.pad(my_slots, ((0, 0), (0, 128 - owned)))
-    slot_cols = my_slots.reshape(groups, rows_here, owned).transpose(0, 2, 1).astype(F32)
-    grad_perm, grad_shared = spread_grad(all_grad, slot_cols, sh_out, cap)
+    first_expert = (group_pos * owned).astype(jnp.int32).reshape(1)
+    grad_perm, grad_shared = spread_grad(first_expert, all_grad, sh_out, groups, owned, cap)
     flat = (owned, groups * cap)
     grad_inner = expert_grads(grad_perm.reshape(*flat, D), expert_out)
 
@@ -1709,19 +1818,12 @@
 
     all_feed, grad_inner = lax.optimization_barrier((all_feed, grad_inner))
 
-    def my_columns(start):
-        return lax.dynamic_slice(
-            all_feed, (0, start + group_pos * owned), (groups * rows_here, owned)
-        ).astype(F32)
-
-    my_probs = my_columns(D) + my_columns(D + experts_all)
-    prob_cols = my_probs.reshape(groups, rows_here, owned).transpose(0, 2, 1)
     feed_perm, gates, inner_shared, gact_shared = spread_feed(
-        all_feed, slot_cols, prob_cols, grad_shared, sh_in, cap
+        first_expert, all_feed, all_grad, grad_shared, sh_in, groups, owned, cap, experts_all
     )
     gates = gates.reshape(*flat, 128)
     slot_perm, inner = run_experts(
-        (group_pos * owned).astype(jnp.int32).reshape(1),
+        first_expert,
         feed_perm.reshape(*flat, D),
         grad_inner,
         gates,
@@ -1729,16 +1831,33 @@
         experts_all,
     )
     grad_part = collect(
-        slot_perm.reshape(owned, groups, cap, D + 128), slot_rows, gact_shared, sh_in, True
-    )
+        first_expert,
+        slot_perm.reshape(owned, groups, cap, D + 128),
+        all_grad,
+        gact_shared,
+        sh_in,
+        (D + 128,),
+        True,
+    )[0]
     grad_sum = lax.psum_scatter(grad_part, "expert", scatter_dimension=0, tiled=True)
     inner, grad_part = lax.optimization_barrier((inner, grad_part))
     rows_perm = expert_rows(inner, gates, expert_out)
-    row_part = collect(
-        rows_perm.reshape(owned, groups, cap, D), slot_rows, inner_shared, sh_out, False
-    )
+    row_part, late_part = collect(
+        first_expert,
+        rows_perm.reshape(owned, groups, cap, D),
+        all_grad,
+        inner_shared,
+        sh_out,
+        (1280, D - 1280),
+        False,
+    )
+
+    level, grad_part = lax.optimization_barrier((level, grad_part))
+    far, near = chances(
+        nb, info, q_nope, q_rope, cos_pair, sin_pair, limit_rows, tree_latent, keys_values, level
+    )
+    grad_sum, far, row_part = lax.optimization_barrier((grad_sum, far, row_part))
     row_sum = lax.psum_scatter(row_part, "expert", scatter_dimension=0, tiled=True)
-
     grad_mixed, grad_output_mid, grad_attended = turn(
         nb,
         offset,
@@ -1760,15 +1879,15 @@
         q_rope,
         cos_pair,
         sin_pair,
-        limit_rows,
         tree_latent,
         keys_values,
         mix_up,
         up_extra,
         grad_attended,
         attended,
-        level,
-        jnp.pad(upper_in, ((HALF, LATW - KVR - HALF - rank), (0, 0))),
+        far,
+        near,
+        upper_extra,
     )
     own_tree = grad_tree
     if trees_here > 1:
@@ -1781,8 +1900,8 @@
         grad_latent = lax.psum_scatter(
             grad_tree, "expert", scatter_dimension=0, tiled=True
         ).astype(F32)
-    row_sum, grad_latent = lax.optimization_barrier((row_sum, grad_latent))
-    block_output = (mixed_state + row_sum.astype(F32)).astype(BF)
+    row_sum, late_part, grad_latent = lax.optimization_barrier((row_sum, late_part, grad_latent))
+    late_sum = lax.psum_scatter(late_part, "expert", scatter_dimension=0, tiled=True)
     offsets, end = [], 0
     for width in (
         query_entry.shape[2],
@@ -1804,7 +1923,7 @@
         [
             dq_nope,
             dq_rope,
-            jnp.concatenate([qn_out, qr_out], 1),
+            query_out,
             query_mid,
             hidden,
             grad_latent.astype(F32),
@@ -1854,6 +1973,9 @@
         grad_input = (grad_mixed + norm_one_back(grad_hidden)[0]).astype(BF)
         gradients = [joined[:, at : at + width] for at, width in offsets]
         banks = reduce_banks(gradients, local_tree, trees_here, adapter_index, adapters)
+    late_sum, grad_input = lax.optimization_barrier((late_sum, grad_input))
+    row_sum = jnp.concatenate([row_sum, late_sum], 1).astype(F32)
+    block_output = (mixed_state + row_sum).astype(BF)
     return (block_output, grad_input, *banks)
 
 

time: 715 us -> 700 us (0.979)
  Pallas kernels: 598 us -> 611 us
  waiting for transfers between devices: 54.7 us -> 42.5 us
  local copies, waits for them, and re-layouts: 20.9 us -> 10.2 us
    pallas_call x3 -> x4, Pallas kernels: 41.1 us -> 63 us  [the longest x1 21.3 us: spread_feed(): pl.pallas_call(functools.partial(spread_feed_kernel, owned, cap, experts)...]
    reduce_scatter x1, waiting for transfers between devices: 37.1 us -> 20.4 us  [body(): lax.psum_scatter(grad_part, 'expert', scatter_dimension=0, tiled=True)]
    pallas_call x1, Pallas kernels: 60 us -> 50.9 us  [attend_back(): pl.pallas_call(functools.partial(attend_back_kernel, nb), out_shape=(jax....]
  transfers between devices with their start and end apart: 7 -> 8, of which waited for: 2 -> 3; matrix products, arithmetic and copies ran while one was open for 2% -> 1% of each run, Pallas kernels for 38% -> 48%
where the time goes in v3:
time: 700 us; the launch traced here: 692 us
  Pallas kernels  611 us (87%)
  waiting for transfers between devices  42.5 us (6%)
  between operations  14.4 us (2%)
  local copies, waits for them, and re-layouts  10.2 us (1%)
  other arithmetic  9.75 us (1%)
    pallas_call x2, Pallas kernels, gather_blocks(): pl.pallas_call(functools.partial(gather_kernel, planes, depth, pieces, co...  177 us
    pallas_call x1, Pallas kernels, run_experts(): pl.pallas_call(functools.partial(expert_kernel, experts), out_shape=(jax....  72.8 us
    pallas_call x1, Pallas kernels, attend_back(): pl.pallas_call(functools.partial(attend_back_kernel, nb), out_shape=(jax....  50.9 us
    pallas_call x1, Pallas kernels, exchange_banks(): pl.pallas_call(functools.partial(bank_kernel, planes, wide), out_shape=[j...  39.8 us
    pallas_call x2, Pallas kernels, collect(): pl.pallas_call(functools.partial(collect_kernel, owned, cap, transposed=t...  35.9 us
    pallas_call x1, Pallas kernels, attend(): pl.pallas_call(functools.partial(attend_kernel, nb), out_shape=(jax.Shape...  35.2 us
    pallas_call x1, Pallas kernels, expert_rows(): pl.pallas_call(expert_rows_kernel, out_shape=jax.ShapeDtypeStruct((owned,...  28.2 us
    pallas_call x1, Pallas kernels, expert_grads(): pl.pallas_call(expert_grad_kernel, out_shape=jax.ShapeDtypeStruct((owned,...  27.4 us
  transfers between devices with their start and end apart: 8, of which 3 were waited for; matrix products, arithmetic and copies ran while one was open for 1% of the time, Pallas kernels for 48%

profile of v3, /device:TPU:0, one launch (start us, length us, event | category | flops | bytes accessed | tf_op | source)
XLA Modules:
  0.0 692.3 jit_solution(9879321537944419756)
XLA Ops:
  7.2 0.0 all-gather.5.cloned.1.call-start
  7.3 0.8 convert_reduce_fusion
  8.1 0.2 convolution_multiply_fusion
  8.3 0.1 copy.44
  8.4 1.2 dynamic_slice.25.info
  9.7 0.8 add_select_fusion.1
  10.4 0.8 fusion.4
  11.2 1.4 fusion
  12.6 3.2 concatenate.21
  15.8 4.2 prepare.1
  20.1 143.5 %gather1.1 = (bf16[4,8,64,3712]{3,2,1,0:T(8,128)(2,1)}, bf16[4,8,16,4096]{3,2,1,0:T(8,128)(2,1)}, bf16[4,8,64,2048]{3,2,1,0:T(8,128)(2,1)}, bf16[4,8,64,768]{3,2,1,0:T(8,128)(2,1)}) custom-call(bf16[64,3712]{1,0:T(8,128)(2,1)} %get-tuple-element.88.refs_0_, bf16[16,4096]{1,0:T(8,128)(2,1)} %refs_1_.3, bf16[64,2048]{1,0:T(8,128)(2,1)} %refs_2_.3, ...), custom_call_target="tpu_custom_call" | custom-call | tf_op jit(solution)/shard_map/gather1/pallas_call | solution.py:1316
  163.5 0.0 copy-start.4
  163.6 15.4 %project.1 = (bf16[384,2048]{1,0:T(8,128)(2,1)}, f32[384,1024]{1,0:T(8,128)}, bf16[320,640]{1,0:T(8,128)(2,1)}, f32[320,512]{1,0:T(8,128)}, bf16[320,2048]{1,0:T...) custom-call(s32[1]{0:T(128)} %bitcast.info, bf16[320,2048]{1,0:T(8,128)(2,1)} %tokens.5, ...), custom_call_target="tpu_custom_call" | custom-call | flops 5000000000 | bytes 20000000 | tf_op jit(solution)/shard_map/project/pallas_call | solution.py:552
  178.9 0.0 all-gather.5.cloned.1.call-update
  179.0 0.0 all-gather.3.cloned.1.call-start
  179.0 2.6 collective-permute-start.2
  181.6 1.1 collective-permute-start
  182.7 0.1 slice_reduce_fusion
  182.8 0.6 gather_fusion
  183.5 0.1 slice_reduce_fusion.1
  183.6 0.6 gather_fusion.1
  184.2 33.1 %gather2.1 = bf16[1,8,320,640]{3,2,1,0:T(8,128)(2,1)} custom-call(bf16[320,640]{1,0:T(8,128)(2,1)} %get-tuple-element.99.refs_0_), custom_call_target="tpu_custom_call" | custom-call | tf_op jit(solution)/shard_map/gather2/pallas_call | solution.py:1316
  217.4 0.1 dynamic_update_slice.12.qlim
  217.6 0.2 select_reduce_fusion
  217.8 0.6 pad_add_fusion.info
  218.4 0.2 maximum_dynamic-update-slice_fusion.cosp
  218.6 0.0 copy-start.6
  218.6 0.7 copy-done.6
  219.3 0.2 maximum_dynamic-update-slice_fusion.1.sinp
  219.5 0.7 copy-done.5
  220.2 35.2 %attend.1 = (bf16[384,2048]{1,0:T(8,128)(2,1)}, f32[8,8,384]{2,1,0:T(8,128)}, bf16[1792,4096]{1,0:T(8,128)(2,1)}) custom-call(s32[12]{0:T(128)} %pad_add_fusion.info, bf16[384,2048]{1,0:T(8,128)(2,1)} %get-tuple-element.96.qn, f32[384,1024]{1,0:T(8,128)} %get-tuple-element.97.qr, f32[384,128]{1,0:T(8,128)} %copy-done.6, f32[384,128]{1,0:T(8,128)} %copy-done.5, ...), custom_call_target="tpu_custom_call" | custom-call | flops 30000001024 | bytes 25000000 | tf_op jit(solution)/shard_map/attend/pallas_call | solution.py:272
  255.5 1.3 pad_maximum_fusion
  256.8 0.2 constant_dynamic-slice_fusion.3
  257.0 0.2 pad_maximum_fusion.1
  257.2 1.3 pad.4.sh_out.weight
  258.5 12.0 %mix.1 = (f32[320,2048]{1,0:T(8,128)}, bf16[320,2176]{1,0:T(8,128)(2,1)}, f32[320,64]{1,0:T(8,128)}, bf16[320,16]{1,0:T(8,128)(2,1)}) custom-call(s32[1]{0:T(128)} %bitcast.info, bf16[384,2048]{1,0:T(8,128)(2,1)} %get-tuple-element.104.attended.att, bf16[320,2048]{1,0:T(8,128)(2,1)} %tokens.5, bf16[2048,2048]{1,0:T(8,128)(2,1)} %bitcast.29, ...), custom_call_target="tpu_custom_call" | custom-call | flops 3000000000 | bytes 14000000 | tf_op jit(solution)/shard_map/mix/pallas_call | solution.py:615
  270.5 0.0 all-gather.3.cloned.1.call-update
  270.5 0.2 reduce-scatter.4.cloned.1.call-start
  270.7 0.0 all-gather.5.cloned.1.call-done.pay.marks.slots
  270.8 17.7 %spread_grad.1 = (bf16[8,8,40,2048]{3,2,1,0:T(8,128)(2,1)}, f32[2560,384]{1,0:T(8,128)}) custom-call(s32[1]{0:T(128)} %bitcast.16.first, bf16[2560,2176]{1,0:T(8,128)(2,1)} %all-gather.5.cloned.1.call-done.pay.marks.slots, bf16[384,2048]{1,0:T(8,128)(2,1)} %pad.4.sh_out.weight), custom_call_target="tpu_custom_call" | custom-call | flops 12000000000 | bytes 28000000 | tf_op jit(solution)/shard_map/spread_grad/pallas_call | solution.py:931
  288.5 27.4 %expert_grads.1.back = bf16[8,320,1408]{2,1,0:T(8,128)(2,1)} custom-call(bf16[8,320,2048]{2,1,0:T(8,128)(2,1)} %bitcast.37, bf16[8,1408,2048]{2,1,0:T(8,128)(2,1)} %w_out.3), custom_call_target="tpu_custom_call" | custom-call | flops 14763950080 | bytes 67108864 | tf_op jit(solution)/shard_map/expert_grads/pallas_call | solution.py:1002
  315.9 20.4 %all-gather.3.cloned.1.call-done.pay = bf16[2560,2176]{1,0:T(8,128)(2,1)} async-done(((bf16[320,2176]{1,0:T(8,128)(2,1)}), bf16[2560,2176]{1,0:T(8,128)(2,1)}) %all-gather.3.cloned.1.call-update) | async-done | bytes 11141136 | tf_op jit(solution)/shard_map/all_gather | solution.py:1817
  336.3 21.3 %spread_feed.1 = (bf16[8,8,40,2048]{3,2,1,0:T(8,128)(2,1)}, f32[8,8,40,128]{3,2,1,0:T(8,128)}, bf16[2560,384]{1,0:T(8,128)(2,1)}, bf16[2560,768]{1,0:T(8,128)(2,1)}) custom-call(s32[1]{0:T(128)} %bitcast.16.first, bf16[2560,2176]{1,0:T(8,128)(2,1)} %all-gather.3.cloned.1.call-done.pay, bf16[2560,2176]{1,0:T(8,128)(2,1)} %all-gather.5.cloned.1.call-done.pay.marks.slots, ...), custom_call_target="tpu_custom_call" | custom-call | flops 14000000000 | bytes 28000000 | tf_op jit(solution)/shard_map/spread_feed/pallas_call | solution.py:950
  357.6 72.8 %experts.1 = (bf16[8,320,2176]{2,1,0:T(8,128)(2,1)}, bf16[8,320,1408]{2,1,0:T(8,128)(2,1)}) custom-call(s32[1]{0:T(128)} %bitcast.16.first, bf16[8,320,2048]{2,1,0:T(8,128)(2,1)} %bitcast.56, bf16[8,320,1408]{2,1,0:T(8,128)(2,1)} %expert_grads.1.back, f32[8,320,128]{2,1,0:T(8,128)} %bitcast.39, bf16[8,2048,2816]{2,1,0:T(8,128)(2,1)} %w_in.1), custom_call_target="tpu_custom_call" | custom-call | flops 59055800320 | bytes 92274688 | tf_op jit(solution)/shard_map/experts/pallas_call | solution.py:1017
  430.4 19.9 %collect_grad.1 = bf16[2560,2176]{1,0:T(8,128)(2,1)} custom-call(s32[1]{0:T(128)} %bitcast.16.first, bf16[8,8,40,2176]{3,2,1,0:T(8,128)(2,1)} %bitcast.55, bf16[2560,2176]{1,0:T(8,128)(2,1)} %all-gather.5.cloned.1.call-done.pay.marks.slots, bf16[2560,768]{1,0:T(8,128)(2,1)} %get-tuple-element.120.inner, bf16[2048,768]{1,0:T(8,128)(2,1)} %bitcast.54), custom_call_target="tpu_custom_call" | custom-call | flops 14000000000 | bytes 28000000 | tf_op jit(solution)/shard_map/collect_grad/pallas_call | solution.py:1052
  450.3 0.0 reduce-scatter.4.cloned.1.call-update
  450.3 0.4 reduce-scatter.6.cloned.1.call-start
  450.8 19.7 %chances.1 = (bf16[8,2,1024,384]{3,2,1,0:T(8,128)(2,1)}, bf16[8,2,3,256,128]{4,3,2,1,0:T(8,128)(2,1)}) custom-call(s32[12]{0:T(128)} %pad_add_fusion.info, bf16[384,2048]{1,0:T(8,128)(2,1)} %get-tuple-element.96.qn, f32[384,1024]{1,0:T(8,128)} %get-tuple-element.97.qr, f32[384,128]{1,0:T(8,128)} %copy-done.6, f32[384,128]{1,0:T(8,128)} %copy-done.5, ...), custom_call_target="tpu_custom_call" | custom-call | flops 6000000000 | bytes 32000000 | tf_op jit(solution)/shard_map/chances/pallas_call | solution.py:318
  470.5 28.2 %expert_rows.1 = bf16[8,320,2048]{2,1,0:T(8,128)(2,1)} custom-call(bf16[8,320,1408]{2,1,0:T(8,128)(2,1)} %get-tuple-element.125.inner, f32[8,320,128]{2,1,0:T(8,128)} %bitcast.40, bf16[8,1408,2048]{2,1,0:T(8,128)(2,1)} %w_out.3), custom_call_target="tpu_custom_call" | custom-call | flops 14763950080 | bytes 67108864 | tf_op jit(solution)/shard_map/expert_rows/pallas_call | solution.py:1038
  498.7 16.1 %collect_rows.1 = (bf16[2560,1280]{1,0:T(8,128)(2,1)}, bf16[2560,768]{1,0:T(8,128)(2,1)}) custom-call(s32[1]{0:T(128)} %bitcast.16.first, bf16[8,8,40,2048]{3,2,1,0:T(8,128)(2,1)} %bitcast.36, bf16[2560,2176]{1,0:T(8,128)(2,1)} %all-gather.5.cloned.1.call-done.pay.marks.slots, bf16[2560,384]{1,0:T(8,128)(2,1)} %get-tuple-element.126.inner, ...), custom_call_target="tpu_custom_call" | custom-call | flops 14000000000 | bytes 28000000 | tf_op jit(solution)/shard_map/collect_rows/pallas_call | solution.py:1052
  514.8 20.4 %reduce-scatter.4.cloned.1.call-done.sums = bf16[320,2176]{1,0:T(8,128)(2,1)} async-done(((bf16[2560,2176]{1,0:T(8,128)(2,1)}), bf16[320,2176]{1,0:T(8,128)(2,1)}) %reduce-scatter.4.cloned.1.call-update) | async-done | bytes 1392656 | tf_op jit(solution)/shard_map/reduce_scatter | solution.py:1842
  535.2 0.0 reduce-scatter.6.cloned.1.call-update
  535.2 0.0 reduce-scatter.8.cloned.1.call-start
  535.2 11.3 %turn.1 = (f32[320,2048]{1,0:T(8,128)}, bf16[320,16]{1,0:T(8,128)(2,1)}, bf16[384,2048]{1,0:T(8,128)(2,1)}) custom-call(s32[1]{0:T(128)} %bitcast.info, bf16[320,2176]{1,0:T(8,128)(2,1)} %reduce-scatter.4.cloned.1.call-done.sums, f32[320,64]{1,0:T(8,128)} %get-tuple-element.131.probs, f32[320,2048]{1,0:T(8,128)} %get-tuple-element.108.mixed, ...), custom_call_target="tpu_custom_call" | custom-call | flops 3000000000 | bytes 18000000 | tf_op jit(solution)/shard_map/turn/pallas_call | solution.py:676
  546.6 50.9 %attend_back.1 = (bf16[384,2048]{1,0:T(8,128)(2,1)}, bf16[384,1024]{1,0:T(8,128)(2,1)}, f32[128,4096]{1,0:T(8,128)}, bf16[2560,640]{1,0:T(8,128)(2,1)}) custom-call(s32[12]{0:T(128)} %pad_add_fusion.info, bf16[384,2048]{1,0:T(8,128)(2,1)} %get-tuple-element.96.qn, f32[384,1024]{1,0:T(8,128)} %get-tuple-element.97.qr, f32[384,128]{1,0:T(8,128)} %copy-done.6, ...), custom_call_target="tpu_custom_call" | custom-call | flops 54000001024 | bytes 30000000 | tf_op jit(solution)/shard_map/attend_back/pallas_call | solution.py:352
  597.5 23.7 %scatter5.1.sums = f32[320,640]{1,0:T(8,128)} custom-call(bf16[8,320,640]{2,1,0:T(8,128)(2,1)} %bitcast.35), custom_call_target="tpu_custom_call" | custom-call | tf_op jit(solution)/shard_map/scatter5/pallas_call | solution.py:1548
  621.3 0.0 reduce-scatter.6.cloned.1.call-done
  621.3 0.0 reduce-scatter.8.cloned.1.call-update
  621.3 10.6 %join.1 = (bf16[320,3712]{1,0:T(8,128)(2,1)}, bf16[16,17408]{1,0:T(8,128)(2,1)}, bf16[320,16]{1,0:T(8,128)(2,1)}, bf16[320,16]{1,0:T(8,128)(2,1)}) custom-call(s32[1]{0:T(128)} %bitcast.info, bf16[384,2048]{1,0:T(8,128)(2,1)} %get-tuple-element.139.dqn, bf16[384,1024]{1,0:T(8,128)(2,1)} %get-tuple-element.140.dqr, ...), custom_call_target="tpu_custom_call" | custom-call | flops 3000000000 | bytes 25000000 | tf_op jit(solution)/shard_map/join/pallas_call | solution.py:772
  631.9 39.8 %banks6.1 = (bf16[4,8,16,2176]{3,2,1,0:T(8,128)(2,1)}, bf16[320,2048]{1,0:T(8,128)(2,1)}) custom-call(bf16[16,17408]{1,0:T(8,128)(2,1)} %get-tuple-element.150.parts, bf16[2048,3712]{1,0:T(8,128)(2,1)} %bitcast.28, bf16[320,3712]{1,0:T(8,128)(2,1)} %get-tuple-element.151.grads, bf16[320,16]{1,0:T(8,128)(2,1)} %get-tuple-element.152.query_mid, ...), custom_call_target="tpu_custom_call" | custom-call | tf_op jit(solution)/shard_map/banks6/pallas_call | solution.py:1409
  671.7 7.8 %place_banks.1 = (f32[8,16,2048]{2,1,0:T(8,128)}, f32[8,16,3072]{2,1,0:T(8,128)}, f32[8,16,2048]{2,1,0:T(8,128)}, f32[8,16,576]{2,1,0:T(8,128)}, f32[8,16,512]{2...) custom-call(s32[4]{0:T(128)} %chosen.1, ...), custom_call_target="tpu_custom_call" | custom-call | flops 1000000 | bytes 11000000 | tf_op jit(solution)/shard_map/place_banks/pallas_call | solution.py:1453
  679.6 1.6 reduce-scatter.8.cloned.1.call-done
  681.2 3.4 add_convert_fusion
  684.5 1.1 copy.49
  (30 shorter events, 0.1 us)
Async XLA Ops:
  7.2 263.6 %all-gather.5.cloned.1.call-start = ((), (), s32[]{:S(2)}) async-start(), calls=%async_computation.4 | async-start | bytes 12533760 | tf_op jit(solution)/shard_map/all_gather | solution.py:1788
  163.5 15.5 %copy-start.4 = (bf16[88,2048]{1,0:T(8,128)(2,1)S(1)}, bf16[88,2048]{1,0:T(8,128)(2,1)}, u32[]{:S(2)}) copy-start(bf16[88,2048]{1,0:T(8,128)(2,1)} %param.41) | copy-start | bytes 1081348
  163.5 19.2 %copy-start.7 = (s32[2560]{0:T(1024)S(1)}, s32[2560]{0:T(1024)}, u32[]{:S(2)}) copy-start(s32[2560]{0:T(1024)} %param.29) | copy-start | bytes 30724
  163.6 19.9 %copy-start.8 = (s32[2560]{0:T(1024)S(1)}, s32[2560]{0:T(1024)}, u32[]{:S(2)}) copy-start(s32[2560]{0:T(1024)} %param.28) | copy-start | bytes 30724
  179.0 157.3 %all-gather.3.cloned.1.call-start = ((), (), s32[]{:S(2)}) async-start(), calls=%async_computation.3 | async-start | bytes 12533760 | tf_op jit(solution)/shard_map/all_gather | solution.py:1817
  179.0 76.5 %collective-permute-start.2 = (bf16[88,2048]{1,0:T(8,128)(2,1)S(1)}, bf16[88,2048]{1,0:T(8,128)(2,1)S(1)}, u32[]{:S(2)}, u32[]{:S(2)}) collective-permute-start(bf16[88,2048]{1,0:T(8,128)(2,1)S(1)} %copy-done.4), channel_id=1, source_target_pairs={{0,24},{8,0},{16,8},{24,16},{1,25},{9,1},{17,9},{25,17},{2,26},{10... | collective-permute-start | bytes 1081352 | tf_op jit(solution)/shard_map/ppermute | solution.py:1574
  181.6 73.9 %collective-permute-start.1 = (bf16[88,2048]{1,0:T(8,128)(2,1)S(1)}, bf16[88,2048]{1,0:T(8,128)(2,1)}, u32[]{:S(2)}, u32[]{:S(2)}) collective-permute-start(bf16[88,2048]{1,0:T(8,128)(2,1)S(1)} %copy-done.4), channel_id=1, source_target_pairs={{0,16},{8,24},{16,0},{24,8},{1,17},{9,25},{17,1},{25,9},{2,18},{10... | collective-permute-start | bytes 1081352 | tf_op jit(solution)/shard_map/ppermute | solution.py:1574
  181.6 73.9 %collective-permute-start = (bf16[88,2048]{1,0:T(8,128)(2,1)S(1)}, bf16[88,2048]{1,0:T(8,128)(2,1)}, u32[]{:S(2)}, u32[]{:S(2)}) collective-permute-start(bf16[88,2048]{1,0:T(8,128)(2,1)S(1)} %copy-done.4), channel_id=1, source_target_pairs={{0,8},{8,16},{16,24},{24,0},{1,9},{9,17},{17,25},{25,1},{2,10},{10... | collective-permute-start | bytes 1081352 | tf_op jit(solution)/shard_map/ppermute | solution.py:1574
  184.2 34.2 %copy-start.1 = (f32[320,32]{1,0:T(8,128)S(1)}, f32[320,32]{1,0:T(8,128)}, u32[]{:S(2)}) copy-start(f32[320,32]{1,0:T(8,128)} %get-tuple-element.176.cos) | copy-start | bytes 122884
  184.2 35.1 %copy-start = (f32[320,32]{1,0:T(8,128)S(1)}, f32[320,32]{1,0:T(8,128)}, u32[]{:S(2)}) copy-start(f32[320,32]{1,0:T(8,128)} %get-tuple-element.175.sin) | copy-start | bytes 122884
  217.6 2.6 copy-start.9
  218.6 0.7 copy-start.6
  219.5 0.7 copy-start.5
  270.5 264.7 %reduce-scatter.4.cloned.1.call-start = ((), (), s32[]{:S(2)}) async-start(), calls=%async_computation.5 | async-start | bytes 12533760 | tf_op jit(solution)/shard_map/reduce_scatter | solution.py:1842
  450.3 171.0 %reduce-scatter.6.cloned.1.call-start = ((), (), s32[]{:S(2)}) async-start(), calls=%async_computation.6 | async-start | bytes 7372800 | tf_op jit(solution)/shard_map/reduce_scatter | solution.py:1860
  535.2 146.0 %reduce-scatter.8.cloned.1.call-start = ((), (), s32[]{:S(2)}) async-start(), calls=%async_computation.7 | async-start | bytes 4423680 | tf_op jit(solution)/shard_map/reduce_scatter | solution.py:1904
  671.7 9.5 %copy-start.3 = (bf16[320,1280]{1,0:T(8,128)(2,1)S(1)}, bf16[320,1280]{1,0:T(8,128)(2,1)}, u32[]{:S(2)}) copy-start(bf16[320,1280]{1,0:T(8,128)(2,1)} %reduce-scatter.6.cloned.1.call-done) | copy-start | bytes 2457604
  681.2 3.4 copy-start.2
Sparse Core Ops, SparseCore 0:
  179.1 76.2 all-gather.4
  270.6 65.6 all-gather.2
  450.4 84.6 reduce-scatter.3
  538.9 62.9 reduce-scatter.5
  621.4 59.6 reduce-scatter.7

commit v4 on v3

--- a/solution.py
+++ b/solution.py
@@ -232,7 +232,7 @@
         dqn[:, a * 128 : a * 128 + 128] = dq[:, :128].astype(BF)
         dq_rope = dq[:, 128:] if dq_rope is None else dq_rope + dq[:, 128:]
     dqr[...] = (dq_rope * cosp[...] + pltpu.roll(dq_rope * sinp[...], ROPE, 1)).astype(BF)
-    gup[...] = product_left(tail[...], dkv[...])
+    gup[...] = product_left(tail[...], dkv[...])[HALF : HALF + gup.shape[0]]
     for at in range(0, tail.shape[0], 256):
         acc[at : at + 256, :KVR] += product_t(dkv[at : at + 256, :], up[...])
         acc[at : at + 256, KVR:] += product_t(dkv[at : at + 256, :], upx[...])
@@ -347,14 +347,14 @@
     )(info, qn, qr, cosp, sinp, qlim[None, :], lat, kv, stats)
 
 
-def attend_back(nb, info, qn, qr, cosp, sinp, lat, kv, up, upx, do, att, pt, pn, upper):
+def attend_back(nb, info, qn, qr, cosp, sinp, lat, kv, up, upx, do, att, pt, pn, upper, rank):
     rows, keys = qn.shape[0], TRUNK + 2 * nb * SEGLEN
     return pl.pallas_call(
         functools.partial(attend_back_kernel, nb),
         out_shape=(
             jax.ShapeDtypeStruct((rows, HEADS * NOPE), BF),
             jax.ShapeDtypeStruct((rows, HEADS * ROPE), BF),
-            jax.ShapeDtypeStruct((128, HEADS * (NOPE + VDIM)), F32),
+            jax.ShapeDtypeStruct((rank, HEADS * (NOPE + VDIM)), F32),
             jax.ShapeDtypeStruct((TREE, LATW), BF),
         ),
         grid_spec=pltpu.PrefetchScalarGridSpec(
@@ -378,7 +378,7 @@
             out_specs=(
                 pair_spec(rows, 256),
                 pair_spec(rows, 128),
-                pair_spec(128, 512),
+                pair_spec(rank, 512),
                 whole_spec((TREE, LATW)),
             ),
             scratch_shapes=[
@@ -411,7 +411,13 @@
 
 def prepare_kernel(planes, picked, info, *refs):
     query, down, router, shared = refs[:4]
-    banks, (front, cut), chosen = refs[4 : 4 + picked], refs[4 + picked : 6 + picked], refs[6 + picked :]
+    cotangent, slots, banks = refs[4], refs[5], refs[6 : 6 + picked]
+    front, cut, payload = refs[6 + picked : 9 + picked]
+    chosen = refs[9 + picked :]
+    payload[:, :D] = cotangent[...]
+    marks = slots[...]
+    blank = jnp.zeros((marks.shape[0], 128 - marks.shape[1]), F32)
+    payload[:, D:] = jnp.concatenate([marks, blank], 1).astype(BF)
     rest = [down[...].astype(F32), router[...].astype(F32)]
     front[...] = jnp.concatenate(head_columns(query[...].astype(F32)) + rest, 1).astype(BF)
     whole = shared[...].astype(F32)
@@ -447,10 +453,14 @@
 
 
 def prepare(chosen, matrices, banks, planes, groups, padded):
-    query, down, router, shared = matrices
+    query, down, router, shared, cotangent, _ = matrices
     rows, rank = query.shape[0], banks[0].shape[1]
     width = query.shape[1] + down.shape[1] + router.shape[1]
-    shapes = [(rows, width), (groups, rows, 2 * padded)]
+    shapes = [
+        (rows, width),
+        (groups, rows, 2 * padded),
+        (cotangent.shape[0], D + 128),
+    ]
     for n, bank in enumerate(banks):
         shapes.append((LATW - KVR if n in (4, 5) else rank, bank.shape[2]))
     shapes.append((rank, banks[4].shape[2]))
@@ -752,8 +762,8 @@
         jnp.concatenate(heads, 1),
         product_left(back_low, hidden[...]),
         product_left(lower_mid[...], low),
-        product_left(tree[:, KVR:], lat[:, :KVR])[HALF : HALF + rank],
-        upper_exit[HALF : HALF + rank, :],
+        product_left(tree[...], lat[...])[HALF : HALF + rank],
+        upper_exit[...],
         product_left(grad_out_mid[...], attended[here, :]),
         product_left(out_mid[...], mixed[...].astype(BF)),
     )
@@ -775,7 +785,12 @@
         grid_spec=pltpu.PrefetchScalarGridSpec(
             num_scalar_prefetch=1,
             grid=(1,),
-            in_specs=[fixed_at(v) for v in operands],
+            in_specs=[
+                *[fixed_at(v) for v in operands[:12]],
+                pl.BlockSpec((TREE, LATW - KVR), lambda i, info: (0, KVR // (LATW - KVR))),
+                pl.BlockSpec((TREE, KVR), lambda i, info: (0, 0)),
+                *[fixed_at(v) for v in operands[14:]],
+            ],
             out_specs=[whole_out(shape) for shape, _ in shapes],
         ),
         name="join",
@@ -1566,16 +1581,24 @@
     )(blocks)
 
 
-def gather_dp(shard):
+def pieces_dp(shard):
     size = lax.axis_size("dp")
-    me = lax.axis_index("dp")
     pieces = [shard]
     for k in range(1, size):
         pieces.append(lax.ppermute(shard, "dp", [(i, (i + k) % size) for i in range(size)]))
+    return pieces
+
+
+def joined_dp(pieces):
+    size, me = len(pieces), lax.axis_index("dp")
     stacked = jnp.stack(pieces)
     return jnp.concatenate(
         [lax.dynamic_index_in_dim(stacked, (me - s) % size, 0, keepdims=True) for s in range(size)], 0
     )
+
+
+def gather_dp(shard):
+    return joined_dp(pieces_dp(shard))
 
 
 def gather_plane(value):
@@ -1659,12 +1682,21 @@
     both = ("dp", "expert")
     fast = groups == PLANE and planes == 4 and groups * rows_here == TREE and hidden_shared % 8 == 0
 
+    mask = jnp.sum(
+        (routes[:, :, None] == jnp.arange(experts_all, dtype=jnp.int32)).astype(F32), axis=1
+    )
+    lower = (
+        jnp.arange(rows_here)[:, None] >= jnp.arange(rows_here)[None, :]
+    ).astype(BF)
+    slots_here = product(lower, mask.astype(BF)) * mask
+
     weight_rows = query_matrix.shape[0]
     padded_shared = -(-planes * hidden_shared // 128) * 128
     fill = padded_shared - planes * hidden_shared
     (
         front,
         cut,
+        grad_payload,
         query_in,
         query_out,
         lower_in,
@@ -1676,7 +1708,7 @@
         upper_in,
     ) = prepare(
         chosen,
-        (query_matrix, latent_down, router_matrix, shared_in),
+        (query_matrix, latent_down, router_matrix, shared_in, cotangent, slots_here),
         (
             query_entry,
             query_exit,
@@ -1751,14 +1783,6 @@
     sin_pair = pad_rows(jnp.concatenate([-sin_half, -sin_half, sin_half, sin_half], -1))
     limit_rows = pad_rows(query_limit)
 
-    mask = jnp.sum(
-        (routes[:, :, None] == jnp.arange(experts_all, dtype=jnp.int32)).astype(F32), axis=1
-    )
-    lower = (
-        jnp.arange(rows_here)[:, None] >= jnp.arange(rows_here)[None, :]
-    ).astype(BF)
-    slots_here = product(lower, mask.astype(BF)) * mask
-
     offset = shift.astype(jnp.int32).reshape(1)
     q_nope, q_rope, latent_ext, latent_raw, hidden, query_mid, lower_mid = project(
         nb,
@@ -1777,14 +1801,7 @@
             sin_half,
         ),
     )
-    grad_payload = jnp.concatenate(
-        [cotangent, slots_here.astype(BF), jnp.zeros((rows_here, 128 - experts_all), BF)], 1
-    )
-    grad_payload, latent_ext, out_rows = lax.optimization_barrier(
-        (grad_payload, latent_ext, shared_out)
-    )
-    sh_out = gather_dp(out_rows).reshape(planes * hidden_shared, D)
-    sh_out = jnp.pad(sh_out, ((0, fill), (0, 0)))
+    grad_payload, latent_ext = lax.optimization_barrier((grad_payload, latent_ext))
     all_grad = lax.all_gather(grad_payload, "expert", axis=0, tiled=True)
     rank = query_mid.shape[1]
     if fast:
@@ -1793,10 +1810,12 @@
         all_latent = lax.all_gather(latent_ext, "expert", axis=0, tiled=True)
     tree_latent = lax.dynamic_slice_in_dim(all_latent, local_tree * TREE, TREE, 0)
     sh_in = sh_in.reshape(D, 2 * padded_shared)
+    out_rows, tree_latent = lax.optimization_barrier((shared_out, tree_latent))
+    out_rows = pieces_dp(out_rows)
     attended, level, keys_values = attend(
         nb, info, q_nope, q_rope, cos_pair, sin_pair, limit_rows, tree_latent, mix_up, up_extra
     )
-    attended, sh_out = lax.optimization_barrier((attended, sh_out))
+    attended, out_rows = lax.optimization_barrier((attended, out_rows))
     mixed_state, feed_payload, router_probs, output_mid = mix(
         offset,
         attended,
@@ -1809,6 +1828,9 @@
         experts_all,
     )
 
+    router_probs, out_rows = lax.optimization_barrier((router_probs, out_rows))
+    sh_out = joined_dp(out_rows).reshape(planes * hidden_shared, D)
+    sh_out = jnp.pad(sh_out, ((0, fill), (0, 0)))
     first_expert = (group_pos * owned).astype(jnp.int32).reshape(1)
     grad_perm, grad_shared = spread_grad(first_expert, all_grad, sh_out, groups, owned, cap)
     flat = (owned, groups * cap)
@@ -1888,6 +1910,7 @@
         far,
         near,
         upper_extra,
+        rank,
     )
     own_tree = grad_tree
     if trees_here > 1:

time: 700 us -> 691 us (0.987)
  no operation moved by 1% of the time
where the time goes in v4:
time: 691 us; the launch traced here: 682 us
  Pallas kernels  606 us (88%)
  waiting for transfers between devices  40.4 us (6%)
  between operations  14.4 us (2%)
  other arithmetic  9.82 us (1%)
  local copies, waits for them, and re-layouts  7.61 us (1%)
    pallas_call x2, Pallas kernels, gather_blocks(): pl.pallas_call(functools.partial(gather_kernel, planes, depth, pieces, co...  172 us
    pallas_call x1, Pallas kernels, run_experts(): pl.pallas_call(functools.partial(expert_kernel, experts), out_shape=(jax....  72.8 us
    pallas_call x1, Pallas kernels, attend_back(): pl.pallas_call(functools.partial(attend_back_kernel, nb), out_shape=(jax....  50.9 us
    pallas_call x1, Pallas kernels, exchange_banks(): pl.pallas_call(functools.partial(bank_kernel, planes, wide), out_shape=[j...  41.4 us
    pallas_call x2, Pallas kernels, collect(): pl.pallas_call(functools.partial(collect_kernel, owned, cap, transposed=t...  35.9 us
    pallas_call x1, Pallas kernels, attend(): pl.pallas_call(functools.partial(attend_kernel, nb), out_shape=(jax.Shape...  34.4 us
    pallas_call x1, Pallas kernels, expert_rows(): pl.pallas_call(expert_rows_kernel, out_shape=jax.ShapeDtypeStruct((owned,...  28.2 us
    pallas_call x1, Pallas kernels, expert_grads(): pl.pallas_call(expert_grad_kernel, out_shape=jax.ShapeDtypeStruct((owned,...  26.8 us
  transfers between devices with their start and end apart: 8, of which 3 were waited for; matrix products, arithmetic and copies ran while one was open for 1% of the time, Pallas kernels for 48%

profile of v4, /device:TPU:0, one launch (start us, length us, event | category | flops | bytes accessed | tf_op | source)
XLA Modules:
  0.0 682.4 jit_solution(9118023256480144253)
XLA Ops:
  7.2 0.0 all-gather.5.cloned.1.call-start
  7.3 0.8 convert_reduce_fusion
  8.1 0.2 convolution_multiply_fusion
  8.3 0.8 copy.44.refs_5_
  9.1 1.2 dynamic_slice.25.info
  10.3 0.8 add_select_fusion.1
  11.1 0.8 fusion.4
  11.9 1.4 fusion
  13.3 5.2 prepare.1
  18.4 143.5 %gather1.1 = (bf16[4,8,64,3712]{3,2,1,0:T(8,128)(2,1)}, bf16[4,8,16,4096]{3,2,1,0:T(8,128)(2,1)}, bf16[4,8,64,2048]{3,2,1,0:T(8,128)(2,1)}, bf16[4,8,64,768]{3,2,1,0:T(8,128)(2,1)}) custom-call(bf16[64,3712]{1,0:T(8,128)(2,1)} %get-tuple-element.98.refs_0_, bf16[16,4096]{1,0:T(8,128)(2,1)} %refs_1_.3, bf16[64,2048]{1,0:T(8,128)(2,1)} %refs_2_.3, ...), custom_call_target="tpu_custom_call" | custom-call | tf_op jit(solution)/shard_map/gather1/pallas_call | solution.py:1331
  161.9 15.3 %project.1 = (bf16[384,2048]{1,0:T(8,128)(2,1)}, f32[384,1024]{1,0:T(8,128)}, bf16[320,640]{1,0:T(8,128)(2,1)}, f32[320,512]{1,0:T(8,128)}, bf16[320,2048]{1,0:T...) custom-call(s32[1]{0:T(128)} %bitcast.info, bf16[320,2048]{1,0:T(8,128)(2,1)} %tokens.5, ...), custom_call_target="tpu_custom_call" | custom-call | flops 5000000000 | bytes 20000000 | tf_op jit(solution)/shard_map/project/pallas_call | solution.py:562
  177.2 0.0 all-gather.5.cloned.1.call-update
  177.3 0.0 copy-start.4
  177.3 0.0 copy-start.7
  177.3 0.0 copy-start.8
  177.3 0.0 all-gather.3.cloned.1.call-start
  177.4 28.6 %gather2.1 = bf16[1,8,320,640]{3,2,1,0:T(8,128)(2,1)} custom-call(bf16[320,640]{1,0:T(8,128)(2,1)} %get-tuple-element.110.refs_0_), custom_call_target="tpu_custom_call" | custom-call | tf_op jit(solution)/shard_map/gather2/pallas_call | solution.py:1331
  206.0 2.5 collective-permute-start.2
  208.5 1.1 collective-permute-start
  209.6 0.1 slice_reduce_fusion
  209.7 0.6 gather_fusion
  210.4 0.1 slice_reduce_fusion.1
  210.5 0.6 gather_fusion.1
  211.1 0.1 dynamic_update_slice.12.qlim
  211.3 0.2 select_reduce_fusion
  211.5 0.7 pad_add_fusion.info
  212.2 0.2 maximum_dynamic-update-slice_fusion.cosp
  212.4 0.0 copy-start.6
  212.4 0.7 copy-done.6
  213.1 0.2 maximum_dynamic-update-slice_fusion.1.sinp
  213.3 0.7 copy-done.5
  214.0 34.4 %attend.1 = (bf16[384,2048]{1,0:T(8,128)(2,1)}, f32[8,8,384]{2,1,0:T(8,128)}, bf16[1792,4096]{1,0:T(8,128)(2,1)}) custom-call(s32[12]{0:T(128)} %pad_add_fusion.info, bf16[384,2048]{1,0:T(8,128)(2,1)} %get-tuple-element.106.qn, f32[384,1024]{1,0:T(8,128)} %get-tuple-element.107.qr, f32[384,128]{1,0:T(8,128)} %copy-done.6, f32[384,128]{1,0:T(8,128)} %copy-done.5, ...), custom_call_target="tpu_custom_call" | custom-call | flops 30000001024 | bytes 25000000 | tf_op jit(solution)/shard_map/attend/pallas_call | solution.py:272
  248.4 12.0 %mix.1 = (f32[320,2048]{1,0:T(8,128)}, bf16[320,2176]{1,0:T(8,128)(2,1)}, f32[320,64]{1,0:T(8,128)}, bf16[320,16]{1,0:T(8,128)(2,1)}) custom-call(s32[1]{0:T(128)} %bitcast.info, bf16[384,2048]{1,0:T(8,128)(2,1)} %get-tuple-element.116.attended.att, bf16[320,2048]{1,0:T(8,128)(2,1)} %tokens.5, bf16[2048,2048]{1,0:T(8,128)(2,1)} %bitcast.29, ...), custom_call_target="tpu_custom_call" | custom-call | flops 3000000000 | bytes 14000000 | tf_op jit(solution)/shard_map/mix/pallas_call | solution.py:625
  260.4 0.0 all-gather.3.cloned.1.call-update
  260.4 0.0 reduce-scatter.4.cloned.1.call-start
  260.5 1.3 pad_maximum_fusion
  261.8 0.2 constant_dynamic-slice_fusion.3
  262.0 0.2 pad_maximum_fusion.1
  262.2 1.3 pad.4.sh_out.weight
  263.5 17.9 %spread_grad.1 = (bf16[8,8,40,2048]{3,2,1,0:T(8,128)(2,1)}, f32[2560,384]{1,0:T(8,128)}) custom-call(s32[1]{0:T(128)} %bitcast.11.first, bf16[2560,2176]{1,0:T(8,128)(2,1)} %all-gather.5.cloned.1.call-done.pay.marks.slots, bf16[384,2048]{1,0:T(8,128)(2,1)} %pad.4.sh_out.weight), custom_call_target="tpu_custom_call" | custom-call | flops 12000000000 | bytes 28000000 | tf_op jit(solution)/shard_map/spread_grad/pallas_call | solution.py:946
  281.4 26.8 %expert_grads.1.back = bf16[8,320,1408]{2,1,0:T(8,128)(2,1)} custom-call(bf16[8,320,2048]{2,1,0:T(8,128)(2,1)} %bitcast.37, bf16[8,1408,2048]{2,1,0:T(8,128)(2,1)} %w_out.3), custom_call_target="tpu_custom_call" | custom-call | flops 14763950080 | bytes 67108864 | tf_op jit(solution)/shard_map/expert_grads/pallas_call | solution.py:1017
  308.2 18.1 %all-gather.3.cloned.1.call-done.pay = bf16[2560,2176]{1,0:T(8,128)(2,1)} async-done(((bf16[320,2176]{1,0:T(8,128)(2,1)}), bf16[2560,2176]{1,0:T(8,128)(2,1)}) %all-gather.3.cloned.1.call-update) | async-done | bytes 11141136 | tf_op jit(solution)/shard_map/all_gather | solution.py:1839
  326.2 21.3 %spread_feed.1 = (bf16[8,8,40,2048]{3,2,1,0:T(8,128)(2,1)}, f32[8,8,40,128]{3,2,1,0:T(8,128)}, bf16[2560,384]{1,0:T(8,128)(2,1)}, bf16[2560,768]{1,0:T(8,128)(2,1)}) custom-call(s32[1]{0:T(128)} %bitcast.11.first, bf16[2560,2176]{1,0:T(8,128)(2,1)} %all-gather.3.cloned.1.call-done.pay, bf16[2560,2176]{1,0:T(8,128)(2,1)} %all-gather.5.cloned.1.call-done.pay.marks.slots, ...), custom_call_target="tpu_custom_call" | custom-call | flops 14000000000 | bytes 28000000 | tf_op jit(solution)/shard_map/spread_feed/pallas_call | solution.py:965
  347.5 72.8 %experts.1 = (bf16[8,320,2176]{2,1,0:T(8,128)(2,1)}, bf16[8,320,1408]{2,1,0:T(8,128)(2,1)}) custom-call(s32[1]{0:T(128)} %bitcast.11.first, bf16[8,320,2048]{2,1,0:T(8,128)(2,1)} %bitcast.56, bf16[8,320,1408]{2,1,0:T(8,128)(2,1)} %expert_grads.1.back, f32[8,320,128]{2,1,0:T(8,128)} %bitcast.39, bf16[8,2048,2816]{2,1,0:T(8,128)(2,1)} %w_in.1), custom_call_target="tpu_custom_call" | custom-call | flops 59055800320 | bytes 92274688 | tf_op jit(solution)/shard_map/experts/pallas_call | solution.py:1032
  420.4 19.9 %collect_grad.1 = bf16[2560,2176]{1,0:T(8,128)(2,1)} custom-call(s32[1]{0:T(128)} %bitcast.11.first, bf16[8,8,40,2176]{3,2,1,0:T(8,128)(2,1)} %bitcast.55, bf16[2560,2176]{1,0:T(8,128)(2,1)} %all-gather.5.cloned.1.call-done.pay.marks.slots, bf16[2560,768]{1,0:T(8,128)(2,1)} %get-tuple-element.140.inner, bf16[2048,768]{1,0:T(8,128)(2,1)} %bitcast.54), custom_call_target="tpu_custom_call" | custom-call | flops 14000000000 | bytes 28000000 | tf_op jit(solution)/shard_map/collect_grad/pallas_call | solution.py:1067
  440.3 0.0 reduce-scatter.4.cloned.1.call-update
  440.3 0.0 reduce-scatter.6.cloned.1.call-start
  440.3 20.1 %chances.1 = (bf16[8,2,1024,384]{3,2,1,0:T(8,128)(2,1)}, bf16[8,2,3,256,128]{4,3,2,1,0:T(8,128)(2,1)}) custom-call(s32[12]{0:T(128)} %pad_add_fusion.info, bf16[384,2048]{1,0:T(8,128)(2,1)} %get-tuple-element.106.qn, f32[384,1024]{1,0:T(8,128)} %get-tuple-element.107.qr, f32[384,128]{1,0:T(8,128)} %copy-done.6, f32[384,128]{1,0:T(8,128)} %copy-done.5, ...), custom_call_target="tpu_custom_call" | custom-call | flops 6000000000 | bytes 32000000 | tf_op jit(solution)/shard_map/chances/pallas_call | solution.py:318
  460.5 28.2 %expert_rows.1 = bf16[8,320,2048]{2,1,0:T(8,128)(2,1)} custom-call(bf16[8,320,1408]{2,1,0:T(8,128)(2,1)} %get-tuple-element.145.inner, f32[8,320,128]{2,1,0:T(8,128)} %bitcast.40, bf16[8,1408,2048]{2,1,0:T(8,128)(2,1)} %w_out.3), custom_call_target="tpu_custom_call" | custom-call | flops 14763950080 | bytes 67108864 | tf_op jit(solution)/shard_map/expert_rows/pallas_call | solution.py:1053
  488.7 16.1 %collect_rows.1 = (bf16[2560,1280]{1,0:T(8,128)(2,1)}, bf16[2560,768]{1,0:T(8,128)(2,1)}) custom-call(s32[1]{0:T(128)} %bitcast.11.first, bf16[8,8,40,2048]{3,2,1,0:T(8,128)(2,1)} %bitcast.36, bf16[2560,2176]{1,0:T(8,128)(2,1)} %all-gather.5.cloned.1.call-done.pay.marks.slots, bf16[2560,384]{1,0:T(8,128)(2,1)} %get-tuple-element.146.inner, ...), custom_call_target="tpu_custom_call" | custom-call | flops 14000000000 | bytes 28000000 | tf_op jit(solution)/shard_map/collect_rows/pallas_call | solution.py:1067
  504.8 20.3 %reduce-scatter.4.cloned.1.call-done.sums = bf16[320,2176]{1,0:T(8,128)(2,1)} async-done(((bf16[2560,2176]{1,0:T(8,128)(2,1)}), bf16[320,2176]{1,0:T(8,128)(2,1)}) %reduce-scatter.4.cloned.1.call-update) | async-done | bytes 1392656 | tf_op jit(solution)/shard_map/reduce_scatter | solution.py:1864
  525.1 0.0 reduce-scatter.6.cloned.1.call-update
  525.1 0.0 reduce-scatter.8.cloned.1.call-start
  525.2 11.3 %turn.1 = (f32[320,2048]{1,0:T(8,128)}, bf16[320,16]{1,0:T(8,128)(2,1)}, bf16[384,2048]{1,0:T(8,128)(2,1)}) custom-call(s32[1]{0:T(128)} %bitcast.info, bf16[320,2176]{1,0:T(8,128)(2,1)} %reduce-scatter.4.cloned.1.call-done.sums, f32[320,64]{1,0:T(8,128)} %get-tuple-element.151.probs, f32[320,2048]{1,0:T(8,128)} %get-tuple-element.120.mixed, ...), custom_call_target="tpu_custom_call" | custom-call | flops 3000000000 | bytes 18000000 | tf_op jit(solution)/shard_map/turn/pallas_call | solution.py:686
  536.5 50.9 %attend_back.1 = (bf16[384,2048]{1,0:T(8,128)(2,1)}, bf16[384,1024]{1,0:T(8,128)(2,1)}, f32[16,4096]{1,0:T(8,128)}, bf16[2560,640]{1,0:T(8,128)(2,1)}) custom-call(s32[12]{0:T(128)} %pad_add_fusion.info, bf16[384,2048]{1,0:T(8,128)(2,1)} %get-tuple-element.106.qn, f32[384,1024]{1,0:T(8,128)} %get-tuple-element.107.qr, f32[384,128]{1,0:T(8,128)} %copy-done.6, ...), custom_call_target="tpu_custom_call" | custom-call | flops 54000001024 | bytes 30000000 | tf_op jit(solution)/shard_map/attend_back/pallas_call | solution.py:352
  587.3 23.8 %scatter5.1.sums = f32[320,640]{1,0:T(8,128)} custom-call(bf16[8,320,640]{2,1,0:T(8,128)(2,1)} %bitcast.35), custom_call_target="tpu_custom_call" | custom-call | tf_op jit(solution)/shard_map/scatter5/pallas_call | solution.py:1563
  611.1 0.0 reduce-scatter.6.cloned.1.call-done
  611.1 0.0 reduce-scatter.8.cloned.1.call-update
  611.2 8.8 %join.1 = (bf16[320,3712]{1,0:T(8,128)(2,1)}, bf16[16,17408]{1,0:T(8,128)(2,1)}, bf16[320,16]{1,0:T(8,128)(2,1)}, bf16[320,16]{1,0:T(8,128)(2,1)}) custom-call(s32[1]{0:T(128)} %bitcast.info, bf16[384,2048]{1,0:T(8,128)(2,1)} %get-tuple-element.159.dqn, bf16[384,1024]{1,0:T(8,128)(2,1)} %get-tuple-element.160.dqr, ...), custom_call_target="tpu_custom_call" | custom-call | flops 3000000000 | bytes 25000000 | tf_op jit(solution)/shard_map/join/pallas_call | solution.py:782
  620.0 41.4 %banks6.1 = (bf16[4,8,16,2176]{3,2,1,0:T(8,128)(2,1)}, bf16[320,2048]{1,0:T(8,128)(2,1)}) custom-call(bf16[16,17408]{1,0:T(8,128)(2,1)} %get-tuple-element.170.parts, bf16[2048,3712]{1,0:T(8,128)(2,1)} %bitcast.28, bf16[320,3712]{1,0:T(8,128)(2,1)} %get-tuple-element.171.grads, bf16[320,16]{1,0:T(8,128)(2,1)} %get-tuple-element.172.query_mid, ...), custom_call_target="tpu_custom_call" | custom-call | tf_op jit(solution)/shard_map/banks6/pallas_call | solution.py:1424
  661.4 7.9 %place_banks.1 = (f32[8,16,2048]{2,1,0:T(8,128)}, f32[8,16,3072]{2,1,0:T(8,128)}, f32[8,16,2048]{2,1,0:T(8,128)}, f32[8,16,576]{2,1,0:T(8,128)}, f32[8,16,512]{2...) custom-call(s32[4]{0:T(128)} %chosen.1, ...), custom_call_target="tpu_custom_call" | custom-call | flops 1000000 | bytes 11000000 | tf_op jit(solution)/shard_map/place_banks/pallas_call | solution.py:1468
  669.3 1.9 reduce-scatter.8.cloned.1.call-done
  671.2 3.4 add_convert_fusion
  674.6 1.1 copy.49
  (28 shorter events, 0.1 us)
Async XLA Ops:
  7.2 256.3 %all-gather.5.cloned.1.call-start = ((), (), s32[]{:S(2)}) async-start(), calls=%async_computation.4 | async-start | bytes 12533760 | tf_op jit(solution)/shard_map/all_gather | solution.py:1805
  177.3 28.7 %copy-start.4 = (bf16[88,2048]{1,0:T(8,128)(2,1)S(1)}, bf16[88,2048]{1,0:T(8,128)(2,1)}, u32[]{:S(2)}) copy-start(bf16[88,2048]{1,0:T(8,128)(2,1)} %param.41) | copy-start | bytes 1081348
  177.3 32.3 %copy-start.7 = (s32[2560]{0:T(1024)S(1)}, s32[2560]{0:T(1024)}, u32[]{:S(2)}) copy-start(s32[2560]{0:T(1024)} %param.29) | copy-start | bytes 30724
  177.3 33.1 %copy-start.8 = (s32[2560]{0:T(1024)S(1)}, s32[2560]{0:T(1024)}, u32[]{:S(2)}) copy-start(s32[2560]{0:T(1024)} %param.28) | copy-start | bytes 30724
  177.3 34.9 %copy-start.1 = (f32[320,32]{1,0:T(8,128)S(1)}, f32[320,32]{1,0:T(8,128)}, u32[]{:S(2)}) copy-start(f32[320,32]{1,0:T(8,128)} %get-tuple-element.196.cos) | copy-start | bytes 122884
  177.3 148.9 %all-gather.3.cloned.1.call-start = ((), (), s32[]{:S(2)}) async-start(), calls=%async_computation.3 | async-start | bytes 12533760 | tf_op jit(solution)/shard_map/all_gather | solution.py:1839
  206.0 7.1 %copy-start = (f32[320,32]{1,0:T(8,128)S(1)}, f32[320,32]{1,0:T(8,128)}, u32[]{:S(2)}) copy-start(f32[320,32]{1,0:T(8,128)} %get-tuple-element.195.sin) | copy-start | bytes 122884
  206.0 42.4 %collective-permute-start.2 = (bf16[88,2048]{1,0:T(8,128)(2,1)S(1)}, bf16[88,2048]{1,0:T(8,128)(2,1)S(1)}, u32[]{:S(2)}, u32[]{:S(2)}) collective-permute-start(bf16[88,2048]{1,0:T(8,128)(2,1)S(1)} %copy-done.4), channel_id=1, source_target_pairs={{0,24},{8,0},{16,8},{24,16},{1,25},{9,1},{17,9},{25,17},{2,26},{10... | collective-permute-start | bytes 1081352 | tf_op jit(solution)/shard_map/ppermute | solution.py:1588
  208.5 39.9 %collective-permute-start.1 = (bf16[88,2048]{1,0:T(8,128)(2,1)S(1)}, bf16[88,2048]{1,0:T(8,128)(2,1)}, u32[]{:S(2)}, u32[]{:S(2)}) collective-permute-start(bf16[88,2048]{1,0:T(8,128)(2,1)S(1)} %copy-done.4), channel_id=1, source_target_pairs={{0,16},{8,24},{16,0},{24,8},{1,17},{9,25},{17,1},{25,9},{2,18},{10... | collective-permute-start | bytes 1081352 | tf_op jit(solution)/shard_map/ppermute | solution.py:1588
  208.5 39.9 %collective-permute-start = (bf16[88,2048]{1,0:T(8,128)(2,1)S(1)}, bf16[88,2048]{1,0:T(8,128)(2,1)}, u32[]{:S(2)}, u32[]{:S(2)}) collective-permute-start(bf16[88,2048]{1,0:T(8,128)(2,1)S(1)} %copy-done.4), channel_id=1, source_target_pairs={{0,8},{8,16},{16,24},{24,0},{1,9},{9,17},{17,25},{25,1},{2,10},{10... | collective-permute-start | bytes 1081352 | tf_op jit(solution)/shard_map/ppermute | solution.py:1588
  211.3 2.7 copy-start.9
  212.4 0.7 copy-start.6
  213.3 0.7 copy-start.5
  260.4 264.7 %reduce-scatter.4.cloned.1.call-start = ((), (), s32[]{:S(2)}) async-start(), calls=%async_computation.5 | async-start | bytes 12533760 | tf_op jit(solution)/shard_map/reduce_scatter | solution.py:1864
  440.3 170.8 %reduce-scatter.6.cloned.1.call-start = ((), (), s32[]{:S(2)}) async-start(), calls=%async_computation.6 | async-start | bytes 7372800 | tf_op jit(solution)/shard_map/reduce_scatter | solution.py:1882
  525.1 146.1 %reduce-scatter.8.cloned.1.call-start = ((), (), s32[]{:S(2)}) async-start(), calls=%async_computation.7 | async-start | bytes 4423680 | tf_op jit(solution)/shard_map/reduce_scatter | solution.py:1927
  661.4 9.8 %copy-start.3 = (bf16[320,1280]{1,0:T(8,128)(2,1)S(1)}, bf16[320,1280]{1,0:T(8,128)(2,1)}, u32[]{:S(2)}) copy-start(bf16[320,1280]{1,0:T(8,128)(2,1)} %reduce-scatter.6.cloned.1.call-done) | copy-start | bytes 2457604
  671.2 3.4 copy-start.2
Sparse Core Ops, SparseCore 0:
  177.4 70.9 all-gather.4
  260.5 65.6 all-gather.2
  440.4 84.6 reduce-scatter.3
  528.8 62.9 reduce-scatter.5
  611.3 59.8 reduce-scatter.7
